TPU v7x, 256 devices: a whole 4x4x8 slice. The times are simulated.
256 devices in a mesh: orb: 8 (over x, core), dom: 32 (over y, z).
Axes of the slice: x: 4, y: 4, z: 8, core: 2. Of those that a mesh axis runs over, the one named last changes fastest.
Arguments:
- orbitals: float32 [768, 128, 8, 128], P('orb', 'dom'), may hold values from -6 to 6
- potential: float32 [128, 8, 128], P('dom'), may hold values from -1 to 3
- prev_gradient: float32 [768, 128, 8, 128], P('orb', 'dom'), may hold values from -24 to 24
- prev_direction: float32 [768, 128, 8, 128], P('orb', 'dom'), may hold values from -24 to 24
Outputs:
- new_orbitals: float32 [768, 128, 8, 128], P('orb', 'dom')
- new_direction: float32 [768, 128, 8, 128], P('orb', 'dom')
- gradient: float32 [768, 128, 8, 128], P('orb', 'dom')
All inputs are finite; a program needn't handle non-finite values.
Results may differ from a plain program's by a relative error of at most 0.0002.
Values sent between devices are 32-bit elements; how exact they have to be, the bound alone decides.
No kernel may reach another device: no remote copies, remote signals or barrier semaphores. Data moves between devices by JAX's collectives and lax.ppermute only.
A program may use at most 128 MiB of HBM per device.

v0:
```python
import jax
import jax.numpy as jnp
from jax import lax
from jax.experimental import pallas as pl
from jax.experimental.pallas import tpu as pltpu
from jax.sharding import PartitionSpec as P

coeffs = (-205.0 / 72.0, 8.0 / 5.0, -1.0 / 5.0, 8.0 / 315.0, -1.0 / 560.0)
step_length = 0.05
VMEM_LIMIT = 32 * 1024 * 1024
ZS = 8


def shift_orb(v, k):
    n = lax.axis_size("orb")
    return lax.ppermute(v, "orb", [(i, (i + k) % n) for i in range(n)])


def swap_core(v):
    n = lax.axis_size("orb")
    return lax.ppermute(v, "orb", [(i, i ^ 1) for i in range(n)])


def flip_z(v, k):
    n = lax.axis_size("dom")
    return lax.ppermute(v, "dom", [(i, i ^ k) for i in range(n)])


def shift_y(v, k):
    n = lax.axis_size("dom")
    return lax.ppermute(v, "dom", [(i, (i + k * ZS) % n) for i in range(n)])


def gather_near(first, second):
    right1, left2 = shift_orb(first, 2), shift_orb(second, -2)
    right2, left1 = shift_orb(second, 2), shift_orb(first, -2)
    blocks = [first, second, right1, left2, right2, left1]
    return blocks + [swap_core(b) for b in blocks]


def gather_far(near):
    far1, far2 = shift_orb(near[2], 2), shift_orb(near[3], -2)
    return [far1, far2, swap_core(far1), swap_core(far2)]


def stencil_kernel(c_ref, l_ref, r_ref, v_ref, o_ref):
    lane = lax.broadcasted_iota(jnp.int32, (8, 128), 1)

    @pl.loop(0, c_ref.shape[0] // 8)
    def _(group):
        rows = pl.ds(pl.multiple_of(group * 8, 8), 8)

        def tile(ref, plane, line):
            start = (plane * 8 + line) * 128
            return ref[rows, start : start + 128]

        def plane_tile(plane, line):
            if plane < 0:
                return tile(l_ref, plane + 4, line)
            if plane > 3:
                return tile(r_ref, plane - 4, line)
            return tile(c_ref, plane, line)

        for plane in range(4):
            for line in range(8):
                start = (plane * 8 + line) * 128
                center = tile(c_ref, plane, line)
                total = (v_ref[:, start : start + 128] - 1.5 * coeffs[0]) * center
                for k in range(1, 5):
                    near = plane_tile(plane + k, line) + plane_tile(plane - k, line)
                    if line + k < 8:
                        near = near + tile(c_ref, plane, line + k)
                    if line - k >= 0:
                        near = near + tile(c_ref, plane, line - k)
                    near = near + jnp.where(lane < 128 - k, pltpu.roll(center, 128 - k, 1), 0.0)
                    near = near + jnp.where(lane >= k, pltpu.roll(center, k, 1), 0.0)
                    total = total + (-0.5 * coeffs[k]) * near
                o_ref[rows, start : start + 128] = total


def apply_hamiltonian(c, left, right, pot):
    rows, cells = c.shape
    step = 24
    block = pl.BlockSpec((step, cells), lambda i: (i, 0))
    return pl.pallas_call(
        stencil_kernel,
        out_shape=jax.ShapeDtypeStruct(c.shape, jnp.float32),
        grid=(rows // step,),
        in_specs=[block, block, block, pl.BlockSpec((1, cells), lambda i: (0, 0))],
        out_specs=block,
        cost_estimate=pl.CostEstimate(flops=40 * rows * cells, bytes_accessed=16 * rows * cells, transcendentals=0),
        name="hamiltonian",
    )(c, left, right, pot)


def split(v):
    hi = v.astype(jnp.bfloat16)
    return hi, (v - hi.astype(jnp.float32)).astype(jnp.bfloat16)


def dot_nt(a, b):
    return lax.dot_general(a, b, (((1,), (1,)), ((), ())), preferred_element_type=jnp.float32)


def store_split(refs, hi_ref, lo_ref):
    at = 0
    for ref in refs:
        hi, lo = split(ref[...])
        hi_ref[at : at + ref.shape[0], :] = hi
        lo_ref[at : at + ref.shape[0], :] = lo
        at += ref.shape[0]


def gram(own_blocks, blocks):
    cells = blocks[0].shape[1]
    count = len(own_blocks)
    rows = sum(b.shape[0] for b in own_blocks)
    total = sum(b.shape[0] for b in blocks)
    chunk = 1024

    def kernel(*rest):
        o_ref, hi_ref, lo_ref, w_ref = rest[-4:]
        store_split(rest[count:-4], hi_ref, lo_ref)
        store_split(rest[:count], w_ref.at[0:rows], w_ref.at[rows : 2 * rows])
        with_hi = dot_nt(w_ref[...], hi_ref[...])
        part = with_hi[:rows] + with_hi[rows:] + dot_nt(w_ref[0:rows, :], lo_ref[...])

        @pl.when(pl.program_id(0) == 0)
        def _():
            o_ref[...] = part

        @pl.when(pl.program_id(0) > 0)
        def _():
            o_ref[...] += part

    return pl.pallas_call(
        kernel,
        out_shape=jax.ShapeDtypeStruct((rows, total), jnp.float32),
        grid=(cells // chunk,),
        in_specs=[pl.BlockSpec((b.shape[0], chunk), lambda i: (0, i)) for b in own_blocks + blocks],
        out_specs=pl.BlockSpec((rows, total), lambda i: (0, 0)),
        scratch_shapes=[
            pltpu.VMEM((total, chunk), jnp.bfloat16),
            pltpu.VMEM((total, chunk), jnp.bfloat16),
            pltpu.VMEM((2 * rows, chunk), jnp.bfloat16),
        ],
        compiler_params=pltpu.CompilerParams(vmem_limit_bytes=VMEM_LIMIT),
        cost_estimate=pl.CostEstimate(
            flops=6 * rows * total * cells, bytes_accessed=4 * cells * (rows + total), transcendentals=0
        ),
        name="gram",
    )(*own_blocks, *blocks)


def sum_over_slabs(part):
    rows, columns = part.shape
    quad = ZS // 2
    z = lax.rem(lax.axis_index("dom"), ZS)
    high, low = z // quad, lax.rem(z, quad)
    pieces = part.reshape(2, quad, rows // ZS, columns)

    def piece(k):
        return lax.dynamic_index_in_dim(pieces, low ^ k, 1, keepdims=False)

    total = piece(0)
    for got in [flip_z(piece(k), k) for k in range(quad - 1, 0, -1)]:
        total = total + got
    other = flip_z(jnp.where(high == 0, total[1], total[0]), quad)
    total = jnp.where(high == 0, total[0], total[1]) + other
    count = lax.axis_size("dom") // ZS
    for got in [shift_y(total, k) for k in range(1, count)]:
        total = total + got
    other = flip_z(total, quad)
    total = jnp.where(high == 0, jnp.stack([total, other]), jnp.stack([other, total]))
    out = jnp.zeros_like(pieces)
    out = lax.dynamic_update_slice_in_dim(out, total[:, None], low, 1)
    for k in range(quad - 1, 0, -1):
        out = lax.dynamic_update_slice_in_dim(out, flip_z(total, k)[:, None], low ^ k, 1)
    return out.reshape(rows, columns)


def gradient_of(overlap, blocks, images, own_image, prev, cells_total):
    own, cells = prev.shape
    total = overlap.shape[1]
    count = len(blocks)
    devices = lax.axis_size("orb") * lax.axis_size("dom")
    chunk = 1024

    def kernel(s_ref, p_ref, *rest):
        g_ref, sums_ref, w_ref, acc_ref, hi_ref, lo_ref = rest[-6:]
        own_refs, refs = rest[:2], rest[2 : 2 + 2 * count]

        @pl.when(pl.program_id(0) == 0)
        def _():
            for index in range(2):
                hi, lo = split(s_ref[(1 - index) * own : (2 - index) * own, :] * (-2.0 / cells_total))
                w_ref[:own, index * total : (index + 1) * total] = hi
                w_ref[own:, index * total : (index + 1) * total] = lo
            acc_ref[...] = jnp.zeros_like(acc_ref)

        store_split(refs, hi_ref, lo_ref)
        with_hi = jnp.dot(w_ref[...], hi_ref[...], preferred_element_type=jnp.float32)
        grad = with_hi[:own] + with_hi[own:]
        grad = grad + jnp.dot(w_ref[:own, :], lo_ref[...], preferred_element_type=jnp.float32)
        grad = grad + 4.0 * jnp.concatenate([own_refs[0][...], own_refs[1][...]], axis=0)
        g_ref[...] = grad
        prev_block = p_ref[...]

        def folded(v):
            v = v.reshape(own // 8, 8, chunk).sum(0)
            return sum(v[:, k * 128 : (k + 1) * 128] for k in range(chunk // 128))

        acc_ref[0:8, :] += folded(grad * grad)
        acc_ref[8:16, :] += folded(grad * prev_block)
        acc_ref[16:24, :] += folded(prev_block * prev_block)

        @pl.when(pl.program_id(0) == cells // chunk - 1)
        def _():
            lane = lax.broadcasted_iota(jnp.int32, (devices, 128), 1)
            row = jnp.zeros((devices, 128), jnp.float32)
            for k in range(3):
                value = acc_ref[8 * k : 8 * k + 8, :].sum(axis=0, keepdims=True).sum(axis=1, keepdims=True)
                row = jnp.where(lane == k, value, row)
            sums_ref[...] = row

    own_block = pl.BlockSpec((own, chunk), lambda i: (0, i))
    column = [pl.BlockSpec((b.shape[0], chunk), lambda i: (0, i)) for b in own_image + blocks + images]
    return pl.pallas_call(
        kernel,
        out_shape=(
            jax.ShapeDtypeStruct((own, cells), jnp.float32),
            jax.ShapeDtypeStruct((devices, 128), jnp.float32),
        ),
        grid=(cells // chunk,),
        in_specs=[pl.BlockSpec((2 * own, total), lambda i: (0, 0)), own_block] + column,
        out_specs=(own_block, pl.BlockSpec((devices, 128), lambda i: (0, 0))),
        scratch_shapes=[
            pltpu.VMEM((2 * own, 2 * total), jnp.bfloat16),
            pltpu.VMEM((24, 128), jnp.float32),
            pltpu.VMEM((2 * total, chunk), jnp.bfloat16),
            pltpu.VMEM((2 * total, chunk), jnp.bfloat16),
        ],
        compiler_params=pltpu.CompilerParams(vmem_limit_bytes=VMEM_LIMIT),
        cost_estimate=pl.CostEstimate(
            flops=12 * own * total * cells, bytes_accessed=8 * cells * total, transcendentals=0
        ),
        name="gradient",
    )(overlap, prev, *own_image, *blocks, *images)


def advance(sums, orbitals, prev_direction, grad):
    step = 16
    rows = orbitals.shape[0]

    def kernel(s_ref, c_ref, d_ref, g_ref, new_ref, dir_ref):
        total = s_ref[...].sum(axis=0, keepdims=True)
        beta = (total[:, 0:1] - total[:, 1:2]) / total[:, 2:3]
        direction = beta[:, None, None, :] * d_ref[...] - g_ref[...]
        dir_ref[...] = direction
        new_ref[...] = c_ref[...] + step_length * direction

    block = pl.BlockSpec((step,) + orbitals.shape[1:], lambda i: (i, 0, 0, 0))
    out = jax.ShapeDtypeStruct(orbitals.shape, jnp.float32)
    return pl.pallas_call(
        kernel,
        out_shape=(out, out),
        grid=(rows // step,),
        in_specs=[pl.BlockSpec(sums.shape, lambda i: (0, 0)), block, block, block],
        out_specs=(block, block),
        cost_estimate=pl.CostEstimate(flops=4 * orbitals.size, bytes_accessed=20 * orbitals.size, transcendentals=0),
        name="advance",
    )(sums, orbitals, prev_direction, grad)


def on_device(orbitals, potential, prev_gradient, prev_direction):
    own = orbitals.shape[0]
    half = own // 2
    slabs = lax.axis_size("dom")
    c = [orbitals[:half].reshape(half, -1), orbitals[half:].reshape(half, -1)]
    near = gather_near(*c)
    far = gather_far(near)
    image = []
    for index in range(2):
        left = lax.ppermute(c[index], "dom", [(i, i + 1) for i in range(slabs - 1)])
        right = lax.ppermute(c[index], "dom", [(i + 1, i) for i in range(slabs - 1)])
        if index == 0:
            prev, left = lax.optimization_barrier((prev_gradient.reshape(own, -1), left))
        image.append(apply_hamiltonian(c[index], left, right, potential.reshape(1, -1)))
    near_image = gather_near(*image)
    far_image = gather_far(near_image)
    part_near = gram(c + image, near)
    part_far = gram(c + image, far)
    overlap = sum_over_slabs(jnp.concatenate([part_near, part_far], axis=1))
    grad, sums = gradient_of(
        overlap, near + far, near_image + far_image, image, prev, slabs * c[0].shape[1]
    )
    sums = lax.all_to_all(sums, ("orb", "dom"), split_axis=0, concat_axis=0, tiled=True)
    grad = grad.reshape(orbitals.shape)
    return (*advance(sums, orbitals, prev_direction, grad), grad)


def solution(mesh):
    in_specs = (
        P("orb", "dom", None, None),
        P("dom", None, None),
        P("orb", "dom", None, None),
        P("orb", "dom", None, None),
    )
    out_specs = (
        P("orb", "dom", None, None),
        P("orb", "dom", None, None),
        P("orb", "dom", None, None),
    )
    return jax.shard_map(
        on_device, mesh=mesh, in_specs=in_specs, out_specs=out_specs, check_vma=False
    )
```

profile of v0, /device:TPU:1, one launch (start us, length us, event | category | flops | bytes accessed | tf_op | source)
XLA Modules:
  0.0 214.7 jit_solution(1623515996479525187)
XLA Ops:
  0.6 1.5 fusion.3
  2.6 3.3 %collective-permute-start.8 = (f32[48,4096]{1,0:T(8,128)S(1)}, f32[48,4096]{1,0:T(8,128)S(1)}, u32[]{:S(2)}, u32[]{:S(2)}) collective-permute-start(f32[48,4096]{1,0:T(8,128)S(1)} %bitcast.55), channel_id=1, source_target_pairs={{0,32},{32,0},{64,96},{96,64},{128,160},{160,128},{192,224},{224,1... | collective-permute-start | bytes 2359304 | tf_op jit(solution)/shard_map/ppermute | solution.py:21
  5.9 0.8 collective-permute-start.7
  6.7 0.7 collective-permute-start.4
  7.4 1.3 collective-permute-start.1
  8.6 4.0 %collective-permute-start = (f32[48,4096]{1,0:T(8,128)S(1)}, f32[48,4096]{1,0:T(8,128)S(1)}, u32[]{:S(2)}, u32[]{:S(2)}) collective-permute-start(f32[48,4096]{1,0:T(8,128)S(1)} %bitcast.59), channel_id=1, source_target_pairs={{0,1},{1,2},{2,3},{3,4},{4,5},{5,6},{6,7},{7,8},{8,9},{9,10},{10,1... | collective-permute-start | bytes 2359304 | tf_op jit(solution)/shard_map/ppermute | solution.py:284
  13.2 1.3 collective-permute-start.9
  14.5 10.5 %collective-permute-done.7.rest_9_.rest_7_ = f32[48,4096]{1,0:T(8,128)S(1)} collective-permute-done((f32[48,4096]{1,0:T(8,128)S(1)}, f32[48,4096]{1,0:T(8,128)S(1)}, u32[]{:S(2)}, u32[]{:S(2)}) %collective-permute-start.7) | collective-permute-done | bytes 786464 | tf_op jit(solution)/shard_map/ppermute | solution.py:16
  25.0 1.7 collective-permute-done.4.rest_6_.rest_4_
  26.7 1.0 collective-permute-start.5
  27.7 1.3 collective-permute-start.3
  29.0 4.2 %collective-permute-start.2 = (f32[48,4096]{1,0:T(8,128)S(1)}, f32[48,4096]{1,0:T(8,128)S(1)}, u32[]{:S(2)}, u32[]{:S(2)}) collective-permute-start(f32[48,4096]{1,0:T(8,128)S(1)} %bitcast.69), channel_id=1, source_target_pairs={{0,1},{1,2},{2,3},{3,4},{4,5},{5,6},{6,7},{7,8},{8,9},{9,10},{10,1... | collective-permute-start | bytes 2359304 | tf_op jit(solution)/shard_map/ppermute | solution.py:284
  33.2 0.9 copy-done.12
  34.1 1.9 collective-permute-start.13
  36.0 8.6 %collective-permute-done.6.rest_8_.rest_6_ = f32[48,4096]{1,0:T(8,128)} collective-permute-done((f32[48,4096]{1,0:T(8,128)S(1)}, f32[48,4096]{1,0:T(8,128)}, u32[]{:S(2)}, u32[]{:S(2)}) %collective-permute-start.6) | collective-permute-done | bytes 786464 | tf_op jit(solution)/shard_map/ppermute | solution.py:16
  44.7 2.6 %collective-permute-start.15 = (f32[48,4096]{1,0:T(8,128)}, f32[48,4096]{1,0:T(8,128)}, u32[]{:S(2)}, u32[]{:S(2)}) collective-permute-start(f32[48,4096]{1,0:T(8,128)} %collective-permute-done.5.rest_7_.rest_5_), channel_id=1, source_target_pairs={{0,192},{32,224},{64,0},{96,32},{128,64},{160,96},{192,128},{224,1... | collective-permute-start | bytes 2359304 | tf_op jit(solution)/shard_map/ppermute | solution.py:16
  47.5 2.2 %collective-permute-start.10 = (f32[48,4096]{1,0:T(8,128)}, f32[48,4096]{1,0:T(8,128)}, u32[]{:S(2)}, u32[]{:S(2)}) collective-permute-start(f32[48,4096]{1,0:T(8,128)} %collective-permute-done.4.rest_6_.rest_4_), channel_id=1, source_target_pairs={{0,32},{32,0},{64,96},{96,64},{128,160},{160,128},{192,224},{224,1... | collective-permute-start | bytes 2359304 | tf_op jit(solution)/shard_map/ppermute | solution.py:21
  49.7 1.2 collective-permute-start.12
  50.9 1.0 copy-done.15
  52.1 11.4 %collective-permute-done.14.rest_4_.rest_14_ = f32[48,4096]{1,0:T(8,128)} collective-permute-done((f32[48,4096]{1,0:T(8,128)}, f32[48,4096]{1,0:T(8,128)}, u32[]{:S(2)}, u32[]{:S(2)}) %collective-permute-start.14) | collective-permute-done | bytes 786464 | tf_op jit(solution)/shard_map/ppermute | solution.py:16
  63.5 2.6 %collective-permute-start.16 = (f32[48,4096]{1,0:T(8,128)}, f32[48,4096]{1,0:T(8,128)}, u32[]{:S(2)}, u32[]{:S(2)}) collective-permute-start(f32[48,4096]{1,0:T(8,128)} %collective-permute-done.14.rest_4_.rest_14_), channel_id=1, source_target_pairs={{0,32},{32,0},{64,96},{96,64},{128,160},{160,128},{192,224},{224,1... | collective-permute-start | bytes 2359304 | tf_op jit(solution)/shard_map/ppermute | solution.py:21
  66.4 3.6 %copy.19 = f32[12,8,32,128]{3,1,2,0:T(8,128)} copy(f32[12,8,32,128]{3,2,1,0:T(8,128)} %bitcast.83) | data formatting | bytes 3145728
  70.0 4.2 %hamiltonian.2.rest_2_.rest_0_.rest_18_ = f32[48,4096]{1,0:T(8,128)} custom-call(f32[48,4096]{1,0:T(8,128)} %bitcast.60, f32[48,4096]{1,0:T(8,128)} %copy-done.24, f32[48,4096]{1,0:T(8,128)} %copy-done.23, f32[1,4096]{1,0:T(1,128)} %bitcast.90), custom_call_target="tpu_custom_call" | custom-call | flops 7864320 | bytes 3145728 | tf_op jit(solution)/shard_map/hamiltonian/pallas_call | solution.py:85
  74.3 4.3 %hamiltonian.3.rest_3_.rest_1_.rest_19_ = f32[48,4096]{1,0:T(8,128)} custom-call(f32[48,4096]{1,0:T(8,128)} %bitcast.70, f32[48,4096]{1,0:T(8,128)} %copy-done.26, f32[48,4096]{1,0:T(8,128)} %copy-done.25, f32[1,4096]{1,0:T(1,128)} %bitcast.91), custom_call_target="tpu_custom_call" | custom-call | flops 7864320 | bytes 3145728 | tf_op jit(solution)/shard_map/hamiltonian/pallas_call | solution.py:85
  78.6 1.1 copy-done.5
  79.8 1.1 copy-done.10
  80.9 1.1 copy-done.13
  82.0 1.1 copy-done.16
  83.2 6.9 %gram.2 = f32[192,576]{1,0:T(8,128)S(1)} custom-call(f32[48,4096]{1,0:T(8,128)S(1)} %bitcast.61, f32[48,4096]{1,0:T(8,128)S(1)} %bitcast.71, f32[48,4096]{1,0:T(8,128)S(1)} %copy-done.4, f32[48,4096]{1,0:T(8,128)S(1)} %copy-done.5, f32[48,4096]{1,0:T(8,128)S(1)} %bitcast.62, f32[48,4096]{1,0:T(8,128)S(1)} %bitcast.72, ...), custom_call_target="tpu_custom_call" | custom-call | flops 2717908992 | bytes 12582912 | tf_op jit(solution)/shard_map/gram/pallas_call | solution.py:136
  90.0 4.2 %gram.3 = f32[192,192]{1,0:T(8,128)S(1)} custom-call(f32[48,4096]{1,0:T(8,128)S(1)} %bitcast.63, f32[48,4096]{1,0:T(8,128)S(1)} %bitcast.73, f32[48,4096]{1,0:T(8,128)S(1)} %copy-done.4, f32[48,4096]{1,0:T(8,128)S(1)} %copy-done.5, f32[48,4096]{1,0:T(8,128)} %collective-permute-done.14.rest_4_.rest_14_, f32[48,4096]{1,0:T(8,128)} %collective-permute-done.15.rest_5_.rest_15_, ...), custom_call_target="tpu_custom_call" | custom-call | flops 905969664 | bytes 6291456 | tf_op jit(solution)/shard_map/gram/pallas_call | solution.py:136
  94.4 0.8 dynamic-slice_bitcast_fusion.2
  95.2 3.7 %collective-permute-start.18 = (f32[2,24,768]{2,1,0:T(8,128)}, f32[2,24,768]{2,1,0:T(8,128)S(1)}, u32[]{:S(2)}, u32[]{:S(2)}) collective-permute-start(f32[2,24,768]{2,1,0:T(8,128)} %get-tuple-element.17), channel_id=1, source_target_pairs={{0,3},{1,2},{2,1},{3,0},{4,7},{5,6},{6,5},{7,4},{8,11},{9,10},{10,... | collective-permute-start | bytes 442376 | tf_op jit(solution)/shard_map/ppermute | solution.py:26
  99.2 0.8 collective-permute-start.33
  100.0 2.2 %collective-permute-start.32 = (f32[48,4096]{1,0:T(8,128)S(1)}, f32[48,4096]{1,0:T(8,128)}, u32[]{:S(2)}, u32[]{:S(2)}) collective-permute-start(f32[48,4096]{1,0:T(8,128)S(1)} %copy-done.4), channel_id=1, source_target_pairs={{0,192},{32,224},{64,0},{96,32},{128,64},{160,96},{192,128},{224,1... | collective-permute-start | bytes 2359304 | tf_op jit(solution)/shard_map/ppermute | solution.py:16
  102.1 1.0 collective-permute-done.18
  103.1 5.1 %collective-permute-done.20 = f32[2,24,768]{2,1,0:T(8,128)S(1)} collective-permute-done((f32[2,24,768]{2,1,0:T(8,128)}, f32[2,24,768]{2,1,0:T(8,128)S(1)}, u32[]{:S(2)}, u32[]{:S(2)}) %collective-permute-start.20) | collective-permute-done | bytes 147488 | tf_op jit(solution)/shard_map/ppermute | solution.py:26
  108.3 2.4 %collective-permute-start.30 = (f32[48,4096]{1,0:T(8,128)S(1)}, f32[48,4096]{1,0:T(8,128)S(1)}, u32[]{:S(2)}, u32[]{:S(2)}) collective-permute-start(f32[48,4096]{1,0:T(8,128)S(1)} %copy-done.6), channel_id=1, source_target_pairs={{0,192},{32,224},{64,0},{96,32},{128,64},{160,96},{192,128},{224,1... | collective-permute-start | bytes 2359304 | tf_op jit(solution)/shard_map/ppermute | solution.py:16
  111.2 1.1 fusion.2
  112.4 5.7 %collective-permute-start.21 = (f32[24,768]{1,0:T(8,128)S(1)}, f32[24,768]{1,0:T(8,128)S(1)}, u32[]{:S(2)}, u32[]{:S(2)}) collective-permute-start(f32[24,768]{1,0:T(8,128)S(1)} %select_bitcast_fusion), channel_id=1, source_target_pairs={{0,4},{1,5},{2,6},{3,7},{4,0},{5,1},{6,2},{7,3},{8,12},{9,13},{10,... | collective-permute-start | bytes 221192 | tf_op jit(solution)/shard_map/ppermute | solution.py:26
  118.1 1.8 collective-permute-done.21
  120.0 2.8 %collective-permute-start.24 = (f32[24,768]{1,0:T(8,128)S(1)}, f32[24,768]{1,0:T(8,128)S(1)}, u32[]{:S(2)}, u32[]{:S(2)}) collective-permute-start(f32[24,768]{1,0:T(8,128)S(1)} %bitcast_add_fusion.1), channel_id=1, source_target_pairs={{0,24},{1,25},{2,26},{3,27},{4,28},{5,29},{6,30},{7,31},{8,0},{9,1... | collective-permute-start | bytes 221192 | tf_op jit(solution)/shard_map/ppermute | solution.py:31
  123.1 0.7 collective-permute-start.22
  124.2 2.8 %collective-permute-start.34 = (f32[48,4096]{1,0:T(8,128)S(1)}, f32[48,4096]{1,0:T(8,128)S(1)}, u32[]{:S(2)}, u32[]{:S(2)}) collective-permute-start(f32[48,4096]{1,0:T(8,128)S(1)} %copy-done.6), channel_id=1, source_target_pairs={{0,32},{32,0},{64,96},{96,64},{128,160},{160,128},{192,224},{224,1... | collective-permute-start | bytes 2359304 | tf_op jit(solution)/shard_map/ppermute | solution.py:21
  127.6 0.7 collective-permute-done.22
  128.3 3.3 %collective-permute-start.38 = (f32[48,4096]{1,0:T(8,128)}, f32[48,4096]{1,0:T(8,128)S(1)}, u32[]{:S(2)}, u32[]{:S(2)}) collective-permute-start(f32[48,4096]{1,0:T(8,128)} %collective-permute-done.32.rest_23_), channel_id=1, source_target_pairs={{0,32},{32,0},{64,96},{96,64},{128,160},{160,128},{192,224},{224,1... | collective-permute-start | bytes 2359304 | tf_op jit(solution)/shard_map/ppermute | solution.py:21
  131.6 5.7 %collective-permute-start.25 = (f32[24,768]{1,0:T(8,128)S(1)}, f32[24,768]{1,0:T(8,128)S(1)}, u32[]{:S(2)}, u32[]{:S(2)}) collective-permute-start(f32[24,768]{1,0:T(8,128)S(1)} %add_add_fusion), channel_id=1, source_target_pairs={{0,4},{1,5},{2,6},{3,7},{4,0},{5,1},{6,2},{7,3},{8,12},{9,13},{10,... | collective-permute-start | bytes 221192 | tf_op jit(solution)/shard_map/ppermute | solution.py:26
  137.5 2.5 %collective-permute-done.25 = f32[24,768]{1,0:T(8,128)S(1)} collective-permute-done((f32[24,768]{1,0:T(8,128)S(1)}, f32[24,768]{1,0:T(8,128)S(1)}, u32[]{:S(2)}, u32[]{:S(2)}) %collective-permute-start.25) | collective-permute-done | bytes 73760 | tf_op jit(solution)/shard_map/ppermute | solution.py:26
  140.0 2.4 %collective-permute-start.40 = (f32[48,4096]{1,0:T(8,128)S(1)}, f32[48,4096]{1,0:T(8,128)S(1)}, u32[]{:S(2)}, u32[]{:S(2)}) collective-permute-start(f32[48,4096]{1,0:T(8,128)S(1)} %collective-permute-done.30.rest_21_), channel_id=1, source_target_pairs={{0,192},{32,224},{64,0},{96,32},{128,64},{160,96},{192,128},{224,1... | collective-permute-start | bytes 2359304 | tf_op jit(solution)/shard_map/ppermute | solution.py:16
  142.5 2.1 collective-permute-done.31.rest_22_
  144.6 1.2 collective-permute-start.27
  145.8 1.2 collective-permute-start.26
  147.0 14.5 %collective-permute-done.39.rest_30_ = f32[48,4096]{1,0:T(8,128)S(1)} collective-permute-done((f32[48,4096]{1,0:T(8,128)S(1)}, f32[48,4096]{1,0:T(8,128)S(1)}, u32[]{:S(2)}, u32[]{:S(2)}) %collective-permute-start.39) | collective-permute-done | bytes 786464 | tf_op jit(solution)/shard_map/ppermute | solution.py:16
  161.5 4.1 %collective-permute-start.35 = (f32[48,4096]{1,0:T(8,128)S(1)}, f32[48,4096]{1,0:T(8,128)S(1)}, u32[]{:S(2)}, u32[]{:S(2)}) collective-permute-start(f32[48,4096]{1,0:T(8,128)S(1)} %collective-permute-done.29.rest_20_), channel_id=1, source_target_pairs={{0,32},{32,0},{64,96},{96,64},{128,160},{160,128},{192,224},{224,1... | collective-permute-start | bytes 2359304 | tf_op jit(solution)/shard_map/ppermute | solution.py:21
  166.8 0.7 collective-permute-done.35.rest_26_
  167.5 2.2 %collective-permute-done.37.rest_28_ = f32[48,4096]{1,0:T(8,128)S(1)} collective-permute-done((f32[48,4096]{1,0:T(8,128)S(1)}, f32[48,4096]{1,0:T(8,128)S(1)}, u32[]{:S(2)}, u32[]{:S(2)}) %collective-permute-start.37) | collective-permute-done | bytes 786464 | tf_op jit(solution)/shard_map/ppermute | solution.py:21
  169.8 1.1 collective-permute-done.41.rest_32_
  170.9 1.1 collective-permute-done.42.rest_33_
  172.0 0.9 copy-done.22
  172.9 10.6 %gradient.1 = (f32[96,4096]{1,0:T(8,128)}, f32[256,128]{1,0:T(8,128)}) custom-call(f32[192,768]{1,0:T(8,128)S(1)} %bitcast.75, f32[96,4096]{1,0:T(8,128)} %bitcast.76, f32[48,4096]{1,0:T(8,128)S(1)} %copy-done.4, f32[48,4096]{1,0:T(8,128)S(1)} %copy-done.6, f32[48,4096]{1,0:T(8,128)S(1)} %bitcast.64, f32[48,4096]{1,0:T(8,128)S(1)} %bitcast.74, ...), custom_call_target="tpu_custom_call" | custom-call | flops 3623878656 | bytes 25165824 | tf_op jit(solution)/shard_map/gradient/pallas_call | solution.py:228
  183.5 11.4 %all-to-all-start = ((f32[256,1,128]{2,1,0:T(1,128)}), f32[256,1,128]{2,1,0:T(1,128)S(1)}, u32[]{:S(2)}, u32[]{:S(2)}) async-start(f32[256,1,128]{2,1,0:T(1,128)} %bitcast.19), calls=%async_computation | async-start | bytes 262144 | tf_op jit(solution)/shard_map/all_to_all | solution.py:297
  195.0 2.8 %copy.15 = f32[12,8,32,128]{3,2,1,0:T(8,128)} copy(f32[12,8,32,128]{3,1,2,0:T(8,128)} %bitcast.84) | data formatting | bytes 3145728
  197.8 10.2 %all-to-all-done = f32[256,1,128]{2,1,0:T(1,128)S(1)} async-done(((f32[256,1,128]{2,1,0:T(1,128)}), f32[256,1,128]{2,1,0:T(1,128)S(1)}, u32[]{:S(2)}, u32[]{:S(2)}) %all-to-all-start) | async-done | bytes 131104 | tf_op jit(solution)/shard_map/all_to_all | solution.py:297
  208.0 0.6 copy-done.27
  208.6 6.1 %advance.1 = (f32[96,4,8,128]{3,2,1,0:T(8,128)}, f32[96,4,8,128]{3,2,1,0:T(8,128)}) custom-call(f32[256,128]{1,0:T(8,128)} %bitcast.87, f32[96,4,8,128]{3,2,1,0:T(8,128)} %c_ref.1, f32[96,4,8,128]{3,2,1,0:T(8,128)} %d_ref.1, f32[96,4,8,128]{3,2,1,0:T(8,128)} %bitcast.77), custom_call_target="tpu_custom_call" | custom-call | flops 1572864 | bytes 7864320 | tf_op jit(solution)/shard_map/advance/pallas_call | solution.py:264
  (103 shorter events, 5.5 us)
Async XLA Ops:
  2.6 67.4 %copy-start = (f32[6,8,32,128]{3,1,2,0:T(8,128)}, f32[6,8,32,128]{3,1,2,0:T(8,128)S(1)}, u32[]{:S(2)}) copy-start(f32[6,8,32,128]{3,1,2,0:T(8,128)S(1)} %copy.21) | copy-start | bytes 2359300
  2.6 10.6 %collective-permute-start.8 = (f32[48,4096]{1,0:T(8,128)S(1)}, f32[48,4096]{1,0:T(8,128)S(1)}, u32[]{:S(2)}, u32[]{:S(2)}) collective-permute-start(f32[48,4096]{1,0:T(8,128)S(1)} %bitcast.55), channel_id=1, source_target_pairs={{0,32},{32,0},{64,96},{96,64},{128,160},{160,128},{192,224},{224,1... | collective-permute-start | bytes 2359304 | tf_op jit(solution)/shard_map/ppermute | solution.py:21
  5.9 19.1 %collective-permute-start.7 = (f32[48,4096]{1,0:T(8,128)S(1)}, f32[48,4096]{1,0:T(8,128)S(1)}, u32[]{:S(2)}, u32[]{:S(2)}) collective-permute-start(f32[48,4096]{1,0:T(8,128)S(1)} %bitcast.56), channel_id=1, source_target_pairs={{0,192},{32,224},{64,0},{96,32},{128,64},{160,96},{192,128},{224,1... | collective-permute-start | bytes 2359304 | tf_op jit(solution)/shard_map/ppermute | solution.py:16
  6.7 20.0 %collective-permute-start.4 = (f32[48,4096]{1,0:T(8,128)S(1)}, f32[48,4096]{1,0:T(8,128)}, u32[]{:S(2)}, u32[]{:S(2)}) collective-permute-start(f32[48,4096]{1,0:T(8,128)S(1)} %bitcast.57), channel_id=1, source_target_pairs={{0,64},{32,96},{64,128},{96,160},{128,192},{160,224},{192,0},{224,... | collective-permute-start | bytes 2359304 | tf_op jit(solution)/shard_map/ppermute | solution.py:16
  7.4 20.3 %collective-permute-start.1 = (f32[48,4096]{1,0:T(8,128)S(1)}, f32[48,4096]{1,0:T(8,128)S(1)}, u32[]{:S(2)}, u32[]{:S(2)}) collective-permute-start(f32[48,4096]{1,0:T(8,128)S(1)} %bitcast.58), channel_id=1, source_target_pairs={{1,0},{2,1},{3,2},{4,3},{5,4},{6,5},{7,6},{8,7},{9,8},{10,9},{11,1... | collective-permute-start | bytes 2359304 | tf_op jit(solution)/shard_map/ppermute | solution.py:285
  8.6 20.3 %collective-permute-start = (f32[48,4096]{1,0:T(8,128)S(1)}, f32[48,4096]{1,0:T(8,128)S(1)}, u32[]{:S(2)}, u32[]{:S(2)}) collective-permute-start(f32[48,4096]{1,0:T(8,128)S(1)} %bitcast.59), channel_id=1, source_target_pairs={{0,1},{1,2},{2,3},{3,4},{4,5},{5,6},{6,7},{7,8},{8,9},{9,10},{10,1... | collective-permute-start | bytes 2359304 | tf_op jit(solution)/shard_map/ppermute | solution.py:284
  13.2 56.9 %copy-start.2 = (f32[6,8,32,128]{3,1,2,0:T(8,128)}, f32[6,8,32,128]{3,1,2,0:T(8,128)S(1)}, u32[]{:S(2)}) copy-start(f32[6,8,32,128]{3,1,2,0:T(8,128)S(1)} %copy.20) | copy-start | bytes 2359300
  13.2 65.4 %copy-start.7 = (f32[48,4096]{1,0:T(8,128)}, f32[48,4096]{1,0:T(8,128)S(1)}, u32[]{:S(2)}) copy-start(f32[48,4096]{1,0:T(8,128)S(1)} %collective-permute-done.8.rest_10_.rest_8_) | copy-start | bytes 2359300
  13.2 20.0 %collective-permute-start.9 = (f32[48,4096]{1,0:T(8,128)S(1)}, f32[48,4096]{1,0:T(8,128)S(1)}, u32[]{:S(2)}, u32[]{:S(2)}) collective-permute-start(f32[48,4096]{1,0:T(8,128)S(1)} %bitcast.65), channel_id=1, source_target_pairs={{0,32},{32,0},{64,96},{96,64},{128,160},{160,128},{192,224},{224,1... | collective-permute-start | bytes 2359304 | tf_op jit(solution)/shard_map/ppermute | solution.py:21
  25.0 45.0 %copy-start.9 = (f32[48,4096]{1,0:T(8,128)}, f32[48,4096]{1,0:T(8,128)S(1)}, u32[]{:S(2)}) copy-start(f32[48,4096]{1,0:T(8,128)S(1)} %collective-permute-done.7.rest_9_.rest_7_) | copy-start | bytes 2359300
  25.0 19.6 %collective-permute-start.6 = (f32[48,4096]{1,0:T(8,128)S(1)}, f32[48,4096]{1,0:T(8,128)}, u32[]{:S(2)}, u32[]{:S(2)}) collective-permute-start(f32[48,4096]{1,0:T(8,128)S(1)} %bitcast.66), channel_id=1, source_target_pairs={{0,64},{32,96},{64,128},{96,160},{128,192},{160,224},{192,0},{224,... | collective-permute-start | bytes 2359304 | tf_op jit(solution)/shard_map/ppermute | solution.py:16
  26.7 18.0 %collective-permute-start.5 = (f32[48,4096]{1,0:T(8,128)S(1)}, f32[48,4096]{1,0:T(8,128)}, u32[]{:S(2)}, u32[]{:S(2)}) collective-permute-start(f32[48,4096]{1,0:T(8,128)S(1)} %bitcast.67), channel_id=1, source_target_pairs={{0,192},{32,224},{64,0},{96,32},{128,64},{160,96},{192,128},{224,1... | collective-permute-start | bytes 2359304 | tf_op jit(solution)/shard_map/ppermute | solution.py:16
  27.7 23.2 %copy-start.23 = (f32[48,4096]{1,0:T(8,128)}, f32[48,4096]{1,0:T(8,128)S(1)}, u32[]{:S(2)}) copy-start(f32[48,4096]{1,0:T(8,128)S(1)} %collective-permute-done.1.r_ref) | copy-start | bytes 2359300
  27.7 19.8 %collective-permute-start.3 = (f32[48,4096]{1,0:T(8,128)S(1)}, f32[48,4096]{1,0:T(8,128)S(1)}, u32[]{:S(2)}, u32[]{:S(2)}) collective-permute-start(f32[48,4096]{1,0:T(8,128)S(1)} %bitcast.68), channel_id=1, source_target_pairs={{1,0},{2,1},{3,2},{4,3},{5,4},{6,5},{7,6},{8,7},{9,8},{10,9},{11,1... | collective-permute-start | bytes 2359304 | tf_op jit(solution)/shard_map/ppermute | solution.py:285
  29.0 23.1 %copy-start.24 = (f32[48,4096]{1,0:T(8,128)}, f32[48,4096]{1,0:T(8,128)S(1)}, u32[]{:S(2)}) copy-start(f32[48,4096]{1,0:T(8,128)S(1)} %collective-permute-done.l_ref) | copy-start | bytes 2359300
  29.0 20.7 %collective-permute-start.2 = (f32[48,4096]{1,0:T(8,128)S(1)}, f32[48,4096]{1,0:T(8,128)S(1)}, u32[]{:S(2)}, u32[]{:S(2)}) collective-permute-start(f32[48,4096]{1,0:T(8,128)S(1)} %bitcast.69), channel_id=1, source_target_pairs={{0,1},{1,2},{2,3},{3,4},{4,5},{5,6},{6,7},{7,8},{8,9},{9,10},{10,1... | collective-permute-start | bytes 2359304 | tf_op jit(solution)/shard_map/ppermute | solution.py:284
  34.1 16.8 %collective-permute-start.13 = (f32[48,4096]{1,0:T(8,128)S(1)}, f32[48,4096]{1,0:T(8,128)S(1)}, u32[]{:S(2)}, u32[]{:S(2)}) collective-permute-start(f32[48,4096]{1,0:T(8,128)S(1)} %collective-permute-done.7.rest_9_.rest_7_), channel_id=1, source_target_pairs={{0,32},{32,0},{64,96},{96,64},{128,160},{160,128},{192,224},{224,1... | collective-permute-start | bytes 2359304 | tf_op jit(solution)/shard_map/ppermute | solution.py:21
  44.6 18.9 %collective-permute-start.14 = (f32[48,4096]{1,0:T(8,128)}, f32[48,4096]{1,0:T(8,128)}, u32[]{:S(2)}, u32[]{:S(2)}) collective-permute-start(f32[48,4096]{1,0:T(8,128)} %collective-permute-done.4.rest_6_.rest_4_), channel_id=1, source_target_pairs={{0,64},{32,96},{64,128},{96,160},{128,192},{160,224},{192,0},{224,... | collective-permute-start | bytes 2359304 | tf_op jit(solution)/shard_map/ppermute | solution.py:16
  44.7 21.4 %collective-permute-start.15 = (f32[48,4096]{1,0:T(8,128)}, f32[48,4096]{1,0:T(8,128)}, u32[]{:S(2)}, u32[]{:S(2)}) collective-permute-start(f32[48,4096]{1,0:T(8,128)} %collective-permute-done.5.rest_7_.rest_5_), channel_id=1, source_target_pairs={{0,192},{32,224},{64,0},{96,32},{128,64},{160,96},{192,128},{224,1... | collective-permute-start | bytes 2359304 | tf_op jit(solution)/shard_map/ppermute | solution.py:16
  47.4 16.1 %copy-start.25 = (f32[48,4096]{1,0:T(8,128)}, f32[48,4096]{1,0:T(8,128)S(1)}, u32[]{:S(2)}) copy-start(f32[48,4096]{1,0:T(8,128)S(1)} %collective-permute-done.3.r_ref) | copy-start | bytes 2359300
  47.5 31.1 %collective-permute-start.10 = (f32[48,4096]{1,0:T(8,128)}, f32[48,4096]{1,0:T(8,128)}, u32[]{:S(2)}, u32[]{:S(2)}) collective-permute-start(f32[48,4096]{1,0:T(8,128)} %collective-permute-done.4.rest_6_.rest_4_), channel_id=1, source_target_pairs={{0,32},{32,0},{64,96},{96,64},{128,160},{160,128},{192,224},{224,1... | collective-permute-start | bytes 2359304 | tf_op jit(solution)/shard_map/ppermute | solution.py:21
  49.7 16.4 %copy-start.26 = (f32[48,4096]{1,0:T(8,128)}, f32[48,4096]{1,0:T(8,128)S(1)}, u32[]{:S(2)}) copy-start(f32[48,4096]{1,0:T(8,128)S(1)} %collective-permute-done.2.l_ref) | copy-start | bytes 2359300
  49.7 28.9 %collective-permute-start.12 = (f32[48,4096]{1,0:T(8,128)}, f32[48,4096]{1,0:T(8,128)}, u32[]{:S(2)}, u32[]{:S(2)}) collective-permute-start(f32[48,4096]{1,0:T(8,128)} %collective-permute-done.6.rest_8_.rest_6_), channel_id=1, source_target_pairs={{0,32},{32,0},{64,96},{96,64},{128,160},{160,128},{192,224},{224,1... | collective-permute-start | bytes 2359304 | tf_op jit(solution)/shard_map/ppermute | solution.py:21
  51.8 26.7 %collective-permute-start.11 = (f32[48,4096]{1,0:T(8,128)}, f32[48,4096]{1,0:T(8,128)}, u32[]{:S(2)}, u32[]{:S(2)}) collective-permute-start(f32[48,4096]{1,0:T(8,128)} %collective-permute-done.5.rest_7_.rest_5_), channel_id=1, source_target_pairs={{0,32},{32,0},{64,96},{96,64},{128,160},{160,128},{192,224},{224,1... | collective-permute-start | bytes 2359304 | tf_op jit(solution)/shard_map/ppermute | solution.py:21
  63.5 26.5 %collective-permute-start.16 = (f32[48,4096]{1,0:T(8,128)}, f32[48,4096]{1,0:T(8,128)}, u32[]{:S(2)}, u32[]{:S(2)}) collective-permute-start(f32[48,4096]{1,0:T(8,128)} %collective-permute-done.14.rest_4_.rest_14_), channel_id=1, source_target_pairs={{0,32},{32,0},{64,96},{96,64},{128,160},{160,128},{192,224},{224,1... | collective-permute-start | bytes 2359304 | tf_op jit(solution)/shard_map/ppermute | solution.py:21
  66.1 24.0 %collective-permute-start.17 = (f32[48,4096]{1,0:T(8,128)}, f32[48,4096]{1,0:T(8,128)}, u32[]{:S(2)}, u32[]{:S(2)}) collective-permute-start(f32[48,4096]{1,0:T(8,128)} %collective-permute-done.15.rest_5_.rest_15_), channel_id=1, source_target_pairs={{0,32},{32,0},{64,96},{96,64},{128,160},{160,128},{192,224},{224,1... | collective-permute-start | bytes 2359304 | tf_op jit(solution)/shard_map/ppermute | solution.py:21
  74.2 4.3 %copy-start.1 = (f32[6,8,32,128]{3,1,2,0:T(8,128)S(1)}, f32[6,8,32,128]{3,1,2,0:T(8,128)}, u32[]{:S(2)}) copy-start(f32[6,8,32,128]{3,1,2,0:T(8,128)} %copy-done) | copy-start | bytes 2359300
  74.2 4.4 %copy-start.3 = (f32[6,8,32,128]{3,1,2,0:T(8,128)S(1)}, f32[6,8,32,128]{3,1,2,0:T(8,128)}, u32[]{:S(2)}) copy-start(f32[6,8,32,128]{3,1,2,0:T(8,128)} %copy-done.2) | copy-start | bytes 2359300
  74.2 4.4 %copy-start.4 = (f32[48,4096]{1,0:T(8,128)S(1)}, f32[48,4096]{1,0:T(8,128)}, u32[]{:S(2)}) copy-start(f32[48,4096]{1,0:T(8,128)} %hamiltonian.2.rest_2_.rest_0_.rest_18_) | copy-start | bytes 2359300
  78.6 1.1 copy-start.5
  94.3 14.0 %copy-start.6 = (f32[48,4096]{1,0:T(8,128)S(1)}, f32[48,4096]{1,0:T(8,128)}, u32[]{:S(2)}) copy-start(f32[48,4096]{1,0:T(8,128)} %hamiltonian.3.rest_3_.rest_1_.rest_19_) | copy-start | bytes 2359300
  94.4 4.8 %copy-start.18 = (f32[192,768]{1,0:T(8,128)}, f32[192,768]{1,0:T(8,128)S(1)}, u32[]{:S(2)}) copy-start(f32[192,768]{1,0:T(8,128)S(1)} %pad_maximum_fusion) | copy-start | bytes 1769476
  95.2 8.0 %collective-permute-start.18 = (f32[2,24,768]{2,1,0:T(8,128)}, f32[2,24,768]{2,1,0:T(8,128)S(1)}, u32[]{:S(2)}, u32[]{:S(2)}) collective-permute-start(f32[2,24,768]{2,1,0:T(8,128)} %get-tuple-element.17), channel_id=1, source_target_pairs={{0,3},{1,2},{2,1},{3,0},{4,7},{5,6},{6,5},{7,4},{8,11},{9,10},{10,... | collective-permute-start | bytes 442376 | tf_op jit(solution)/shard_map/ppermute | solution.py:26
  98.9 9.4 %collective-permute-start.20 = (f32[2,24,768]{2,1,0:T(8,128)}, f32[2,24,768]{2,1,0:T(8,128)S(1)}, u32[]{:S(2)}, u32[]{:S(2)}) collective-permute-start(f32[2,24,768]{2,1,0:T(8,128)} %get-tuple-element.18), channel_id=1, source_target_pairs={{0,1},{1,0},{2,3},{3,2},{4,5},{5,4},{6,7},{7,6},{8,9},{9,8},{10,11... | collective-permute-start | bytes 442376 | tf_op jit(solution)/shard_map/ppermute | solution.py:26
  98.9 12.3 %collective-permute-start.19 = (f32[2,24,768]{2,1,0:T(8,128)}, f32[2,24,768]{2,1,0:T(8,128)}, u32[]{:S(2)}, u32[]{:S(2)}) collective-permute-start(f32[2,24,768]{2,1,0:T(8,128)} %get-tuple-element.19), channel_id=1, source_target_pairs={{0,2},{1,3},{2,0},{3,1},{4,6},{5,7},{6,4},{7,5},{8,10},{9,11},{10,... | collective-permute-start | bytes 442376 | tf_op jit(solution)/shard_map/ppermute | solution.py:26
  99.2 23.6 %collective-permute-start.33 = (f32[48,4096]{1,0:T(8,128)S(1)}, f32[48,4096]{1,0:T(8,128)}, u32[]{:S(2)}, u32[]{:S(2)}) collective-permute-start(f32[48,4096]{1,0:T(8,128)S(1)} %copy-done.4), channel_id=1, source_target_pairs={{0,32},{32,0},{64,96},{96,64},{128,160},{160,128},{192,224},{224,1... | collective-permute-start | bytes 2359304 | tf_op jit(solution)/shard_map/ppermute | solution.py:21
  100.0 23.2 %collective-permute-start.32 = (f32[48,4096]{1,0:T(8,128)S(1)}, f32[48,4096]{1,0:T(8,128)}, u32[]{:S(2)}, u32[]{:S(2)}) collective-permute-start(f32[48,4096]{1,0:T(8,128)S(1)} %copy-done.4), channel_id=1, source_target_pairs={{0,192},{32,224},{64,0},{96,32},{128,64},{160,96},{192,128},{224,1... | collective-permute-start | bytes 2359304 | tf_op jit(solution)/shard_map/ppermute | solution.py:16
  103.1 28.5 %collective-permute-start.29 = (f32[48,4096]{1,0:T(8,128)S(1)}, f32[48,4096]{1,0:T(8,128)S(1)}, u32[]{:S(2)}, u32[]{:S(2)}) collective-permute-start(f32[48,4096]{1,0:T(8,128)S(1)} %copy-done.4), channel_id=1, source_target_pairs={{0,64},{32,96},{64,128},{96,160},{128,192},{160,224},{192,0},{224,... | collective-permute-start | bytes 2359304 | tf_op jit(solution)/shard_map/ppermute | solution.py:16
  108.3 29.1 %collective-permute-start.30 = (f32[48,4096]{1,0:T(8,128)S(1)}, f32[48,4096]{1,0:T(8,128)S(1)}, u32[]{:S(2)}, u32[]{:S(2)}) collective-permute-start(f32[48,4096]{1,0:T(8,128)S(1)} %copy-done.6), channel_id=1, source_target_pairs={{0,192},{32,224},{64,0},{96,32},{128,64},{160,96},{192,128},{224,1... | collective-permute-start | bytes 2359304 | tf_op jit(solution)/shard_map/ppermute | solution.py:16
  111.2 61.7 %copy-start.17 = (f32[48,4096]{1,0:T(8,128)S(1)}, f32[48,4096]{1,0:T(8,128)}, u32[]{:S(2)}) copy-start(f32[48,4096]{1,0:T(8,128)} %copy-done.15) | copy-start | bytes 2359300
  112.3 60.6 %copy-start.8 = (f32[48,4096]{1,0:T(8,128)S(1)}, f32[48,4096]{1,0:T(8,128)}, u32[]{:S(2)}) copy-start(f32[48,4096]{1,0:T(8,128)} %copy-done.7) | copy-start | bytes 2359300
  112.3 60.6 %copy-start.11 = (f32[48,4096]{1,0:T(8,128)S(1)}, f32[48,4096]{1,0:T(8,128)}, u32[]{:S(2)}) copy-start(f32[48,4096]{1,0:T(8,128)} %copy-done.9) | copy-start | bytes 2359300
  112.4 60.6 %copy-start.14 = (f32[48,4096]{1,0:T(8,128)S(1)}, f32[48,4096]{1,0:T(8,128)}, u32[]{:S(2)}) copy-start(f32[48,4096]{1,0:T(8,128)} %copy-done.12) | copy-start | bytes 2359300
  112.4 7.6 %collective-permute-start.21 = (f32[24,768]{1,0:T(8,128)S(1)}, f32[24,768]{1,0:T(8,128)S(1)}, u32[]{:S(2)}, u32[]{:S(2)}) collective-permute-start(f32[24,768]{1,0:T(8,128)S(1)} %select_bitcast_fusion), channel_id=1, source_target_pairs={{0,4},{1,5},{2,6},{3,7},{4,0},{5,1},{6,2},{7,3},{8,12},{9,13},{10,... | collective-permute-start | bytes 221192 | tf_op jit(solution)/shard_map/ppermute | solution.py:26
  120.0 4.2 %collective-permute-start.24 = (f32[24,768]{1,0:T(8,128)S(1)}, f32[24,768]{1,0:T(8,128)S(1)}, u32[]{:S(2)}, u32[]{:S(2)}) collective-permute-start(f32[24,768]{1,0:T(8,128)S(1)} %bitcast_add_fusion.1), channel_id=1, source_target_pairs={{0,24},{1,25},{2,26},{3,27},{4,28},{5,29},{6,30},{7,31},{8,0},{9,1... | collective-permute-start | bytes 221192 | tf_op jit(solution)/shard_map/ppermute | solution.py:31
  122.8 4.8 %collective-permute-start.23 = (f32[24,768]{1,0:T(8,128)S(1)}, f32[24,768]{1,0:T(8,128)S(1)}, u32[]{:S(2)}, u32[]{:S(2)}) collective-permute-start(f32[24,768]{1,0:T(8,128)S(1)} %bitcast_add_fusion.1), channel_id=1, source_target_pairs={{0,16},{1,17},{2,18},{3,19},{4,20},{5,21},{6,22},{7,23},{8,24},{9,... | collective-permute-start | bytes 221192 | tf_op jit(solution)/shard_map/ppermute | solution.py:31
  123.1 5.2 %collective-permute-start.22 = (f32[24,768]{1,0:T(8,128)S(1)}, f32[24,768]{1,0:T(8,128)S(1)}, u32[]{:S(2)}, u32[]{:S(2)}) collective-permute-start(f32[24,768]{1,0:T(8,128)S(1)} %bitcast_add_fusion.1), channel_id=1, source_target_pairs={{0,8},{1,9},{2,10},{3,11},{4,12},{5,13},{6,14},{7,15},{8,16},{9,17... | collective-permute-start | bytes 221192 | tf_op jit(solution)/shard_map/ppermute | solution.py:31
  124.2 18.2 %collective-permute-start.34 = (f32[48,4096]{1,0:T(8,128)S(1)}, f32[48,4096]{1,0:T(8,128)S(1)}, u32[]{:S(2)}, u32[]{:S(2)}) collective-permute-start(f32[48,4096]{1,0:T(8,128)S(1)} %copy-done.6), channel_id=1, source_target_pairs={{0,32},{32,0},{64,96},{96,64},{128,160},{160,128},{192,224},{224,1... | collective-permute-start | bytes 2359304 | tf_op jit(solution)/shard_map/ppermute | solution.py:21
  127.6 17.0 %collective-permute-start.31 = (f32[48,4096]{1,0:T(8,128)S(1)}, f32[48,4096]{1,0:T(8,128)S(1)}, u32[]{:S(2)}, u32[]{:S(2)}) collective-permute-start(f32[48,4096]{1,0:T(8,128)S(1)} %copy-done.6), channel_id=1, source_target_pairs={{0,64},{32,96},{64,128},{96,160},{128,192},{160,224},{192,0},{224,... | collective-permute-start | bytes 2359304 | tf_op jit(solution)/shard_map/ppermute | solution.py:16
  128.3 17.5 %collective-permute-start.38 = (f32[48,4096]{1,0:T(8,128)}, f32[48,4096]{1,0:T(8,128)S(1)}, u32[]{:S(2)}, u32[]{:S(2)}) collective-permute-start(f32[48,4096]{1,0:T(8,128)} %collective-permute-done.32.rest_23_), channel_id=1, source_target_pairs={{0,32},{32,0},{64,96},{96,64},{128,160},{160,128},{192,224},{224,1... | collective-permute-start | bytes 2359304 | tf_op jit(solution)/shard_map/ppermute | solution.py:21
  131.6 8.4 %collective-permute-start.25 = (f32[24,768]{1,0:T(8,128)S(1)}, f32[24,768]{1,0:T(8,128)S(1)}, u32[]{:S(2)}, u32[]{:S(2)}) collective-permute-start(f32[24,768]{1,0:T(8,128)S(1)} %add_add_fusion), channel_id=1, source_target_pairs={{0,4},{1,5},{2,6},{3,7},{4,0},{5,1},{6,2},{7,3},{8,12},{9,13},{10,... | collective-permute-start | bytes 221192 | tf_op jit(solution)/shard_map/ppermute | solution.py:26
  137.4 24.1 %collective-permute-start.39 = (f32[48,4096]{1,0:T(8,128)S(1)}, f32[48,4096]{1,0:T(8,128)S(1)}, u32[]{:S(2)}, u32[]{:S(2)}) collective-permute-start(f32[48,4096]{1,0:T(8,128)S(1)} %collective-permute-done.29.rest_20_), channel_id=1, source_target_pairs={{0,64},{32,96},{64,128},{96,160},{128,192},{160,224},{192,0},{224,... | collective-permute-start | bytes 2359304 | tf_op jit(solution)/shard_map/ppermute | solution.py:16
  140.0 25.6 %collective-permute-start.40 = (f32[48,4096]{1,0:T(8,128)S(1)}, f32[48,4096]{1,0:T(8,128)S(1)}, u32[]{:S(2)}, u32[]{:S(2)}) collective-permute-start(f32[48,4096]{1,0:T(8,128)S(1)} %collective-permute-done.30.rest_21_), channel_id=1, source_target_pairs={{0,192},{32,224},{64,0},{96,32},{128,64},{160,96},{192,128},{224,1... | collective-permute-start | bytes 2359304 | tf_op jit(solution)/shard_map/ppermute | solution.py:16
  142.4 23.3 %collective-permute-start.28 = (f32[2,24,768]{2,1,0:T(8,128)S(1)}, f32[2,24,768]{2,1,0:T(8,128)S(1)}, u32[]{:S(2)}, u32[]{:S(2)}) collective-permute-start(f32[2,24,768]{2,1,0:T(8,128)S(1)} %maximum_select_fusion.1), channel_id=1, source_target_pairs={{0,1},{1,0},{2,3},{3,2},{4,5},{5,4},{6,7},{7,6},{8,9},{9,8},{10,11... | collective-permute-start | bytes 442376 | tf_op jit(solution)/shard_map/ppermute | solution.py:26
  144.6 21.5 %collective-permute-start.27 = (f32[2,24,768]{2,1,0:T(8,128)S(1)}, f32[2,24,768]{2,1,0:T(8,128)S(1)}, u32[]{:S(2)}, u32[]{:S(2)}) collective-permute-start(f32[2,24,768]{2,1,0:T(8,128)S(1)} %maximum_select_fusion.1), channel_id=1, source_target_pairs={{0,2},{1,3},{2,0},{3,1},{4,6},{5,7},{6,4},{7,5},{8,10},{9,11},{10,... | collective-permute-start | bytes 442376 | tf_op jit(solution)/shard_map/ppermute | solution.py:26
  145.8 20.4 %collective-permute-start.26 = (f32[2,24,768]{2,1,0:T(8,128)S(1)}, f32[2,24,768]{2,1,0:T(8,128)S(1)}, u32[]{:S(2)}, u32[]{:S(2)}) collective-permute-start(f32[2,24,768]{2,1,0:T(8,128)S(1)} %maximum_select_fusion.1), channel_id=1, source_target_pairs={{0,3},{1,2},{2,1},{3,0},{4,7},{5,6},{6,5},{7,4},{8,11},{9,10},{10,... | collective-permute-start | bytes 442376 | tf_op jit(solution)/shard_map/ppermute | solution.py:26
  161.5 10.5 %copy-start.19 = (f32[48,4096]{1,0:T(8,128)}, f32[48,4096]{1,0:T(8,128)S(1)}, u32[]{:S(2)}) copy-start(f32[48,4096]{1,0:T(8,128)S(1)} %collective-permute-done.39.rest_30_) | copy-start | bytes 2359300
  161.5 6.0 %collective-permute-start.35 = (f32[48,4096]{1,0:T(8,128)S(1)}, f32[48,4096]{1,0:T(8,128)S(1)}, u32[]{:S(2)}, u32[]{:S(2)}) collective-permute-start(f32[48,4096]{1,0:T(8,128)S(1)} %collective-permute-done.29.rest_20_), channel_id=1, source_target_pairs={{0,32},{32,0},{64,96},{96,64},{128,160},{160,128},{192,224},{224,1... | collective-permute-start | bytes 2359304 | tf_op jit(solution)/shard_map/ppermute | solution.py:21
  165.6 6.4 %copy-start.20 = (f32[48,4096]{1,0:T(8,128)}, f32[48,4096]{1,0:T(8,128)S(1)}, u32[]{:S(2)}) copy-start(f32[48,4096]{1,0:T(8,128)S(1)} %collective-permute-done.40.rest_31_) | copy-start | bytes 2359300
  165.6 4.2 %collective-permute-start.36 = (f32[48,4096]{1,0:T(8,128)S(1)}, f32[48,4096]{1,0:T(8,128)S(1)}, u32[]{:S(2)}, u32[]{:S(2)}) collective-permute-start(f32[48,4096]{1,0:T(8,128)S(1)} %collective-permute-done.30.rest_21_), channel_id=1, source_target_pairs={{0,32},{32,0},{64,96},{96,64},{128,160},{160,128},{192,224},{224,1... | collective-permute-start | bytes 2359304 | tf_op jit(solution)/shard_map/ppermute | solution.py:21
  165.7 4.1 %collective-permute-start.37 = (f32[48,4096]{1,0:T(8,128)S(1)}, f32[48,4096]{1,0:T(8,128)S(1)}, u32[]{:S(2)}, u32[]{:S(2)}) collective-permute-start(f32[48,4096]{1,0:T(8,128)S(1)} %collective-permute-done.31.rest_22_), channel_id=1, source_target_pairs={{0,32},{32,0},{64,96},{96,64},{128,160},{160,128},{192,224},{224,1... | collective-permute-start | bytes 2359304 | tf_op jit(solution)/shard_map/ppermute | solution.py:21
  166.1 4.8 %collective-permute-start.41 = (f32[48,4096]{1,0:T(8,128)S(1)}, f32[48,4096]{1,0:T(8,128)S(1)}, u32[]{:S(2)}, u32[]{:S(2)}) collective-permute-start(f32[48,4096]{1,0:T(8,128)S(1)} %collective-permute-done.39.rest_30_), channel_id=1, source_target_pairs={{0,32},{32,0},{64,96},{96,64},{128,160},{160,128},{192,224},{224,1... | collective-permute-start | bytes 2359304 | tf_op jit(solution)/shard_map/ppermute | solution.py:21
  166.2 5.8 %collective-permute-start.42 = (f32[48,4096]{1,0:T(8,128)S(1)}, f32[48,4096]{1,0:T(8,128)S(1)}, u32[]{:S(2)}, u32[]{:S(2)}) collective-permute-start(f32[48,4096]{1,0:T(8,128)S(1)} %collective-permute-done.40.rest_31_), channel_id=1, source_target_pairs={{0,32},{32,0},{64,96},{96,64},{128,160},{160,128},{192,224},{224,1... | collective-permute-start | bytes 2359304 | tf_op jit(solution)/shard_map/ppermute | solution.py:21
  183.5 24.4 %all-to-all-start = ((f32[256,1,128]{2,1,0:T(1,128)}), f32[256,1,128]{2,1,0:T(1,128)S(1)}, u32[]{:S(2)}, u32[]{:S(2)}) async-start(f32[256,1,128]{2,1,0:T(1,128)} %bitcast.19), calls=%async_computation | async-start | bytes 262144 | tf_op jit(solution)/shard_map/all_to_all | solution.py:297
  (8 other events, 7.9 us)
where the time goes:
time: 216 us; the launch traced here: 215 us
  starting transfers between devices  81.2 us (38%)
  waiting for transfers between devices  77.2 us (36%)
  Pallas kernels  36.3 us (17%)
  local copies, waits for them, and re-layouts  17.7 us (8%)
    ppermute x12, waiting for transfers between devices, shift_orb(): return lax.ppermute(v, 'orb', [(i, (i + k) % n) for i in range(n)])  48.9 us
    ppermute x16, starting transfers between devices, swap_core(): return lax.ppermute(v, 'orb', [(i, i ^ 1) for i in range(n)])  25.1 us
    ppermute x8, starting transfers between devices, flip_z(): return lax.ppermute(v, 'dom', [(i, i ^ k) for i in range(n)])  17.9 us
    unnamed x60, local copies, waits for them, and re-layouts  15.4 us
    ppermute x12, starting transfers between devices, shift_orb(): return lax.ppermute(v, 'orb', [(i, (i + k) % n) for i in range(n)])  12.1 us
    all_to_all x1, starting transfers between devices, on_device(): lax.all_to_all(sums, ('orb', 'dom'), split_axis=0, concat_axis=0, tiled=T...  11.4 us
    pallas_call x2, Pallas kernels, gram(): pl.pallas_call(kernel, out_shape=jax.ShapeDtypeStruct((rows, total), jnp....  11.1 us
    ppermute x8, waiting for transfers between devices, flip_z(): return lax.ppermute(v, 'dom', [(i, i ^ k) for i in range(n)])  11 us
  transfers between devices with their start and end apart: 44, of which 21 were waited for; matrix products, arithmetic and copies ran while one was open for 4% of the time, Pallas kernels for 7%

commit v1 on v0

--- a/solution.py
+++ b/solution.py
@@ -21,9 +21,14 @@
     return lax.ppermute(v, "orb", [(i, i ^ 1) for i in range(n)])
 
 
-def flip_z(v, k):
+def flip_z(v):
     n = lax.axis_size("dom")
-    return lax.ppermute(v, "dom", [(i, i ^ k) for i in range(n)])
+    return lax.ppermute(v, "dom", [(i, i ^ 1) for i in range(n)])
+
+
+def shift_z(v, k):
+    n = lax.axis_size("dom")
+    return lax.ppermute(v, "dom", [(i, (i // ZS) * ZS + (i + k) % ZS) for i in range(n)])
 
 
 def shift_y(v, k):
@@ -156,26 +161,28 @@
     rows, columns = part.shape
     quad = ZS // 2
     z = lax.rem(lax.axis_index("dom"), ZS)
-    high, low = z // quad, lax.rem(z, quad)
-    pieces = part.reshape(2, quad, rows // ZS, columns)
+    even = lax.rem(z, 2) == 0
+    slot = z // 2
+    pieces = part.reshape(quad, 2, rows // ZS, columns)
+    order = sorted(range(1, quad), key=lambda k: -min(k, quad - k))
 
     def piece(k):
-        return lax.dynamic_index_in_dim(pieces, low ^ k, 1, keepdims=False)
+        return lax.dynamic_index_in_dim(pieces, lax.rem(slot + k, quad), 0, keepdims=False)
 
     total = piece(0)
-    for got in [flip_z(piece(k), k) for k in range(quad - 1, 0, -1)]:
+    for got in [shift_z(piece(k), 2 * k) for k in order]:
         total = total + got
-    other = flip_z(jnp.where(high == 0, total[1], total[0]), quad)
-    total = jnp.where(high == 0, total[0], total[1]) + other
+    other = flip_z(jnp.where(even, total[1], total[0]))
+    total = jnp.where(even, total[0], total[1]) + other
     count = lax.axis_size("dom") // ZS
     for got in [shift_y(total, k) for k in range(1, count)]:
         total = total + got
-    other = flip_z(total, quad)
-    total = jnp.where(high == 0, jnp.stack([total, other]), jnp.stack([other, total]))
+    other = flip_z(total)
+    total = jnp.where(even, jnp.stack([total, other]), jnp.stack([other, total]))
     out = jnp.zeros_like(pieces)
-    out = lax.dynamic_update_slice_in_dim(out, total[:, None], low, 1)
-    for k in range(quad - 1, 0, -1):
-        out = lax.dynamic_update_slice_in_dim(out, flip_z(total, k)[:, None], low ^ k, 1)
+    out = lax.dynamic_update_slice_in_dim(out, total[None], slot, 0)
+    for k in order:
+        out = lax.dynamic_update_slice_in_dim(out, shift_z(total, 2 * k)[None], lax.rem(slot - k + quad, quad), 0)
     return out.reshape(rows, columns)
 
 
@@ -249,7 +256,7 @@
 
 
 def advance(sums, orbitals, prev_direction, grad):
-    step = 16
+    step = 48
     rows = orbitals.shape[0]
 
     def kernel(s_ref, c_ref, d_ref, g_ref, new_ref, dir_ref):

time: 216 us -> 219 us (1.014)
  local copies, waits for them, and re-layouts: 17.7 us -> 27.8 us
  starting transfers between devices: 81.2 us -> 72.6 us
  waiting for transfers between devices: 77.2 us -> 80.2 us
    unnamed x60 -> x68, local copies, waits for them, and re-layouts: 15.4 us -> 23.6 us
    ppermute x8, starting transfers between devices: 17.9 us -> 13.7 us  [the longest x6 13.5 us: shift_z(): lax.ppermute(v, 'dom', [(i, i // ZS * ZS + (i + k) % ZS) for i in range(n)])]
    all_to_all x1, starting transfers between devices: 11.4 us -> 7.22 us  [on_device(): lax.all_to_all(sums, ('orb', 'dom'), split_axis=0, concat_axis=0, tiled=T...]
    ppermute x12, waiting for transfers between devices: 48.9 us -> 51.6 us  [shift_orb(): return lax.ppermute(v, 'orb', [(i, (i + k) % n) for i in range(n)])]
  transfers between devices with their start and end apart: 44 -> 44, of which waited for: 21 -> 18; matrix products, arithmetic and copies ran while one was open for 4% -> 5% of each run, Pallas kernels for 7% -> 7%
where the time goes in v1:
time: 219 us; the launch traced here: 218 us
  waiting for transfers between devices  80.2 us (37%)
  starting transfers between devices  72.6 us (33%)
  Pallas kernels  34.3 us (16%)
  local copies, waits for them, and re-layouts  27.8 us (13%)
    ppermute x12, waiting for transfers between devices, shift_orb(): return lax.ppermute(v, 'orb', [(i, (i + k) % n) for i in range(n)])  51.6 us
    ppermute x16, starting transfers between devices, swap_core(): return lax.ppermute(v, 'orb', [(i, i ^ 1) for i in range(n)])  24 us
    unnamed x68, local copies, waits for them, and re-layouts  23.6 us
    ppermute x6, starting transfers between devices, shift_z(): lax.ppermute(v, 'dom', [(i, i // ZS * ZS + (i + k) % ZS) for i in range(n)])  13.5 us
    ppermute x12, starting transfers between devices, shift_orb(): return lax.ppermute(v, 'orb', [(i, (i + k) % n) for i in range(n)])  13 us
    pallas_call x2, Pallas kernels, gram(): pl.pallas_call(kernel, out_shape=jax.ShapeDtypeStruct((rows, total), jnp....  11.1 us
    pallas_call x1, Pallas kernels, gradient_of(): pl.pallas_call(kernel, out_shape=(jax.ShapeDtypeStruct((own, cells), jnp....  10.7 us
    all_to_all x1, waiting for transfers between devices, on_device(): lax.all_to_all(sums, ('orb', 'dom'), split_axis=0, concat_axis=0, tiled=T...  10.2 us
  transfers between devices with their start and end apart: 44, of which 18 were waited for; matrix products, arithmetic and copies ran while one was open for 5% of the time, Pallas kernels for 7%

profile of v1, /device:TPU:1, one launch (start us, length us, event | category | flops | bytes accessed | tf_op | source)
XLA Modules:
  0.0 217.8 jit_solution(14873859258974032522)
XLA Ops:
  0.6 1.5 fusion.3
  2.6 3.3 %collective-permute-start.8 = (f32[48,4096]{1,0:T(8,128)S(1)}, f32[48,4096]{1,0:T(8,128)S(1)}, u32[]{:S(2)}, u32[]{:S(2)}) collective-permute-start(f32[48,4096]{1,0:T(8,128)S(1)} %bitcast.51), channel_id=1, source_target_pairs={{0,32},{32,0},{64,96},{96,64},{128,160},{160,128},{192,224},{224,1... | collective-permute-start | bytes 2359304 | tf_op jit(solution)/shard_map/ppermute | solution.py:21
  7.4 1.3 collective-permute-start.1
  8.6 4.0 %collective-permute-start = (f32[48,4096]{1,0:T(8,128)S(1)}, f32[48,4096]{1,0:T(8,128)S(1)}, u32[]{:S(2)}, u32[]{:S(2)}) collective-permute-start(f32[48,4096]{1,0:T(8,128)S(1)} %bitcast.55), channel_id=1, source_target_pairs={{0,1},{1,2},{2,3},{3,4},{4,5},{5,6},{6,7},{7,8},{8,9},{9,10},{10,1... | collective-permute-start | bytes 2359304 | tf_op jit(solution)/shard_map/ppermute | solution.py:291
  13.2 1.3 collective-permute-start.9
  14.5 10.5 %collective-permute-done.7.rest_9_.rest_7_ = f32[48,4096]{1,0:T(8,128)S(1)} collective-permute-done((f32[48,4096]{1,0:T(8,128)S(1)}, f32[48,4096]{1,0:T(8,128)S(1)}, u32[]{:S(2)}, u32[]{:S(2)}) %collective-permute-start.7) | collective-permute-done | bytes 786464 | tf_op jit(solution)/shard_map/ppermute | solution.py:16
  25.0 1.7 collective-permute-done.4.rest_6_.rest_4_
  26.7 1.0 collective-permute-start.5
  27.7 1.3 collective-permute-start.3
  29.0 4.2 %collective-permute-start.2 = (f32[48,4096]{1,0:T(8,128)S(1)}, f32[48,4096]{1,0:T(8,128)S(1)}, u32[]{:S(2)}, u32[]{:S(2)}) collective-permute-start(f32[48,4096]{1,0:T(8,128)S(1)} %bitcast.65), channel_id=1, source_target_pairs={{0,1},{1,2},{2,3},{3,4},{4,5},{5,6},{6,7},{7,8},{8,9},{9,10},{10,1... | collective-permute-start | bytes 2359304 | tf_op jit(solution)/shard_map/ppermute | solution.py:291
  34.1 1.9 collective-permute-start.13
  36.0 8.6 %collective-permute-done.6.rest_8_.rest_6_ = f32[48,4096]{1,0:T(8,128)} collective-permute-done((f32[48,4096]{1,0:T(8,128)S(1)}, f32[48,4096]{1,0:T(8,128)}, u32[]{:S(2)}, u32[]{:S(2)}) %collective-permute-start.6) | collective-permute-done | bytes 786464 | tf_op jit(solution)/shard_map/ppermute | solution.py:16
  44.7 2.6 %collective-permute-start.15 = (f32[48,4096]{1,0:T(8,128)}, f32[48,4096]{1,0:T(8,128)}, u32[]{:S(2)}, u32[]{:S(2)}) collective-permute-start(f32[48,4096]{1,0:T(8,128)} %collective-permute-done.5.rest_7_.rest_5_), channel_id=1, source_target_pairs={{0,192},{32,224},{64,0},{96,32},{128,64},{160,96},{192,128},{224,1... | collective-permute-start | bytes 2359304 | tf_op jit(solution)/shard_map/ppermute | solution.py:16
  47.5 2.2 %collective-permute-start.10 = (f32[48,4096]{1,0:T(8,128)}, f32[48,4096]{1,0:T(8,128)}, u32[]{:S(2)}, u32[]{:S(2)}) collective-permute-start(f32[48,4096]{1,0:T(8,128)} %collective-permute-done.4.rest_6_.rest_4_), channel_id=1, source_target_pairs={{0,32},{32,0},{64,96},{96,64},{128,160},{160,128},{192,224},{224,1... | collective-permute-start | bytes 2359304 | tf_op jit(solution)/shard_map/ppermute | solution.py:21
  49.7 1.2 collective-permute-start.12
  50.9 0.9 copy-done.15
  52.1 11.4 %collective-permute-done.14.rest_4_.rest_14_ = f32[48,4096]{1,0:T(8,128)} collective-permute-done((f32[48,4096]{1,0:T(8,128)}, f32[48,4096]{1,0:T(8,128)}, u32[]{:S(2)}, u32[]{:S(2)}) %collective-permute-start.14) | collective-permute-done | bytes 786464 | tf_op jit(solution)/shard_map/ppermute | solution.py:16
  63.5 2.6 %collective-permute-start.16 = (f32[48,4096]{1,0:T(8,128)}, f32[48,4096]{1,0:T(8,128)}, u32[]{:S(2)}, u32[]{:S(2)}) collective-permute-start(f32[48,4096]{1,0:T(8,128)} %collective-permute-done.14.rest_4_.rest_14_), channel_id=1, source_target_pairs={{0,32},{32,0},{64,96},{96,64},{128,160},{160,128},{192,224},{224,1... | collective-permute-start | bytes 2359304 | tf_op jit(solution)/shard_map/ppermute | solution.py:21
  66.4 3.6 %copy.15 = f32[12,8,32,128]{3,1,2,0:T(8,128)} copy(f32[12,8,32,128]{3,2,1,0:T(8,128)} %bitcast.79) | data formatting | bytes 3145728
  70.0 4.2 %hamiltonian.2.rest_2_.rest_0_.rest_18_ = f32[48,4096]{1,0:T(8,128)} custom-call(f32[48,4096]{1,0:T(8,128)} %bitcast.56, f32[48,4096]{1,0:T(8,128)} %copy-done.28, f32[48,4096]{1,0:T(8,128)} %copy-done.27, f32[1,4096]{1,0:T(1,128)} %bitcast.86), custom_call_target="tpu_custom_call" | custom-call | flops 7864320 | bytes 3145728 | tf_op jit(solution)/shard_map/hamiltonian/pallas_call | solution.py:90
  74.2 4.3 %hamiltonian.3.rest_3_.rest_1_.rest_19_ = f32[48,4096]{1,0:T(8,128)} custom-call(f32[48,4096]{1,0:T(8,128)} %bitcast.66, f32[48,4096]{1,0:T(8,128)} %copy-done.30, f32[48,4096]{1,0:T(8,128)} %copy-done.29, f32[1,4096]{1,0:T(1,128)} %bitcast.87), custom_call_target="tpu_custom_call" | custom-call | flops 7864320 | bytes 3145728 | tf_op jit(solution)/shard_map/hamiltonian/pallas_call | solution.py:90
  78.6 1.1 copy-done.5
  79.7 1.1 copy-done.10
  80.8 1.1 copy-done.13
  82.0 1.1 copy-done.16
  83.1 6.9 %gram.2 = f32[192,576]{1,0:T(8,128)S(1)} custom-call(f32[48,4096]{1,0:T(8,128)S(1)} %bitcast.57, f32[48,4096]{1,0:T(8,128)S(1)} %bitcast.67, f32[48,4096]{1,0:T(8,128)S(1)} %copy-done.4, f32[48,4096]{1,0:T(8,128)S(1)} %copy-done.5, f32[48,4096]{1,0:T(8,128)S(1)} %bitcast.58, f32[48,4096]{1,0:T(8,128)S(1)} %bitcast.68, ...), custom_call_target="tpu_custom_call" | custom-call | flops 2717908992 | bytes 12582912 | tf_op jit(solution)/shard_map/gram/pallas_call | solution.py:141
  90.0 4.2 %gram.3 = f32[192,192]{1,0:T(8,128)S(1)} custom-call(f32[48,4096]{1,0:T(8,128)S(1)} %bitcast.59, f32[48,4096]{1,0:T(8,128)S(1)} %bitcast.69, f32[48,4096]{1,0:T(8,128)S(1)} %copy-done.4, f32[48,4096]{1,0:T(8,128)S(1)} %copy-done.5, f32[48,4096]{1,0:T(8,128)} %collective-permute-done.14.rest_4_.rest_14_, f32[48,4096]{1,0:T(8,128)} %collective-permute-done.15.rest_5_.rest_15_, ...), custom_call_target="tpu_custom_call" | custom-call | flops 905969664 | bytes 6291456 | tf_op jit(solution)/shard_map/gram/pallas_call | solution.py:141
  95.1 6.3 %collective-permute-start.18 = (f32[2,24,768]{2,1,0:T(8,128)}, f32[2,24,768]{2,1,0:T(8,128)S(1)}, u32[]{:S(2)}, u32[]{:S(2)}) collective-permute-start(f32[2,24,768]{2,1,0:T(8,128)} %get-tuple-element.17), channel_id=1, source_target_pairs={{0,4},{1,5},{2,6},{3,7},{4,0},{5,1},{6,2},{7,3},{8,12},{9,13},{10,... | collective-permute-start | bytes 442376 | tf_op jit(solution)/shard_map/ppermute | solution.py:31
  101.4 2.4 %collective-permute-start.19 = (f32[2,24,768]{2,1,0:T(8,128)}, f32[2,24,768]{2,1,0:T(8,128)}, u32[]{:S(2)}, u32[]{:S(2)}) collective-permute-start(f32[2,24,768]{2,1,0:T(8,128)} %get-tuple-element.19), channel_id=1, source_target_pairs={{0,2},{1,3},{2,4},{3,5},{4,6},{5,7},{6,0},{7,1},{8,10},{9,11},{10,... | collective-permute-start | bytes 442376 | tf_op jit(solution)/shard_map/ppermute | solution.py:31
  103.8 1.1 collective-permute-start.33
  104.8 2.2 collective-permute-start.32
  107.0 8.9 %collective-permute-done.20 = f32[2,24,768]{2,1,0:T(8,128)S(1)} collective-permute-done((f32[2,24,768]{2,1,0:T(8,128)}, f32[2,24,768]{2,1,0:T(8,128)S(1)}, u32[]{:S(2)}, u32[]{:S(2)}) %collective-permute-start.20) | collective-permute-done | bytes 147488 | tf_op jit(solution)/shard_map/ppermute | solution.py:31
  116.0 2.4 %collective-permute-start.30 = (f32[48,4096]{1,0:T(8,128)S(1)}, f32[48,4096]{1,0:T(8,128)}, u32[]{:S(2)}, u32[]{:S(2)}) collective-permute-start(f32[48,4096]{1,0:T(8,128)S(1)} %copy-done.6), channel_id=1, source_target_pairs={{0,192},{32,224},{64,0},{96,32},{128,64},{160,96},{192,128},{224,1... | collective-permute-start | bytes 2359304 | tf_op jit(solution)/shard_map/ppermute | solution.py:16
  118.4 1.0 fusion.2
  119.5 3.6 %collective-permute-done.21 = f32[24,768]{1,0:T(8,128)S(1)} collective-permute-done((f32[24,768]{1,0:T(8,128)S(1)}, f32[24,768]{1,0:T(8,128)S(1)}, u32[]{:S(2)}, u32[]{:S(2)}) %collective-permute-start.21) | collective-permute-done | bytes 73760 | tf_op jit(solution)/shard_map/ppermute | solution.py:26
  123.1 2.8 %collective-permute-start.24 = (f32[24,768]{1,0:T(8,128)S(1)}, f32[24,768]{1,0:T(8,128)S(1)}, u32[]{:S(2)}, u32[]{:S(2)}) collective-permute-start(f32[24,768]{1,0:T(8,128)S(1)} %bitcast_add_fusion.1), channel_id=1, source_target_pairs={{0,24},{1,25},{2,26},{3,27},{4,28},{5,29},{6,30},{7,31},{8,0},{9,1... | collective-permute-start | bytes 221192 | tf_op jit(solution)/shard_map/ppermute | solution.py:36
  127.4 2.2 %collective-permute-start.34 = (f32[48,4096]{1,0:T(8,128)S(1)}, f32[48,4096]{1,0:T(8,128)S(1)}, u32[]{:S(2)}, u32[]{:S(2)}) collective-permute-start(f32[48,4096]{1,0:T(8,128)S(1)} %copy-done.6), channel_id=1, source_target_pairs={{0,32},{32,0},{64,96},{96,64},{128,160},{160,128},{192,224},{224,1... | collective-permute-start | bytes 2359304 | tf_op jit(solution)/shard_map/ppermute | solution.py:21
  129.6 1.1 collective-permute-done.23
  131.5 2.8 %collective-permute-start.38 = (f32[48,4096]{1,0:T(8,128)}, f32[48,4096]{1,0:T(8,128)S(1)}, u32[]{:S(2)}, u32[]{:S(2)}) collective-permute-start(f32[48,4096]{1,0:T(8,128)} %collective-permute-done.32.rest_23_), channel_id=1, source_target_pairs={{0,32},{32,0},{64,96},{96,64},{128,160},{160,128},{192,224},{224,1... | collective-permute-start | bytes 2359304 | tf_op jit(solution)/shard_map/ppermute | solution.py:21
  134.4 6.5 %collective-permute-done.30.rest_21_ = f32[48,4096]{1,0:T(8,128)} collective-permute-done((f32[48,4096]{1,0:T(8,128)S(1)}, f32[48,4096]{1,0:T(8,128)}, u32[]{:S(2)}, u32[]{:S(2)}) %collective-permute-start.30) | collective-permute-done | bytes 786464 | tf_op jit(solution)/shard_map/ppermute | solution.py:16
  140.9 3.4 %collective-permute-start.40 = (f32[48,4096]{1,0:T(8,128)}, f32[48,4096]{1,0:T(8,128)}, u32[]{:S(2)}, u32[]{:S(2)}) collective-permute-start(f32[48,4096]{1,0:T(8,128)} %collective-permute-done.30.rest_21_), channel_id=1, source_target_pairs={{0,192},{32,224},{64,0},{96,32},{128,64},{160,96},{192,128},{224,1... | collective-permute-start | bytes 2359304 | tf_op jit(solution)/shard_map/ppermute | solution.py:16
  145.0 0.9 copy-done.18
  145.8 0.9 collective-permute-start.28
  146.8 1.5 collective-permute-done.31.rest_22_
  149.8 0.9 copy-done.22
  150.6 3.3 %collective-permute-start.26 = (f32[2,24,768]{2,1,0:T(8,128)}, f32[2,24,768]{2,1,0:T(8,128)}, u32[]{:S(2)}, u32[]{:S(2)}) collective-permute-start(f32[2,24,768]{2,1,0:T(8,128)} %maximum_select_fusion.1), channel_id=1, source_target_pairs={{0,4},{1,5},{2,6},{3,7},{4,0},{5,1},{6,2},{7,3},{8,12},{9,13},{10,... | collective-permute-start | bytes 442376 | tf_op jit(solution)/shard_map/ppermute | solution.py:31
  153.9 11.3 %collective-permute-done.39.rest_30_ = f32[48,4096]{1,0:T(8,128)} collective-permute-done((f32[48,4096]{1,0:T(8,128)}, f32[48,4096]{1,0:T(8,128)}, u32[]{:S(2)}, u32[]{:S(2)}) %collective-permute-start.39) | collective-permute-done | bytes 786464 | tf_op jit(solution)/shard_map/ppermute | solution.py:16
  165.2 3.6 %collective-permute-start.35 = (f32[48,4096]{1,0:T(8,128)}, f32[48,4096]{1,0:T(8,128)S(1)}, u32[]{:S(2)}, u32[]{:S(2)}) collective-permute-start(f32[48,4096]{1,0:T(8,128)} %collective-permute-done.29.rest_20_), channel_id=1, source_target_pairs={{0,32},{32,0},{64,96},{96,64},{128,160},{160,128},{192,224},{224,1... | collective-permute-start | bytes 2359304 | tf_op jit(solution)/shard_map/ppermute | solution.py:21
  170.1 0.9 bitcast_dynamic-update-slice_fusion.2
  171.1 0.9 bitcast_dynamic-update-slice_fusion.1
  172.0 1.2 collective-permute-done.37.rest_28_
  173.2 1.1 collective-permute-done.41.rest_32_
  174.4 1.1 collective-permute-done.42.rest_33_
  175.5 0.9 copy-done.26
  176.4 1.1 copy-done.14
  177.6 1.1 copy-done.17
  178.7 1.1 copy-done.19
  179.8 1.1 copy-done.21
  181.0 1.1 copy-done.23
  182.1 10.7 %gradient.1 = (f32[96,4096]{1,0:T(8,128)}, f32[256,128]{1,0:T(8,128)}) custom-call(f32[192,768]{1,0:T(8,128)S(1)} %bitcast.71, f32[96,4096]{1,0:T(8,128)} %bitcast.72, f32[48,4096]{1,0:T(8,128)S(1)} %copy-done.4, f32[48,4096]{1,0:T(8,128)S(1)} %copy-done.6, f32[48,4096]{1,0:T(8,128)S(1)} %bitcast.60, f32[48,4096]{1,0:T(8,128)S(1)} %bitcast.70, ...), custom_call_target="tpu_custom_call" | custom-call | flops 3623878656 | bytes 25165824 | tf_op jit(solution)/shard_map/gradient/pallas_call | solution.py:235
  192.8 7.2 %all-to-all-start = ((f32[256,1,128]{2,1,0:T(1,128)}), f32[256,1,128]{2,1,0:T(1,128)S(1)}, u32[]{:S(2)}, u32[]{:S(2)}) async-start(f32[256,1,128]{2,1,0:T(1,128)} %bitcast.17), calls=%async_computation | async-start | bytes 262144 | tf_op jit(solution)/shard_map/all_to_all | solution.py:304
  200.0 2.8 %copy.11 = f32[12,8,32,128]{3,2,1,0:T(8,128)} copy(f32[12,8,32,128]{3,1,2,0:T(8,128)} %bitcast.80) | data formatting | bytes 3145728
  202.8 10.2 %all-to-all-done = f32[256,1,128]{2,1,0:T(1,128)S(1)} async-done(((f32[256,1,128]{2,1,0:T(1,128)}), f32[256,1,128]{2,1,0:T(1,128)S(1)}, u32[]{:S(2)}, u32[]{:S(2)}) %all-to-all-start) | async-done | bytes 131104 | tf_op jit(solution)/shard_map/all_to_all | solution.py:304
  213.7 4.1 %advance.1 = (f32[96,4,8,128]{3,2,1,0:T(8,128)}, f32[96,4,8,128]{3,2,1,0:T(8,128)}) custom-call(f32[256,128]{1,0:T(8,128)} %bitcast.83, f32[96,4,8,128]{3,2,1,0:T(8,128)} %c_ref.1, f32[96,4,8,128]{3,2,1,0:T(8,128)} %d_ref.1, f32[96,4,8,128]{3,2,1,0:T(8,128)} %bitcast.73), custom_call_target="tpu_custom_call" | custom-call | flops 1572864 | bytes 7864320 | tf_op jit(solution)/shard_map/advance/pallas_call | solution.py:271
  (111 shorter events, 11.6 us)
Async XLA Ops:
  2.6 67.4 %copy-start = (f32[6,8,32,128]{3,1,2,0:T(8,128)}, f32[6,8,32,128]{3,1,2,0:T(8,128)S(1)}, u32[]{:S(2)}) copy-start(f32[6,8,32,128]{3,1,2,0:T(8,128)S(1)} %copy.17) | copy-start | bytes 2359300
  2.6 10.6 %collective-permute-start.8 = (f32[48,4096]{1,0:T(8,128)S(1)}, f32[48,4096]{1,0:T(8,128)S(1)}, u32[]{:S(2)}, u32[]{:S(2)}) collective-permute-start(f32[48,4096]{1,0:T(8,128)S(1)} %bitcast.51), channel_id=1, source_target_pairs={{0,32},{32,0},{64,96},{96,64},{128,160},{160,128},{192,224},{224,1... | collective-permute-start | bytes 2359304 | tf_op jit(solution)/shard_map/ppermute | solution.py:21
  5.9 19.1 %collective-permute-start.7 = (f32[48,4096]{1,0:T(8,128)S(1)}, f32[48,4096]{1,0:T(8,128)S(1)}, u32[]{:S(2)}, u32[]{:S(2)}) collective-permute-start(f32[48,4096]{1,0:T(8,128)S(1)} %bitcast.52), channel_id=1, source_target_pairs={{0,192},{32,224},{64,0},{96,32},{128,64},{160,96},{192,128},{224,1... | collective-permute-start | bytes 2359304 | tf_op jit(solution)/shard_map/ppermute | solution.py:16
  6.7 20.0 %collective-permute-start.4 = (f32[48,4096]{1,0:T(8,128)S(1)}, f32[48,4096]{1,0:T(8,128)}, u32[]{:S(2)}, u32[]{:S(2)}) collective-permute-start(f32[48,4096]{1,0:T(8,128)S(1)} %bitcast.53), channel_id=1, source_target_pairs={{0,64},{32,96},{64,128},{96,160},{128,192},{160,224},{192,0},{224,... | collective-permute-start | bytes 2359304 | tf_op jit(solution)/shard_map/ppermute | solution.py:16
  7.4 20.3 %collective-permute-start.1 = (f32[48,4096]{1,0:T(8,128)S(1)}, f32[48,4096]{1,0:T(8,128)S(1)}, u32[]{:S(2)}, u32[]{:S(2)}) collective-permute-start(f32[48,4096]{1,0:T(8,128)S(1)} %bitcast.54), channel_id=1, source_target_pairs={{1,0},{2,1},{3,2},{4,3},{5,4},{6,5},{7,6},{8,7},{9,8},{10,9},{11,1... | collective-permute-start | bytes 2359304 | tf_op jit(solution)/shard_map/ppermute | solution.py:292
  8.6 20.3 %collective-permute-start = (f32[48,4096]{1,0:T(8,128)S(1)}, f32[48,4096]{1,0:T(8,128)S(1)}, u32[]{:S(2)}, u32[]{:S(2)}) collective-permute-start(f32[48,4096]{1,0:T(8,128)S(1)} %bitcast.55), channel_id=1, source_target_pairs={{0,1},{1,2},{2,3},{3,4},{4,5},{5,6},{6,7},{7,8},{8,9},{9,10},{10,1... | collective-permute-start | bytes 2359304 | tf_op jit(solution)/shard_map/ppermute | solution.py:291
  13.2 56.9 %copy-start.2 = (f32[6,8,32,128]{3,1,2,0:T(8,128)}, f32[6,8,32,128]{3,1,2,0:T(8,128)S(1)}, u32[]{:S(2)}) copy-start(f32[6,8,32,128]{3,1,2,0:T(8,128)S(1)} %copy.16) | copy-start | bytes 2359300
  13.2 65.4 %copy-start.7 = (f32[48,4096]{1,0:T(8,128)}, f32[48,4096]{1,0:T(8,128)S(1)}, u32[]{:S(2)}) copy-start(f32[48,4096]{1,0:T(8,128)S(1)} %collective-permute-done.8.rest_10_.rest_8_) | copy-start | bytes 2359300
  13.2 20.0 %collective-permute-start.9 = (f32[48,4096]{1,0:T(8,128)S(1)}, f32[48,4096]{1,0:T(8,128)S(1)}, u32[]{:S(2)}, u32[]{:S(2)}) collective-permute-start(f32[48,4096]{1,0:T(8,128)S(1)} %bitcast.61), channel_id=1, source_target_pairs={{0,32},{32,0},{64,96},{96,64},{128,160},{160,128},{192,224},{224,1... | collective-permute-start | bytes 2359304 | tf_op jit(solution)/shard_map/ppermute | solution.py:21
  25.0 45.0 %copy-start.9 = (f32[48,4096]{1,0:T(8,128)}, f32[48,4096]{1,0:T(8,128)S(1)}, u32[]{:S(2)}) copy-start(f32[48,4096]{1,0:T(8,128)S(1)} %collective-permute-done.7.rest_9_.rest_7_) | copy-start | bytes 2359300
  25.0 19.6 %collective-permute-start.6 = (f32[48,4096]{1,0:T(8,128)S(1)}, f32[48,4096]{1,0:T(8,128)}, u32[]{:S(2)}, u32[]{:S(2)}) collective-permute-start(f32[48,4096]{1,0:T(8,128)S(1)} %bitcast.62), channel_id=1, source_target_pairs={{0,64},{32,96},{64,128},{96,160},{128,192},{160,224},{192,0},{224,... | collective-permute-start | bytes 2359304 | tf_op jit(solution)/shard_map/ppermute | solution.py:16
  26.7 18.0 %collective-permute-start.5 = (f32[48,4096]{1,0:T(8,128)S(1)}, f32[48,4096]{1,0:T(8,128)}, u32[]{:S(2)}, u32[]{:S(2)}) collective-permute-start(f32[48,4096]{1,0:T(8,128)S(1)} %bitcast.63), channel_id=1, source_target_pairs={{0,192},{32,224},{64,0},{96,32},{128,64},{160,96},{192,128},{224,1... | collective-permute-start | bytes 2359304 | tf_op jit(solution)/shard_map/ppermute | solution.py:16
  27.7 23.2 %copy-start.27 = (f32[48,4096]{1,0:T(8,128)}, f32[48,4096]{1,0:T(8,128)S(1)}, u32[]{:S(2)}) copy-start(f32[48,4096]{1,0:T(8,128)S(1)} %collective-permute-done.1.r_ref) | copy-start | bytes 2359300
  27.7 19.8 %collective-permute-start.3 = (f32[48,4096]{1,0:T(8,128)S(1)}, f32[48,4096]{1,0:T(8,128)S(1)}, u32[]{:S(2)}, u32[]{:S(2)}) collective-permute-start(f32[48,4096]{1,0:T(8,128)S(1)} %bitcast.64), channel_id=1, source_target_pairs={{1,0},{2,1},{3,2},{4,3},{5,4},{6,5},{7,6},{8,7},{9,8},{10,9},{11,1... | collective-permute-start | bytes 2359304 | tf_op jit(solution)/shard_map/ppermute | solution.py:292
  29.0 23.1 %copy-start.28 = (f32[48,4096]{1,0:T(8,128)}, f32[48,4096]{1,0:T(8,128)S(1)}, u32[]{:S(2)}) copy-start(f32[48,4096]{1,0:T(8,128)S(1)} %collective-permute-done.l_ref) | copy-start | bytes 2359300
  29.0 20.7 %collective-permute-start.2 = (f32[48,4096]{1,0:T(8,128)S(1)}, f32[48,4096]{1,0:T(8,128)S(1)}, u32[]{:S(2)}, u32[]{:S(2)}) collective-permute-start(f32[48,4096]{1,0:T(8,128)S(1)} %bitcast.65), channel_id=1, source_target_pairs={{0,1},{1,2},{2,3},{3,4},{4,5},{5,6},{6,7},{7,8},{8,9},{9,10},{10,1... | collective-permute-start | bytes 2359304 | tf_op jit(solution)/shard_map/ppermute | solution.py:291
  34.1 16.8 %collective-permute-start.13 = (f32[48,4096]{1,0:T(8,128)S(1)}, f32[48,4096]{1,0:T(8,128)S(1)}, u32[]{:S(2)}, u32[]{:S(2)}) collective-permute-start(f32[48,4096]{1,0:T(8,128)S(1)} %collective-permute-done.7.rest_9_.rest_7_), channel_id=1, source_target_pairs={{0,32},{32,0},{64,96},{96,64},{128,160},{160,128},{192,224},{224,1... | collective-permute-start | bytes 2359304 | tf_op jit(solution)/shard_map/ppermute | solution.py:21
  44.6 18.9 %collective-permute-start.14 = (f32[48,4096]{1,0:T(8,128)}, f32[48,4096]{1,0:T(8,128)}, u32[]{:S(2)}, u32[]{:S(2)}) collective-permute-start(f32[48,4096]{1,0:T(8,128)} %collective-permute-done.4.rest_6_.rest_4_), channel_id=1, source_target_pairs={{0,64},{32,96},{64,128},{96,160},{128,192},{160,224},{192,0},{224,... | collective-permute-start | bytes 2359304 | tf_op jit(solution)/shard_map/ppermute | solution.py:16
  44.7 21.4 %collective-permute-start.15 = (f32[48,4096]{1,0:T(8,128)}, f32[48,4096]{1,0:T(8,128)}, u32[]{:S(2)}, u32[]{:S(2)}) collective-permute-start(f32[48,4096]{1,0:T(8,128)} %collective-permute-done.5.rest_7_.rest_5_), channel_id=1, source_target_pairs={{0,192},{32,224},{64,0},{96,32},{128,64},{160,96},{192,128},{224,1... | collective-permute-start | bytes 2359304 | tf_op jit(solution)/shard_map/ppermute | solution.py:16
  47.4 16.1 %copy-start.29 = (f32[48,4096]{1,0:T(8,128)}, f32[48,4096]{1,0:T(8,128)S(1)}, u32[]{:S(2)}) copy-start(f32[48,4096]{1,0:T(8,128)S(1)} %collective-permute-done.3.r_ref) | copy-start | bytes 2359300
  47.5 31.1 %collective-permute-start.10 = (f32[48,4096]{1,0:T(8,128)}, f32[48,4096]{1,0:T(8,128)}, u32[]{:S(2)}, u32[]{:S(2)}) collective-permute-start(f32[48,4096]{1,0:T(8,128)} %collective-permute-done.4.rest_6_.rest_4_), channel_id=1, source_target_pairs={{0,32},{32,0},{64,96},{96,64},{128,160},{160,128},{192,224},{224,1... | collective-permute-start | bytes 2359304 | tf_op jit(solution)/shard_map/ppermute | solution.py:21
  49.7 16.4 %copy-start.30 = (f32[48,4096]{1,0:T(8,128)}, f32[48,4096]{1,0:T(8,128)S(1)}, u32[]{:S(2)}) copy-start(f32[48,4096]{1,0:T(8,128)S(1)} %collective-permute-done.2.l_ref) | copy-start | bytes 2359300
  49.7 28.8 %collective-permute-start.12 = (f32[48,4096]{1,0:T(8,128)}, f32[48,4096]{1,0:T(8,128)}, u32[]{:S(2)}, u32[]{:S(2)}) collective-permute-start(f32[48,4096]{1,0:T(8,128)} %collective-permute-done.6.rest_8_.rest_6_), channel_id=1, source_target_pairs={{0,32},{32,0},{64,96},{96,64},{128,160},{160,128},{192,224},{224,1... | collective-permute-start | bytes 2359304 | tf_op jit(solution)/shard_map/ppermute | solution.py:21
  51.8 26.7 %collective-permute-start.11 = (f32[48,4096]{1,0:T(8,128)}, f32[48,4096]{1,0:T(8,128)}, u32[]{:S(2)}, u32[]{:S(2)}) collective-permute-start(f32[48,4096]{1,0:T(8,128)} %collective-permute-done.5.rest_7_.rest_5_), channel_id=1, source_target_pairs={{0,32},{32,0},{64,96},{96,64},{128,160},{160,128},{192,224},{224,1... | collective-permute-start | bytes 2359304 | tf_op jit(solution)/shard_map/ppermute | solution.py:21
  63.5 26.5 %collective-permute-start.16 = (f32[48,4096]{1,0:T(8,128)}, f32[48,4096]{1,0:T(8,128)}, u32[]{:S(2)}, u32[]{:S(2)}) collective-permute-start(f32[48,4096]{1,0:T(8,128)} %collective-permute-done.14.rest_4_.rest_14_), channel_id=1, source_target_pairs={{0,32},{32,0},{64,96},{96,64},{128,160},{160,128},{192,224},{224,1... | collective-permute-start | bytes 2359304 | tf_op jit(solution)/shard_map/ppermute | solution.py:21
  66.1 23.9 %collective-permute-start.17 = (f32[48,4096]{1,0:T(8,128)}, f32[48,4096]{1,0:T(8,128)}, u32[]{:S(2)}, u32[]{:S(2)}) collective-permute-start(f32[48,4096]{1,0:T(8,128)} %collective-permute-done.15.rest_5_.rest_15_), channel_id=1, source_target_pairs={{0,32},{32,0},{64,96},{96,64},{128,160},{160,128},{192,224},{224,1... | collective-permute-start | bytes 2359304 | tf_op jit(solution)/shard_map/ppermute | solution.py:21
  74.2 4.3 %copy-start.1 = (f32[6,8,32,128]{3,1,2,0:T(8,128)S(1)}, f32[6,8,32,128]{3,1,2,0:T(8,128)}, u32[]{:S(2)}) copy-start(f32[6,8,32,128]{3,1,2,0:T(8,128)} %copy-done) | copy-start | bytes 2359300
  74.2 4.4 %copy-start.3 = (f32[6,8,32,128]{3,1,2,0:T(8,128)S(1)}, f32[6,8,32,128]{3,1,2,0:T(8,128)}, u32[]{:S(2)}) copy-start(f32[6,8,32,128]{3,1,2,0:T(8,128)} %copy-done.2) | copy-start | bytes 2359300
  74.2 4.4 %copy-start.4 = (f32[48,4096]{1,0:T(8,128)S(1)}, f32[48,4096]{1,0:T(8,128)}, u32[]{:S(2)}) copy-start(f32[48,4096]{1,0:T(8,128)} %hamiltonian.2.rest_2_.rest_0_.rest_18_) | copy-start | bytes 2359300
  78.6 1.1 copy-start.5
  79.7 1.1 copy-start.10
  80.8 1.1 copy-start.13
  94.2 21.7 %copy-start.6 = (f32[48,4096]{1,0:T(8,128)S(1)}, f32[48,4096]{1,0:T(8,128)}, u32[]{:S(2)}) copy-start(f32[48,4096]{1,0:T(8,128)} %hamiltonian.3.rest_3_.rest_1_.rest_19_) | copy-start | bytes 2359300
  94.3 9.4 %copy-start.24 = (f32[192,768]{1,0:T(8,128)}, f32[192,768]{1,0:T(8,128)S(1)}, u32[]{:S(2)}) copy-start(f32[192,768]{1,0:T(8,128)S(1)} %pad_maximum_fusion) | copy-start | bytes 1769476
  95.1 11.9 %collective-permute-start.18 = (f32[2,24,768]{2,1,0:T(8,128)}, f32[2,24,768]{2,1,0:T(8,128)S(1)}, u32[]{:S(2)}, u32[]{:S(2)}) collective-permute-start(f32[2,24,768]{2,1,0:T(8,128)} %get-tuple-element.17), channel_id=1, source_target_pairs={{0,4},{1,5},{2,6},{3,7},{4,0},{5,1},{6,2},{7,3},{8,12},{9,13},{10,... | collective-permute-start | bytes 442376 | tf_op jit(solution)/shard_map/ppermute | solution.py:31
  101.4 14.6 %collective-permute-start.20 = (f32[2,24,768]{2,1,0:T(8,128)}, f32[2,24,768]{2,1,0:T(8,128)S(1)}, u32[]{:S(2)}, u32[]{:S(2)}) collective-permute-start(f32[2,24,768]{2,1,0:T(8,128)} %get-tuple-element.18), channel_id=1, source_target_pairs={{0,6},{1,7},{2,0},{3,1},{4,2},{5,3},{6,4},{7,5},{8,14},{9,15},{10,... | collective-permute-start | bytes 442376 | tf_op jit(solution)/shard_map/ppermute | solution.py:31
  101.4 17.0 %collective-permute-start.19 = (f32[2,24,768]{2,1,0:T(8,128)}, f32[2,24,768]{2,1,0:T(8,128)}, u32[]{:S(2)}, u32[]{:S(2)}) collective-permute-start(f32[2,24,768]{2,1,0:T(8,128)} %get-tuple-element.19), channel_id=1, source_target_pairs={{0,2},{1,3},{2,4},{3,5},{4,6},{5,7},{6,0},{7,1},{8,10},{9,11},{10,... | collective-permute-start | bytes 442376 | tf_op jit(solution)/shard_map/ppermute | solution.py:31
  103.8 22.2 %collective-permute-start.33 = (f32[48,4096]{1,0:T(8,128)S(1)}, f32[48,4096]{1,0:T(8,128)}, u32[]{:S(2)}, u32[]{:S(2)}) collective-permute-start(f32[48,4096]{1,0:T(8,128)S(1)} %copy-done.4), channel_id=1, source_target_pairs={{0,32},{32,0},{64,96},{96,64},{128,160},{160,128},{192,224},{224,1... | collective-permute-start | bytes 2359304 | tf_op jit(solution)/shard_map/ppermute | solution.py:21
  104.8 21.5 %collective-permute-start.32 = (f32[48,4096]{1,0:T(8,128)S(1)}, f32[48,4096]{1,0:T(8,128)}, u32[]{:S(2)}, u32[]{:S(2)}) collective-permute-start(f32[48,4096]{1,0:T(8,128)S(1)} %copy-done.4), channel_id=1, source_target_pairs={{0,192},{32,224},{64,0},{96,32},{128,64},{160,96},{192,128},{224,1... | collective-permute-start | bytes 2359304 | tf_op jit(solution)/shard_map/ppermute | solution.py:16
  107.0 27.3 %collective-permute-start.29 = (f32[48,4096]{1,0:T(8,128)S(1)}, f32[48,4096]{1,0:T(8,128)}, u32[]{:S(2)}, u32[]{:S(2)}) collective-permute-start(f32[48,4096]{1,0:T(8,128)S(1)} %copy-done.4), channel_id=1, source_target_pairs={{0,64},{32,96},{64,128},{96,160},{128,192},{160,224},{192,0},{224,... | collective-permute-start | bytes 2359304 | tf_op jit(solution)/shard_map/ppermute | solution.py:16
  116.0 24.9 %collective-permute-start.30 = (f32[48,4096]{1,0:T(8,128)S(1)}, f32[48,4096]{1,0:T(8,128)}, u32[]{:S(2)}, u32[]{:S(2)}) collective-permute-start(f32[48,4096]{1,0:T(8,128)S(1)} %copy-done.6), channel_id=1, source_target_pairs={{0,192},{32,224},{64,0},{96,32},{128,64},{160,96},{192,128},{224,1... | collective-permute-start | bytes 2359304 | tf_op jit(solution)/shard_map/ppermute | solution.py:16
  119.4 3.7 %collective-permute-start.21 = (f32[24,768]{1,0:T(8,128)S(1)}, f32[24,768]{1,0:T(8,128)S(1)}, u32[]{:S(2)}, u32[]{:S(2)}) collective-permute-start(f32[24,768]{1,0:T(8,128)S(1)} %select_bitcast_fusion), channel_id=1, source_target_pairs={{0,1},{1,0},{2,3},{3,2},{4,5},{5,4},{6,7},{7,6},{8,9},{9,8},{10,11... | collective-permute-start | bytes 221192 | tf_op jit(solution)/shard_map/ppermute | solution.py:26
  123.1 4.2 %collective-permute-start.24 = (f32[24,768]{1,0:T(8,128)S(1)}, f32[24,768]{1,0:T(8,128)S(1)}, u32[]{:S(2)}, u32[]{:S(2)}) collective-permute-start(f32[24,768]{1,0:T(8,128)S(1)} %bitcast_add_fusion.1), channel_id=1, source_target_pairs={{0,24},{1,25},{2,26},{3,27},{4,28},{5,29},{6,30},{7,31},{8,0},{9,1... | collective-permute-start | bytes 221192 | tf_op jit(solution)/shard_map/ppermute | solution.py:36
  126.0 4.8 %collective-permute-start.23 = (f32[24,768]{1,0:T(8,128)S(1)}, f32[24,768]{1,0:T(8,128)S(1)}, u32[]{:S(2)}, u32[]{:S(2)}) collective-permute-start(f32[24,768]{1,0:T(8,128)S(1)} %bitcast_add_fusion.1), channel_id=1, source_target_pairs={{0,16},{1,17},{2,18},{3,19},{4,20},{5,21},{6,22},{7,23},{8,24},{9,... | collective-permute-start | bytes 221192 | tf_op jit(solution)/shard_map/ppermute | solution.py:36
  126.3 5.1 %collective-permute-start.22 = (f32[24,768]{1,0:T(8,128)S(1)}, f32[24,768]{1,0:T(8,128)S(1)}, u32[]{:S(2)}, u32[]{:S(2)}) collective-permute-start(f32[24,768]{1,0:T(8,128)S(1)} %bitcast_add_fusion.1), channel_id=1, source_target_pairs={{0,8},{1,9},{2,10},{3,11},{4,12},{5,13},{6,14},{7,15},{8,16},{9,17... | collective-permute-start | bytes 221192 | tf_op jit(solution)/shard_map/ppermute | solution.py:36
  127.4 17.6 %collective-permute-start.34 = (f32[48,4096]{1,0:T(8,128)S(1)}, f32[48,4096]{1,0:T(8,128)S(1)}, u32[]{:S(2)}, u32[]{:S(2)}) collective-permute-start(f32[48,4096]{1,0:T(8,128)S(1)} %copy-done.6), channel_id=1, source_target_pairs={{0,32},{32,0},{64,96},{96,64},{128,160},{160,128},{192,224},{224,1... | collective-permute-start | bytes 2359304 | tf_op jit(solution)/shard_map/ppermute | solution.py:21
  130.7 17.5 %collective-permute-start.31 = (f32[48,4096]{1,0:T(8,128)S(1)}, f32[48,4096]{1,0:T(8,128)S(1)}, u32[]{:S(2)}, u32[]{:S(2)}) collective-permute-start(f32[48,4096]{1,0:T(8,128)S(1)} %copy-done.6), channel_id=1, source_target_pairs={{0,64},{32,96},{64,128},{96,160},{128,192},{160,224},{192,0},{224,... | collective-permute-start | bytes 2359304 | tf_op jit(solution)/shard_map/ppermute | solution.py:16
  131.5 18.3 %collective-permute-start.38 = (f32[48,4096]{1,0:T(8,128)}, f32[48,4096]{1,0:T(8,128)S(1)}, u32[]{:S(2)}, u32[]{:S(2)}) collective-permute-start(f32[48,4096]{1,0:T(8,128)} %collective-permute-done.32.rest_23_), channel_id=1, source_target_pairs={{0,32},{32,0},{64,96},{96,64},{128,160},{160,128},{192,224},{224,1... | collective-permute-start | bytes 2359304 | tf_op jit(solution)/shard_map/ppermute | solution.py:21
  134.3 6.6 %collective-permute-start.25 = (f32[24,768]{1,0:T(8,128)S(1)}, f32[24,768]{1,0:T(8,128)S(1)}, u32[]{:S(2)}, u32[]{:S(2)}) collective-permute-start(f32[24,768]{1,0:T(8,128)S(1)} %add_add_fusion), channel_id=1, source_target_pairs={{0,1},{1,0},{2,3},{3,2},{4,5},{5,4},{6,7},{7,6},{8,9},{9,8},{10,11... | collective-permute-start | bytes 221192 | tf_op jit(solution)/shard_map/ppermute | solution.py:26
  140.9 24.3 %collective-permute-start.39 = (f32[48,4096]{1,0:T(8,128)}, f32[48,4096]{1,0:T(8,128)}, u32[]{:S(2)}, u32[]{:S(2)}) collective-permute-start(f32[48,4096]{1,0:T(8,128)} %collective-permute-done.29.rest_20_), channel_id=1, source_target_pairs={{0,64},{32,96},{64,128},{96,160},{128,192},{160,224},{192,0},{224,... | collective-permute-start | bytes 2359304 | tf_op jit(solution)/shard_map/ppermute | solution.py:16
  140.9 28.0 %collective-permute-start.40 = (f32[48,4096]{1,0:T(8,128)}, f32[48,4096]{1,0:T(8,128)}, u32[]{:S(2)}, u32[]{:S(2)}) collective-permute-start(f32[48,4096]{1,0:T(8,128)} %collective-permute-done.30.rest_21_), channel_id=1, source_target_pairs={{0,192},{32,224},{64,0},{96,32},{128,64},{160,96},{192,128},{224,1... | collective-permute-start | bytes 2359304 | tf_op jit(solution)/shard_map/ppermute | solution.py:16
  145.8 23.0 %collective-permute-start.28 = (f32[2,24,768]{2,1,0:T(8,128)}, f32[2,24,768]{2,1,0:T(8,128)S(1)}, u32[]{:S(2)}, u32[]{:S(2)}) collective-permute-start(f32[2,24,768]{2,1,0:T(8,128)} %maximum_select_fusion.1), channel_id=1, source_target_pairs={{0,6},{1,7},{2,0},{3,1},{4,2},{5,3},{6,4},{7,5},{8,14},{9,15},{10,... | collective-permute-start | bytes 442376 | tf_op jit(solution)/shard_map/ppermute | solution.py:31
  149.1 20.2 %collective-permute-start.27 = (f32[2,24,768]{2,1,0:T(8,128)}, f32[2,24,768]{2,1,0:T(8,128)}, u32[]{:S(2)}, u32[]{:S(2)}) collective-permute-start(f32[2,24,768]{2,1,0:T(8,128)} %maximum_select_fusion.1), channel_id=1, source_target_pairs={{0,2},{1,3},{2,4},{3,5},{4,6},{5,7},{6,0},{7,1},{8,10},{9,11},{10,... | collective-permute-start | bytes 442376 | tf_op jit(solution)/shard_map/ppermute | solution.py:31
  150.6 18.8 %collective-permute-start.26 = (f32[2,24,768]{2,1,0:T(8,128)}, f32[2,24,768]{2,1,0:T(8,128)}, u32[]{:S(2)}, u32[]{:S(2)}) collective-permute-start(f32[2,24,768]{2,1,0:T(8,128)} %maximum_select_fusion.1), channel_id=1, source_target_pairs={{0,4},{1,5},{2,6},{3,7},{4,0},{5,1},{6,2},{7,3},{8,12},{9,13},{10,... | collective-permute-start | bytes 442376 | tf_op jit(solution)/shard_map/ppermute | solution.py:31
  153.9 22.5 %copy-start.8 = (f32[48,4096]{1,0:T(8,128)S(1)}, f32[48,4096]{1,0:T(8,128)}, u32[]{:S(2)}) copy-start(f32[48,4096]{1,0:T(8,128)} %copy-done.7) | copy-start | bytes 2359300
  153.9 22.5 %copy-start.11 = (f32[48,4096]{1,0:T(8,128)S(1)}, f32[48,4096]{1,0:T(8,128)}, u32[]{:S(2)}) copy-start(f32[48,4096]{1,0:T(8,128)} %copy-done.9) | copy-start | bytes 2359300
  165.2 6.8 %collective-permute-start.35 = (f32[48,4096]{1,0:T(8,128)}, f32[48,4096]{1,0:T(8,128)S(1)}, u32[]{:S(2)}, u32[]{:S(2)}) collective-permute-start(f32[48,4096]{1,0:T(8,128)} %collective-permute-done.29.rest_20_), channel_id=1, source_target_pairs={{0,32},{32,0},{64,96},{96,64},{128,160},{160,128},{192,224},{224,1... | collective-permute-start | bytes 2359304 | tf_op jit(solution)/shard_map/ppermute | solution.py:21
  168.9 4.4 %collective-permute-start.36 = (f32[48,4096]{1,0:T(8,128)}, f32[48,4096]{1,0:T(8,128)S(1)}, u32[]{:S(2)}, u32[]{:S(2)}) collective-permute-start(f32[48,4096]{1,0:T(8,128)} %collective-permute-done.30.rest_21_), channel_id=1, source_target_pairs={{0,32},{32,0},{64,96},{96,64},{128,160},{160,128},{192,224},{224,1... | collective-permute-start | bytes 2359304 | tf_op jit(solution)/shard_map/ppermute | solution.py:21
  168.9 4.4 %collective-permute-start.37 = (f32[48,4096]{1,0:T(8,128)}, f32[48,4096]{1,0:T(8,128)S(1)}, u32[]{:S(2)}, u32[]{:S(2)}) collective-permute-start(f32[48,4096]{1,0:T(8,128)} %copy-done.20), channel_id=1, source_target_pairs={{0,32},{32,0},{64,96},{96,64},{128,160},{160,128},{192,224},{224,1... | collective-permute-start | bytes 2359304 | tf_op jit(solution)/shard_map/ppermute | solution.py:21
  169.4 5.0 %collective-permute-start.41 = (f32[48,4096]{1,0:T(8,128)}, f32[48,4096]{1,0:T(8,128)S(1)}, u32[]{:S(2)}, u32[]{:S(2)}) collective-permute-start(f32[48,4096]{1,0:T(8,128)} %collective-permute-done.39.rest_30_), channel_id=1, source_target_pairs={{0,32},{32,0},{64,96},{96,64},{128,160},{160,128},{192,224},{224,1... | collective-permute-start | bytes 2359304 | tf_op jit(solution)/shard_map/ppermute | solution.py:21
  169.5 6.0 %collective-permute-start.42 = (f32[48,4096]{1,0:T(8,128)}, f32[48,4096]{1,0:T(8,128)S(1)}, u32[]{:S(2)}, u32[]{:S(2)}) collective-permute-start(f32[48,4096]{1,0:T(8,128)} %collective-permute-done.40.rest_31_), channel_id=1, source_target_pairs={{0,32},{32,0},{64,96},{96,64},{128,160},{160,128},{192,224},{224,1... | collective-permute-start | bytes 2359304 | tf_op jit(solution)/shard_map/ppermute | solution.py:21
  176.4 1.1 copy-start.14
  177.5 1.1 copy-start.17
  192.8 20.3 %all-to-all-start = ((f32[256,1,128]{2,1,0:T(1,128)}), f32[256,1,128]{2,1,0:T(1,128)S(1)}, u32[]{:S(2)}, u32[]{:S(2)}) async-start(f32[256,1,128]{2,1,0:T(1,128)} %bitcast.17), calls=%async_computation | async-start | bytes 262144 | tf_op jit(solution)/shard_map/all_to_all | solution.py:304
  (12 other events, 11.7 us)

commit v2 on v1

--- a/solution.py
+++ b/solution.py
@@ -7,7 +7,7 @@
 
 coeffs = (-205.0 / 72.0, 8.0 / 5.0, -1.0 / 5.0, 8.0 / 315.0, -1.0 / 560.0)
 step_length = 0.05
-VMEM_LIMIT = 32 * 1024 * 1024
+VMEM_LIMIT = 56 * 1024 * 1024
 ZS = 8
 
 
@@ -159,30 +159,33 @@
 
 def sum_over_slabs(part):
     rows, columns = part.shape
+    slabs = lax.axis_size("dom")
+    count = slabs // ZS
+    dom = lax.axis_index("dom")
+    slot = dom // ZS
+    even = lax.rem(dom, 2) == 0
+    pieces = part.reshape(count, 2, rows // (2 * count), columns)
     quad = ZS // 2
-    z = lax.rem(lax.axis_index("dom"), ZS)
-    even = lax.rem(z, 2) == 0
-    slot = z // 2
-    pieces = part.reshape(quad, 2, rows // ZS, columns)
-    order = sorted(range(1, quad), key=lambda k: -min(k, quad - k))
 
     def piece(k):
-        return lax.dynamic_index_in_dim(pieces, lax.rem(slot + k, quad), 0, keepdims=False)
+        return lax.dynamic_index_in_dim(pieces, lax.rem(slot + k, count), 0, keepdims=False)
 
     total = piece(0)
-    for got in [shift_z(piece(k), 2 * k) for k in order]:
+    order = sorted(range(1, count), key=lambda k: -min(k, count - k))
+    for got in [shift_y(piece(k), k) for k in order]:
         total = total + got
     other = flip_z(jnp.where(even, total[1], total[0]))
     total = jnp.where(even, total[0], total[1]) + other
-    count = lax.axis_size("dom") // ZS
-    for got in [shift_y(total, k) for k in range(1, count)]:
+    for got in [shift_z(total, 2 * k) for k in sorted(range(1, quad), key=lambda k: -min(k, quad - k))]:
         total = total + got
     other = flip_z(total)
     total = jnp.where(even, jnp.stack([total, other]), jnp.stack([other, total]))
     out = jnp.zeros_like(pieces)
     out = lax.dynamic_update_slice_in_dim(out, total[None], slot, 0)
     for k in order:
-        out = lax.dynamic_update_slice_in_dim(out, shift_z(total, 2 * k)[None], lax.rem(slot - k + quad, quad), 0)
+        out = lax.dynamic_update_slice_in_dim(
+            out, shift_y(total, k)[None], lax.rem(slot - k + count, count), 0
+        )
     return out.reshape(rows, columns)
 
 

time: 219 us -> 212 us (0.968)
  local copies, waits for them, and re-layouts: 27.8 us -> 14 us
  Pallas kernels: 34.3 us -> 39.5 us
  starting transfers between devices: 72.6 us -> 75.6 us
    unnamed x68 -> x52, local copies, waits for them, and re-layouts: 23.6 us -> 9.88 us
    ppermute x6 -> x3, waiting for transfers between devices: 8.96 us -> 0.23 us  [shift_z(): lax.ppermute(v, 'dom', [(i, i // ZS * ZS + (i + k) % ZS) for i in range(n)])]
    ppermute x12, waiting for transfers between devices: 51.6 us -> 60 us  [shift_orb(): return lax.ppermute(v, 'orb', [(i, (i + k) % n) for i in range(n)])]
    ppermute x3 -> x6, starting transfers between devices: 3.85 us -> 8.9 us  [shift_y(): return lax.ppermute(v, 'dom', [(i, (i + k * ZS) % n) for i in range(n)])]
    ppermute x16, starting transfers between devices: 24 us -> 19.9 us  [swap_core(): return lax.ppermute(v, 'orb', [(i, i ^ 1) for i in range(n)])]
    ppermute x2, starting transfers between devices: 0.19 us -> 3.26 us  [flip_z(): return lax.ppermute(v, 'dom', [(i, i ^ 1) for i in range(n)])]
    pallas_call x2, Pallas kernels: 11.1 us -> 13.7 us  [gram(): pl.pallas_call(kernel, out_shape=jax.ShapeDtypeStruct((rows, total), jnp....]
    pallas_call x1, Pallas kernels: 10.7 us -> 13.2 us  [gradient_of(): pl.pallas_call(kernel, out_shape=(jax.ShapeDtypeStruct((own, cells), jnp....]
  transfers between devices with their start and end apart: 44 -> 44, of which waited for: 18 -> 17; matrix products, arithmetic and copies ran while one was open for 5% -> 5% of each run, Pallas kernels for 7% -> 8%
where the time goes in v2:
time: 212 us; the launch traced here: 211 us
  waiting for transfers between devices  79.1 us (37%)
  starting transfers between devices  75.6 us (36%)
  Pallas kernels  39.5 us (19%)
  local copies, waits for them, and re-layouts  14 us (7%)
    ppermute x12, waiting for transfers between devices, shift_orb(): return lax.ppermute(v, 'orb', [(i, (i + k) % n) for i in range(n)])  60 us
    ppermute x16, starting transfers between devices, swap_core(): return lax.ppermute(v, 'orb', [(i, i ^ 1) for i in range(n)])  19.9 us
    pallas_call x2, Pallas kernels, gram(): pl.pallas_call(kernel, out_shape=jax.ShapeDtypeStruct((rows, total), jnp....  13.7 us
    pallas_call x1, Pallas kernels, gradient_of(): pl.pallas_call(kernel, out_shape=(jax.ShapeDtypeStruct((own, cells), jnp....  13.2 us
    ppermute x12, starting transfers between devices, shift_orb(): return lax.ppermute(v, 'orb', [(i, (i + k) % n) for i in range(n)])  12.9 us
    ppermute x3, starting transfers between devices, shift_z(): lax.ppermute(v, 'dom', [(i, i // ZS * ZS + (i + k) % ZS) for i in range(n)])  12.8 us
    all_to_all x1, waiting for transfers between devices, on_device(): lax.all_to_all(sums, ('orb', 'dom'), split_axis=0, concat_axis=0, tiled=T...  10.2 us
    unnamed x52, local copies, waits for them, and re-layouts  9.88 us
  transfers between devices with their start and end apart: 44, of which 17 were waited for; matrix products, arithmetic and copies ran while one was open for 5% of the time, Pallas kernels for 8%

profile of v2, /device:TPU:1, one launch (start us, length us, event | category | flops | bytes accessed | tf_op | source)
XLA Modules:
  0.0 211.2 jit_solution(6219083160975061896)
XLA Ops:
  0.6 1.5 fusion.3
  2.1 0.5 copy.17
  2.6 3.3 %collective-permute-start.8 = (f32[48,4096]{1,0:T(8,128)S(1)}, f32[48,4096]{1,0:T(8,128)S(1)}, u32[]{:S(2)}, u32[]{:S(2)}) collective-permute-start(f32[48,4096]{1,0:T(8,128)S(1)} %bitcast.51), channel_id=1, source_target_pairs={{0,32},{32,0},{64,96},{96,64},{128,160},{160,128},{192,224},{224,1... | collective-permute-start | bytes 2359304 | tf_op jit(solution)/shard_map/ppermute | solution.py:21
  5.9 0.8 collective-permute-start.7
  6.7 0.7 collective-permute-start.4
  7.4 1.3 collective-permute-start.1
  8.6 4.0 %collective-permute-start = (f32[48,4096]{1,0:T(8,128)S(1)}, f32[48,4096]{1,0:T(8,128)S(1)}, u32[]{:S(2)}, u32[]{:S(2)}) collective-permute-start(f32[48,4096]{1,0:T(8,128)S(1)} %bitcast.55), channel_id=1, source_target_pairs={{0,1},{1,2},{2,3},{3,4},{4,5},{5,6},{6,7},{7,8},{8,9},{9,10},{10,1... | collective-permute-start | bytes 2359304 | tf_op jit(solution)/shard_map/ppermute | solution.py:294
  12.7 0.5 copy.16
  13.2 1.3 collective-permute-start.9
  14.5 10.5 %collective-permute-done.7.rest_9_.rest_7_ = f32[48,4096]{1,0:T(8,128)S(1)} collective-permute-done((f32[48,4096]{1,0:T(8,128)S(1)}, f32[48,4096]{1,0:T(8,128)S(1)}, u32[]{:S(2)}, u32[]{:S(2)}) %collective-permute-start.7) | collective-permute-done | bytes 786464 | tf_op jit(solution)/shard_map/ppermute | solution.py:16
  25.0 1.7 collective-permute-done.4.rest_6_.rest_4_
  26.7 1.0 collective-permute-start.5
  27.7 1.3 collective-permute-start.3
  29.0 4.2 %collective-permute-start.2 = (f32[48,4096]{1,0:T(8,128)S(1)}, f32[48,4096]{1,0:T(8,128)S(1)}, u32[]{:S(2)}, u32[]{:S(2)}) collective-permute-start(f32[48,4096]{1,0:T(8,128)S(1)} %bitcast.65), channel_id=1, source_target_pairs={{0,1},{1,2},{2,3},{3,4},{4,5},{5,6},{6,7},{7,8},{8,9},{9,10},{10,1... | collective-permute-start | bytes 2359304 | tf_op jit(solution)/shard_map/ppermute | solution.py:294
  33.2 2.0 collective-permute-start.13
  35.2 9.4 %collective-permute-done.6.rest_8_.rest_6_ = f32[48,4096]{1,0:T(8,128)} collective-permute-done((f32[48,4096]{1,0:T(8,128)S(1)}, f32[48,4096]{1,0:T(8,128)}, u32[]{:S(2)}, u32[]{:S(2)}) %collective-permute-start.6) | collective-permute-done | bytes 786464 | tf_op jit(solution)/shard_map/ppermute | solution.py:16
  44.7 2.6 %collective-permute-start.15 = (f32[48,4096]{1,0:T(8,128)}, f32[48,4096]{1,0:T(8,128)}, u32[]{:S(2)}, u32[]{:S(2)}) collective-permute-start(f32[48,4096]{1,0:T(8,128)} %collective-permute-done.5.rest_7_.rest_5_), channel_id=1, source_target_pairs={{0,192},{32,224},{64,0},{96,32},{128,64},{160,96},{192,128},{224,1... | collective-permute-start | bytes 2359304 | tf_op jit(solution)/shard_map/ppermute | solution.py:16
  47.5 2.2 %collective-permute-start.10 = (f32[48,4096]{1,0:T(8,128)}, f32[48,4096]{1,0:T(8,128)}, u32[]{:S(2)}, u32[]{:S(2)}) collective-permute-start(f32[48,4096]{1,0:T(8,128)} %collective-permute-done.4.rest_6_.rest_4_), channel_id=1, source_target_pairs={{0,32},{32,0},{64,96},{96,64},{128,160},{160,128},{192,224},{224,1... | collective-permute-start | bytes 2359304 | tf_op jit(solution)/shard_map/ppermute | solution.py:21
  49.7 1.2 collective-permute-start.12
  51.0 0.8 copy-done.7
  51.8 11.7 %collective-permute-done.14.rest_4_.rest_14_ = f32[48,4096]{1,0:T(8,128)} collective-permute-done((f32[48,4096]{1,0:T(8,128)}, f32[48,4096]{1,0:T(8,128)}, u32[]{:S(2)}, u32[]{:S(2)}) %collective-permute-start.14) | collective-permute-done | bytes 786464 | tf_op jit(solution)/shard_map/ppermute | solution.py:16
  63.5 2.6 %collective-permute-start.16 = (f32[48,4096]{1,0:T(8,128)}, f32[48,4096]{1,0:T(8,128)}, u32[]{:S(2)}, u32[]{:S(2)}) collective-permute-start(f32[48,4096]{1,0:T(8,128)} %collective-permute-done.14.rest_4_.rest_14_), channel_id=1, source_target_pairs={{0,32},{32,0},{64,96},{96,64},{128,160},{160,128},{192,224},{224,1... | collective-permute-start | bytes 2359304 | tf_op jit(solution)/shard_map/ppermute | solution.py:21
  66.4 3.6 %copy.15 = f32[12,8,32,128]{3,1,2,0:T(8,128)} copy(f32[12,8,32,128]{3,2,1,0:T(8,128)} %bitcast.79) | data formatting | bytes 3145728
  70.1 4.3 %hamiltonian.2.rest_2_.rest_0_.rest_18_ = f32[48,4096]{1,0:T(8,128)} custom-call(f32[48,4096]{1,0:T(8,128)} %bitcast.56, f32[48,4096]{1,0:T(8,128)} %copy-done.20, f32[48,4096]{1,0:T(8,128)} %copy-done.19, f32[1,4096]{1,0:T(1,128)} %bitcast.87), custom_call_target="tpu_custom_call" | custom-call | flops 7864320 | bytes 3145728 | tf_op jit(solution)/shard_map/hamiltonian/pallas_call | solution.py:90
  74.4 4.2 %hamiltonian.3.rest_3_.rest_1_.rest_19_ = f32[48,4096]{1,0:T(8,128)} custom-call(f32[48,4096]{1,0:T(8,128)} %bitcast.66, f32[48,4096]{1,0:T(8,128)} %copy-done.22, f32[48,4096]{1,0:T(8,128)} %copy-done.21, f32[1,4096]{1,0:T(1,128)} %bitcast.88), custom_call_target="tpu_custom_call" | custom-call | flops 7864320 | bytes 3145728 | tf_op jit(solution)/shard_map/hamiltonian/pallas_call | solution.py:90
  78.7 8.5 %gram.2 = f32[192,576]{1,0:T(8,128)} custom-call(f32[48,4096]{1,0:T(8,128)} %bitcast.57, f32[48,4096]{1,0:T(8,128)} %bitcast.67, f32[48,4096]{1,0:T(8,128)} %hamiltonian.2.rest_2_.rest_0_.rest_18_, f32[48,4096]{1,0:T(8,128)} %hamiltonian.3.rest_3_.rest_1_.rest_19_, f32[48,4096]{1,0:T(8,128)} %bitcast.58, f32[48,4096]{1,0:T(8,128)} %bitcast.68, ...), custom_call_target="tpu_custom_call" | custom-call | flops 2717908992 | bytes 12582912 | tf_op jit(solution)/shard_map/gram/pallas_call | solution.py:141
  87.2 5.3 %gram.3 = f32[192,192]{1,0:T(8,128)} custom-call(f32[48,4096]{1,0:T(8,128)} %bitcast.59, f32[48,4096]{1,0:T(8,128)} %bitcast.69, f32[48,4096]{1,0:T(8,128)} %hamiltonian.2.rest_2_.rest_0_.rest_18_, f32[48,4096]{1,0:T(8,128)} %hamiltonian.3.rest_3_.rest_1_.rest_19_, f32[48,4096]{1,0:T(8,128)} %collective-permute-done.14.rest_4_.rest_14_, ...), custom_call_target="tpu_custom_call" | custom-call | flops 905969664 | bytes 6291456 | tf_op jit(solution)/shard_map/gram/pallas_call | solution.py:141
  92.5 1.2 pad_maximum_fusion
  93.6 0.7 dynamic-slice_bitcast_fusion.2
  94.4 2.3 %collective-permute-start.18 = (f32[2,24,768]{2,1,0:T(8,128)}, f32[2,24,768]{2,1,0:T(8,128)S(1)}, u32[]{:S(2)}, u32[]{:S(2)}) collective-permute-start(f32[2,24,768]{2,1,0:T(8,128)} %get-tuple-element.17), channel_id=1, source_target_pairs={{0,16},{1,17},{2,18},{3,19},{4,20},{5,21},{6,22},{7,23},{8,24},{9,... | collective-permute-start | bytes 442376 | tf_op jit(solution)/shard_map/ppermute | solution.py:36
  96.7 0.8 collective-permute-start.20
  97.4 0.7 collective-permute-start.19
  98.1 1.3 collective-permute-start.33
  99.4 1.9 collective-permute-start.32
  101.4 2.7 %collective-permute-done.20 = f32[2,24,768]{2,1,0:T(8,128)S(1)} collective-permute-done((f32[2,24,768]{2,1,0:T(8,128)}, f32[2,24,768]{2,1,0:T(8,128)S(1)}, u32[]{:S(2)}, u32[]{:S(2)}) %collective-permute-start.20) | collective-permute-done | bytes 147488 | tf_op jit(solution)/shard_map/ppermute | solution.py:36
  104.0 2.7 %collective-permute-start.30 = (f32[48,4096]{1,0:T(8,128)S(1)}, f32[48,4096]{1,0:T(8,128)}, u32[]{:S(2)}, u32[]{:S(2)}) collective-permute-start(f32[48,4096]{1,0:T(8,128)S(1)} %copy-done.3), channel_id=1, source_target_pairs={{0,192},{32,224},{64,0},{96,32},{128,64},{160,96},{192,128},{224,1... | collective-permute-start | bytes 2359304 | tf_op jit(solution)/shard_map/ppermute | solution.py:16
  106.8 1.7 collective-permute-start.21
  108.6 2.1 %collective-permute-done.21 = f32[24,768]{1,0:T(8,128)S(1)} collective-permute-done((f32[24,768]{1,0:T(8,128)S(1)}, f32[24,768]{1,0:T(8,128)S(1)}, u32[]{:S(2)}, u32[]{:S(2)}) %collective-permute-start.21) | collective-permute-done | bytes 73760 | tf_op jit(solution)/shard_map/ppermute | solution.py:26
  110.7 5.9 %collective-permute-start.24 = (f32[24,768]{1,0:T(8,128)S(1)}, f32[24,768]{1,0:T(8,128)S(1)}, u32[]{:S(2)}, u32[]{:S(2)}) collective-permute-start(f32[24,768]{1,0:T(8,128)S(1)} %bitcast_add_fusion.1), channel_id=1, source_target_pairs={{0,6},{1,7},{2,0},{3,1},{4,2},{5,3},{6,4},{7,5},{8,14},{9,15},{10,... | collective-permute-start | bytes 221192 | tf_op jit(solution)/shard_map/ppermute | solution.py:31
  116.7 1.9 collective-permute-done.32.rest_23_
  118.6 6.9 %collective-permute-start.22 = (f32[24,768]{1,0:T(8,128)S(1)}, f32[24,768]{1,0:T(8,128)S(1)}, u32[]{:S(2)}, u32[]{:S(2)}) collective-permute-start(f32[24,768]{1,0:T(8,128)S(1)} %bitcast_add_fusion.1), channel_id=1, source_target_pairs={{0,4},{1,5},{2,6},{3,7},{4,0},{5,1},{6,2},{7,3},{8,12},{9,13},{10,... | collective-permute-start | bytes 221192 | tf_op jit(solution)/shard_map/ppermute | solution.py:31
  125.5 1.6 collective-permute-start.34
  127.4 2.2 %collective-permute-start.38 = (f32[48,4096]{1,0:T(8,128)}, f32[48,4096]{1,0:T(8,128)}, u32[]{:S(2)}, u32[]{:S(2)}) collective-permute-start(f32[48,4096]{1,0:T(8,128)} %collective-permute-done.32.rest_23_), channel_id=1, source_target_pairs={{0,32},{32,0},{64,96},{96,64},{128,160},{160,128},{192,224},{224,1... | collective-permute-start | bytes 2359304 | tf_op jit(solution)/shard_map/ppermute | solution.py:21
  129.6 1.5 collective-permute-start.25
  131.1 4.4 %collective-permute-done.30.rest_21_ = f32[48,4096]{1,0:T(8,128)} collective-permute-done((f32[48,4096]{1,0:T(8,128)S(1)}, f32[48,4096]{1,0:T(8,128)}, u32[]{:S(2)}, u32[]{:S(2)}) %collective-permute-start.30) | collective-permute-done | bytes 786464 | tf_op jit(solution)/shard_map/ppermute | solution.py:16
  135.5 3.2 %collective-permute-start.40 = (f32[48,4096]{1,0:T(8,128)}, f32[48,4096]{1,0:T(8,128)}, u32[]{:S(2)}, u32[]{:S(2)}) collective-permute-start(f32[48,4096]{1,0:T(8,128)} %collective-permute-done.30.rest_21_), channel_id=1, source_target_pairs={{0,192},{32,224},{64,0},{96,32},{128,64},{160,96},{192,128},{224,1... | collective-permute-start | bytes 2359304 | tf_op jit(solution)/shard_map/ppermute | solution.py:16
  138.6 0.7 maximum_select_fusion.1
  139.3 2.0 collective-permute-start.28
  141.3 6.6 %collective-permute-done.31.rest_22_ = f32[48,4096]{1,0:T(8,128)S(1)} collective-permute-done((f32[48,4096]{1,0:T(8,128)S(1)}, f32[48,4096]{1,0:T(8,128)S(1)}, u32[]{:S(2)}, u32[]{:S(2)}) %collective-permute-start.31) | collective-permute-done | bytes 786464 | tf_op jit(solution)/shard_map/ppermute | solution.py:16
  148.3 2.8 %collective-permute-start.26 = (f32[2,24,768]{2,1,0:T(8,128)}, f32[2,24,768]{2,1,0:T(8,128)}, u32[]{:S(2)}, u32[]{:S(2)}) collective-permute-start(f32[2,24,768]{2,1,0:T(8,128)} %maximum_select_fusion.1), channel_id=1, source_target_pairs={{0,16},{1,17},{2,18},{3,19},{4,20},{5,21},{6,22},{7,23},{8,24},{9,... | collective-permute-start | bytes 442376 | tf_op jit(solution)/shard_map/ppermute | solution.py:36
  151.1 13.7 %collective-permute-done.39.rest_30_ = f32[48,4096]{1,0:T(8,128)S(1)} collective-permute-done((f32[48,4096]{1,0:T(8,128)}, f32[48,4096]{1,0:T(8,128)S(1)}, u32[]{:S(2)}, u32[]{:S(2)}) %collective-permute-start.39) | collective-permute-done | bytes 786464 | tf_op jit(solution)/shard_map/ppermute | solution.py:16
  164.8 0.9 collective-permute-start.35
  166.7 0.9 bitcast_dynamic-update-slice_fusion.2
  167.7 0.9 bitcast_dynamic-update-slice_fusion.1
  168.7 1.3 collective-permute-done.37.rest_28_
  170.0 1.1 collective-permute-done.41.rest_32_
  171.1 1.1 collective-permute-done.42.rest_33_
  172.3 0.9 copy-done.18
  173.2 13.2 %gradient.1 = (f32[96,4096]{1,0:T(8,128)}, f32[256,128]{1,0:T(8,128)}) custom-call(f32[192,768]{1,0:T(8,128)} %bitcast.78, f32[96,4096]{1,0:T(8,128)} %bitcast.71, f32[48,4096]{1,0:T(8,128)} %hamiltonian.2.rest_2_.rest_0_.rest_18_, f32[48,4096]{1,0:T(8,128)} %hamiltonian.3.rest_3_.rest_1_.rest_19_, f32[48,4096]{1,0:T(8,128)} %bitcast.60, ...), custom_call_target="tpu_custom_call" | custom-call | flops 3623878656 | bytes 25165824 | tf_op jit(solution)/shard_map/gradient/pallas_call | solution.py:238
  186.4 7.1 %all-to-all-start = ((f32[256,1,128]{2,1,0:T(1,128)}), f32[256,1,128]{2,1,0:T(1,128)S(1)}, u32[]{:S(2)}, u32[]{:S(2)}) async-start(f32[256,1,128]{2,1,0:T(1,128)} %bitcast.86), calls=%async_computation | async-start | bytes 262144 | tf_op jit(solution)/shard_map/all_to_all | solution.py:307
  193.5 2.8 %copy.11 = f32[12,8,32,128]{3,2,1,0:T(8,128)} copy(f32[12,8,32,128]{3,1,2,0:T(8,128)} %bitcast.80) | data formatting | bytes 3145728
  196.3 10.2 %all-to-all-done = f32[256,1,128]{2,1,0:T(1,128)S(1)} async-done(((f32[256,1,128]{2,1,0:T(1,128)}), f32[256,1,128]{2,1,0:T(1,128)S(1)}, u32[]{:S(2)}, u32[]{:S(2)}) %all-to-all-start) | async-done | bytes 131104 | tf_op jit(solution)/shard_map/all_to_all | solution.py:307
  206.5 0.7 copy-done.23
  207.2 4.1 %advance.1 = (f32[96,4,8,128]{3,2,1,0:T(8,128)}, f32[96,4,8,128]{3,2,1,0:T(8,128)}) custom-call(f32[256,128]{1,0:T(8,128)} %bitcast.83, f32[96,4,8,128]{3,2,1,0:T(8,128)} %c_ref.1, f32[96,4,8,128]{3,2,1,0:T(8,128)} %d_ref.1, f32[96,4,8,128]{3,2,1,0:T(8,128)} %bitcast.72), custom_call_target="tpu_custom_call" | custom-call | flops 1572864 | bytes 7864320 | tf_op jit(solution)/shard_map/advance/pallas_call | solution.py:274
  (95 shorter events, 2.7 us)
Async XLA Ops:
  2.6 67.5 %copy-start = (f32[6,8,32,128]{3,1,2,0:T(8,128)}, f32[6,8,32,128]{3,1,2,0:T(8,128)S(1)}, u32[]{:S(2)}) copy-start(f32[6,8,32,128]{3,1,2,0:T(8,128)S(1)} %copy.17) | copy-start | bytes 2359300
  2.6 10.6 %collective-permute-start.8 = (f32[48,4096]{1,0:T(8,128)S(1)}, f32[48,4096]{1,0:T(8,128)S(1)}, u32[]{:S(2)}, u32[]{:S(2)}) collective-permute-start(f32[48,4096]{1,0:T(8,128)S(1)} %bitcast.51), channel_id=1, source_target_pairs={{0,32},{32,0},{64,96},{96,64},{128,160},{160,128},{192,224},{224,1... | collective-permute-start | bytes 2359304 | tf_op jit(solution)/shard_map/ppermute | solution.py:21
  5.9 19.1 %collective-permute-start.7 = (f32[48,4096]{1,0:T(8,128)S(1)}, f32[48,4096]{1,0:T(8,128)S(1)}, u32[]{:S(2)}, u32[]{:S(2)}) collective-permute-start(f32[48,4096]{1,0:T(8,128)S(1)} %bitcast.52), channel_id=1, source_target_pairs={{0,192},{32,224},{64,0},{96,32},{128,64},{160,96},{192,128},{224,1... | collective-permute-start | bytes 2359304 | tf_op jit(solution)/shard_map/ppermute | solution.py:16
  6.7 20.0 %collective-permute-start.4 = (f32[48,4096]{1,0:T(8,128)S(1)}, f32[48,4096]{1,0:T(8,128)}, u32[]{:S(2)}, u32[]{:S(2)}) collective-permute-start(f32[48,4096]{1,0:T(8,128)S(1)} %bitcast.53), channel_id=1, source_target_pairs={{0,64},{32,96},{64,128},{96,160},{128,192},{160,224},{192,0},{224,... | collective-permute-start | bytes 2359304 | tf_op jit(solution)/shard_map/ppermute | solution.py:16
  7.4 20.3 %collective-permute-start.1 = (f32[48,4096]{1,0:T(8,128)S(1)}, f32[48,4096]{1,0:T(8,128)S(1)}, u32[]{:S(2)}, u32[]{:S(2)}) collective-permute-start(f32[48,4096]{1,0:T(8,128)S(1)} %bitcast.54), channel_id=1, source_target_pairs={{1,0},{2,1},{3,2},{4,3},{5,4},{6,5},{7,6},{8,7},{9,8},{10,9},{11,1... | collective-permute-start | bytes 2359304 | tf_op jit(solution)/shard_map/ppermute | solution.py:295
  8.6 20.3 %collective-permute-start = (f32[48,4096]{1,0:T(8,128)S(1)}, f32[48,4096]{1,0:T(8,128)S(1)}, u32[]{:S(2)}, u32[]{:S(2)}) collective-permute-start(f32[48,4096]{1,0:T(8,128)S(1)} %bitcast.55), channel_id=1, source_target_pairs={{0,1},{1,2},{2,3},{3,4},{4,5},{5,6},{6,7},{7,8},{8,9},{9,10},{10,1... | collective-permute-start | bytes 2359304 | tf_op jit(solution)/shard_map/ppermute | solution.py:294
  13.2 56.9 %copy-start.1 = (f32[6,8,32,128]{3,1,2,0:T(8,128)}, f32[6,8,32,128]{3,1,2,0:T(8,128)S(1)}, u32[]{:S(2)}) copy-start(f32[6,8,32,128]{3,1,2,0:T(8,128)S(1)} %copy.16) | copy-start | bytes 2359300
  13.2 56.9 %copy-start.4 = (f32[48,4096]{1,0:T(8,128)}, f32[48,4096]{1,0:T(8,128)S(1)}, u32[]{:S(2)}) copy-start(f32[48,4096]{1,0:T(8,128)S(1)} %collective-permute-done.8.rest_10_.rest_8_) | copy-start | bytes 2359300
  13.2 20.0 %collective-permute-start.9 = (f32[48,4096]{1,0:T(8,128)S(1)}, f32[48,4096]{1,0:T(8,128)S(1)}, u32[]{:S(2)}, u32[]{:S(2)}) collective-permute-start(f32[48,4096]{1,0:T(8,128)S(1)} %bitcast.61), channel_id=1, source_target_pairs={{0,32},{32,0},{64,96},{96,64},{128,160},{160,128},{192,224},{224,1... | collective-permute-start | bytes 2359304 | tf_op jit(solution)/shard_map/ppermute | solution.py:21
  25.0 45.1 %copy-start.5 = (f32[48,4096]{1,0:T(8,128)}, f32[48,4096]{1,0:T(8,128)S(1)}, u32[]{:S(2)}) copy-start(f32[48,4096]{1,0:T(8,128)S(1)} %collective-permute-done.7.rest_9_.rest_7_) | copy-start | bytes 2359300
  25.0 19.6 %collective-permute-start.6 = (f32[48,4096]{1,0:T(8,128)S(1)}, f32[48,4096]{1,0:T(8,128)}, u32[]{:S(2)}, u32[]{:S(2)}) collective-permute-start(f32[48,4096]{1,0:T(8,128)S(1)} %bitcast.62), channel_id=1, source_target_pairs={{0,64},{32,96},{64,128},{96,160},{128,192},{160,224},{192,0},{224,... | collective-permute-start | bytes 2359304 | tf_op jit(solution)/shard_map/ppermute | solution.py:16
  26.7 18.0 %collective-permute-start.5 = (f32[48,4096]{1,0:T(8,128)S(1)}, f32[48,4096]{1,0:T(8,128)}, u32[]{:S(2)}, u32[]{:S(2)}) collective-permute-start(f32[48,4096]{1,0:T(8,128)S(1)} %bitcast.63), channel_id=1, source_target_pairs={{0,192},{32,224},{64,0},{96,32},{128,64},{160,96},{192,128},{224,1... | collective-permute-start | bytes 2359304 | tf_op jit(solution)/shard_map/ppermute | solution.py:16
  27.7 35.8 %copy-start.19 = (f32[48,4096]{1,0:T(8,128)}, f32[48,4096]{1,0:T(8,128)S(1)}, u32[]{:S(2)}) copy-start(f32[48,4096]{1,0:T(8,128)S(1)} %collective-permute-done.1.r_ref) | copy-start | bytes 2359300
  27.7 19.8 %collective-permute-start.3 = (f32[48,4096]{1,0:T(8,128)S(1)}, f32[48,4096]{1,0:T(8,128)S(1)}, u32[]{:S(2)}, u32[]{:S(2)}) collective-permute-start(f32[48,4096]{1,0:T(8,128)S(1)} %bitcast.64), channel_id=1, source_target_pairs={{1,0},{2,1},{3,2},{4,3},{5,4},{6,5},{7,6},{8,7},{9,8},{10,9},{11,1... | collective-permute-start | bytes 2359304 | tf_op jit(solution)/shard_map/ppermute | solution.py:295
  29.0 37.1 %copy-start.20 = (f32[48,4096]{1,0:T(8,128)}, f32[48,4096]{1,0:T(8,128)S(1)}, u32[]{:S(2)}) copy-start(f32[48,4096]{1,0:T(8,128)S(1)} %collective-permute-done.l_ref) | copy-start | bytes 2359300
  29.0 20.7 %collective-permute-start.2 = (f32[48,4096]{1,0:T(8,128)S(1)}, f32[48,4096]{1,0:T(8,128)S(1)}, u32[]{:S(2)}, u32[]{:S(2)}) collective-permute-start(f32[48,4096]{1,0:T(8,128)S(1)} %bitcast.65), channel_id=1, source_target_pairs={{0,1},{1,2},{2,3},{3,4},{4,5},{5,6},{6,7},{7,8},{8,9},{9,10},{10,1... | collective-permute-start | bytes 2359304 | tf_op jit(solution)/shard_map/ppermute | solution.py:294
  33.2 17.7 %copy-start.6 = (f32[48,4096]{1,0:T(8,128)}, f32[48,4096]{1,0:T(8,128)S(1)}, u32[]{:S(2)}) copy-start(f32[48,4096]{1,0:T(8,128)S(1)} %collective-permute-done.9.rest_11_.rest_9_) | copy-start | bytes 2359300
  33.2 17.7 %collective-permute-start.13 = (f32[48,4096]{1,0:T(8,128)S(1)}, f32[48,4096]{1,0:T(8,128)S(1)}, u32[]{:S(2)}, u32[]{:S(2)}) collective-permute-start(f32[48,4096]{1,0:T(8,128)S(1)} %collective-permute-done.7.rest_9_.rest_7_), channel_id=1, source_target_pairs={{0,32},{32,0},{64,96},{96,64},{128,160},{160,128},{192,224},{224,1... | collective-permute-start | bytes 2359304 | tf_op jit(solution)/shard_map/ppermute | solution.py:21
  44.6 18.9 %collective-permute-start.14 = (f32[48,4096]{1,0:T(8,128)}, f32[48,4096]{1,0:T(8,128)}, u32[]{:S(2)}, u32[]{:S(2)}) collective-permute-start(f32[48,4096]{1,0:T(8,128)} %collective-permute-done.4.rest_6_.rest_4_), channel_id=1, source_target_pairs={{0,64},{32,96},{64,128},{96,160},{128,192},{160,224},{192,0},{224,... | collective-permute-start | bytes 2359304 | tf_op jit(solution)/shard_map/ppermute | solution.py:16
  44.7 21.4 %collective-permute-start.15 = (f32[48,4096]{1,0:T(8,128)}, f32[48,4096]{1,0:T(8,128)}, u32[]{:S(2)}, u32[]{:S(2)}) collective-permute-start(f32[48,4096]{1,0:T(8,128)} %collective-permute-done.5.rest_7_.rest_5_), channel_id=1, source_target_pairs={{0,192},{32,224},{64,0},{96,32},{128,64},{160,96},{192,128},{224,1... | collective-permute-start | bytes 2359304 | tf_op jit(solution)/shard_map/ppermute | solution.py:16
  47.4 18.6 %copy-start.21 = (f32[48,4096]{1,0:T(8,128)}, f32[48,4096]{1,0:T(8,128)S(1)}, u32[]{:S(2)}) copy-start(f32[48,4096]{1,0:T(8,128)S(1)} %collective-permute-done.3.r_ref) | copy-start | bytes 2359300
  47.5 31.2 %collective-permute-start.10 = (f32[48,4096]{1,0:T(8,128)}, f32[48,4096]{1,0:T(8,128)}, u32[]{:S(2)}, u32[]{:S(2)}) collective-permute-start(f32[48,4096]{1,0:T(8,128)} %collective-permute-done.4.rest_6_.rest_4_), channel_id=1, source_target_pairs={{0,32},{32,0},{64,96},{96,64},{128,160},{160,128},{192,224},{224,1... | collective-permute-start | bytes 2359304 | tf_op jit(solution)/shard_map/ppermute | solution.py:21
  49.7 16.7 %copy-start.22 = (f32[48,4096]{1,0:T(8,128)}, f32[48,4096]{1,0:T(8,128)S(1)}, u32[]{:S(2)}) copy-start(f32[48,4096]{1,0:T(8,128)S(1)} %collective-permute-done.2.l_ref) | copy-start | bytes 2359300
  49.7 29.0 %collective-permute-start.12 = (f32[48,4096]{1,0:T(8,128)}, f32[48,4096]{1,0:T(8,128)}, u32[]{:S(2)}, u32[]{:S(2)}) collective-permute-start(f32[48,4096]{1,0:T(8,128)} %collective-permute-done.6.rest_8_.rest_6_), channel_id=1, source_target_pairs={{0,32},{32,0},{64,96},{96,64},{128,160},{160,128},{192,224},{224,1... | collective-permute-start | bytes 2359304 | tf_op jit(solution)/shard_map/ppermute | solution.py:21
  50.9 27.8 %collective-permute-start.11 = (f32[48,4096]{1,0:T(8,128)}, f32[48,4096]{1,0:T(8,128)}, u32[]{:S(2)}, u32[]{:S(2)}) collective-permute-start(f32[48,4096]{1,0:T(8,128)} %collective-permute-done.5.rest_7_.rest_5_), channel_id=1, source_target_pairs={{0,32},{32,0},{64,96},{96,64},{128,160},{160,128},{192,224},{224,1... | collective-permute-start | bytes 2359304 | tf_op jit(solution)/shard_map/ppermute | solution.py:21
  63.5 23.7 %collective-permute-start.16 = (f32[48,4096]{1,0:T(8,128)}, f32[48,4096]{1,0:T(8,128)}, u32[]{:S(2)}, u32[]{:S(2)}) collective-permute-start(f32[48,4096]{1,0:T(8,128)} %collective-permute-done.14.rest_4_.rest_14_), channel_id=1, source_target_pairs={{0,32},{32,0},{64,96},{96,64},{128,160},{160,128},{192,224},{224,1... | collective-permute-start | bytes 2359304 | tf_op jit(solution)/shard_map/ppermute | solution.py:21
  66.1 21.1 %collective-permute-start.17 = (f32[48,4096]{1,0:T(8,128)}, f32[48,4096]{1,0:T(8,128)}, u32[]{:S(2)}, u32[]{:S(2)}) collective-permute-start(f32[48,4096]{1,0:T(8,128)} %collective-permute-done.15.rest_5_.rest_15_), channel_id=1, source_target_pairs={{0,32},{32,0},{64,96},{96,64},{128,160},{160,128},{192,224},{224,1... | collective-permute-start | bytes 2359304 | tf_op jit(solution)/shard_map/ppermute | solution.py:21
  87.2 5.3 %copy-start.9 = (f32[192,576]{1,0:T(8,128)S(1)}, f32[192,576]{1,0:T(8,128)}, u32[]{:S(2)}) copy-start(f32[192,576]{1,0:T(8,128)} %gram.2) | copy-start | bytes 1327108
  92.4 5.7 %copy-start.2 = (f32[48,4096]{1,0:T(8,128)S(1)}, f32[48,4096]{1,0:T(8,128)}, u32[]{:S(2)}) copy-start(f32[48,4096]{1,0:T(8,128)} %hamiltonian.2.rest_2_.rest_0_.rest_18_) | copy-start | bytes 2359300
  92.5 11.6 %copy-start.3 = (f32[48,4096]{1,0:T(8,128)S(1)}, f32[48,4096]{1,0:T(8,128)}, u32[]{:S(2)}) copy-start(f32[48,4096]{1,0:T(8,128)} %hamiltonian.3.rest_3_.rest_1_.rest_19_) | copy-start | bytes 2359300
  94.4 7.0 %collective-permute-start.18 = (f32[2,24,768]{2,1,0:T(8,128)}, f32[2,24,768]{2,1,0:T(8,128)S(1)}, u32[]{:S(2)}, u32[]{:S(2)}) collective-permute-start(f32[2,24,768]{2,1,0:T(8,128)} %get-tuple-element.17), channel_id=1, source_target_pairs={{0,16},{1,17},{2,18},{3,19},{4,20},{5,21},{6,22},{7,23},{8,24},{9,... | collective-permute-start | bytes 442376 | tf_op jit(solution)/shard_map/ppermute | solution.py:36
  96.7 7.4 %collective-permute-start.20 = (f32[2,24,768]{2,1,0:T(8,128)}, f32[2,24,768]{2,1,0:T(8,128)S(1)}, u32[]{:S(2)}, u32[]{:S(2)}) collective-permute-start(f32[2,24,768]{2,1,0:T(8,128)} %get-tuple-element.18), channel_id=1, source_target_pairs={{0,24},{1,25},{2,26},{3,27},{4,28},{5,29},{6,30},{7,31},{8,0},{9,1... | collective-permute-start | bytes 442376 | tf_op jit(solution)/shard_map/ppermute | solution.py:36
  97.4 9.4 %collective-permute-start.19 = (f32[2,24,768]{2,1,0:T(8,128)S(1)}, f32[2,24,768]{2,1,0:T(8,128)S(1)}, u32[]{:S(2)}, u32[]{:S(2)}) collective-permute-start(f32[2,24,768]{2,1,0:T(8,128)S(1)} %get-tuple-element.19), channel_id=1, source_target_pairs={{0,8},{1,9},{2,10},{3,11},{4,12},{5,13},{6,14},{7,15},{8,16},{9,17... | collective-permute-start | bytes 442376 | tf_op jit(solution)/shard_map/ppermute | solution.py:36
  98.1 18.5 %collective-permute-start.33 = (f32[48,4096]{1,0:T(8,128)S(1)}, f32[48,4096]{1,0:T(8,128)S(1)}, u32[]{:S(2)}, u32[]{:S(2)}) collective-permute-start(f32[48,4096]{1,0:T(8,128)S(1)} %copy-done.2), channel_id=1, source_target_pairs={{0,32},{32,0},{64,96},{96,64},{128,160},{160,128},{192,224},{224,1... | collective-permute-start | bytes 2359304 | tf_op jit(solution)/shard_map/ppermute | solution.py:21
  99.4 19.2 %collective-permute-start.32 = (f32[48,4096]{1,0:T(8,128)S(1)}, f32[48,4096]{1,0:T(8,128)}, u32[]{:S(2)}, u32[]{:S(2)}) collective-permute-start(f32[48,4096]{1,0:T(8,128)S(1)} %copy-done.2), channel_id=1, source_target_pairs={{0,192},{32,224},{64,0},{96,32},{128,64},{160,96},{192,128},{224,1... | collective-permute-start | bytes 2359304 | tf_op jit(solution)/shard_map/ppermute | solution.py:16
  101.4 28.2 %collective-permute-start.29 = (f32[48,4096]{1,0:T(8,128)S(1)}, f32[48,4096]{1,0:T(8,128)}, u32[]{:S(2)}, u32[]{:S(2)}) collective-permute-start(f32[48,4096]{1,0:T(8,128)S(1)} %copy-done.2), channel_id=1, source_target_pairs={{0,64},{32,96},{64,128},{96,160},{128,192},{160,224},{192,0},{224,... | collective-permute-start | bytes 2359304 | tf_op jit(solution)/shard_map/ppermute | solution.py:16
  104.0 31.4 %collective-permute-start.30 = (f32[48,4096]{1,0:T(8,128)S(1)}, f32[48,4096]{1,0:T(8,128)}, u32[]{:S(2)}, u32[]{:S(2)}) collective-permute-start(f32[48,4096]{1,0:T(8,128)S(1)} %copy-done.3), channel_id=1, source_target_pairs={{0,192},{32,224},{64,0},{96,32},{128,64},{160,96},{192,128},{224,1... | collective-permute-start | bytes 2359304 | tf_op jit(solution)/shard_map/ppermute | solution.py:16
  106.8 3.9 %collective-permute-start.21 = (f32[24,768]{1,0:T(8,128)S(1)}, f32[24,768]{1,0:T(8,128)S(1)}, u32[]{:S(2)}, u32[]{:S(2)}) collective-permute-start(f32[24,768]{1,0:T(8,128)S(1)} %select_bitcast_fusion), channel_id=1, source_target_pairs={{0,1},{1,0},{2,3},{3,2},{4,5},{5,4},{6,7},{7,6},{8,9},{9,8},{10,11... | collective-permute-start | bytes 221192 | tf_op jit(solution)/shard_map/ppermute | solution.py:26
  110.7 14.8 %collective-permute-start.24 = (f32[24,768]{1,0:T(8,128)S(1)}, f32[24,768]{1,0:T(8,128)S(1)}, u32[]{:S(2)}, u32[]{:S(2)}) collective-permute-start(f32[24,768]{1,0:T(8,128)S(1)} %bitcast_add_fusion.1), channel_id=1, source_target_pairs={{0,6},{1,7},{2,0},{3,1},{4,2},{5,3},{6,4},{7,5},{8,14},{9,15},{10,... | collective-permute-start | bytes 221192 | tf_op jit(solution)/shard_map/ppermute | solution.py:31
  116.7 55.6 %copy-start.10 = (f32[48,4096]{1,0:T(8,128)}, f32[48,4096]{1,0:T(8,128)S(1)}, u32[]{:S(2)}) copy-start(f32[48,4096]{1,0:T(8,128)S(1)} %collective-permute-done.33.rest_24_) | copy-start | bytes 2359300
  116.7 10.5 %collective-permute-start.23 = (f32[24,768]{1,0:T(8,128)S(1)}, f32[24,768]{1,0:T(8,128)S(1)}, u32[]{:S(2)}, u32[]{:S(2)}) collective-permute-start(f32[24,768]{1,0:T(8,128)S(1)} %bitcast_add_fusion.1), channel_id=1, source_target_pairs={{0,2},{1,3},{2,4},{3,5},{4,6},{5,7},{6,0},{7,1},{8,10},{9,11},{10,... | collective-permute-start | bytes 221192 | tf_op jit(solution)/shard_map/ppermute | solution.py:31
  118.6 8.8 %collective-permute-start.22 = (f32[24,768]{1,0:T(8,128)S(1)}, f32[24,768]{1,0:T(8,128)S(1)}, u32[]{:S(2)}, u32[]{:S(2)}) collective-permute-start(f32[24,768]{1,0:T(8,128)S(1)} %bitcast_add_fusion.1), channel_id=1, source_target_pairs={{0,4},{1,5},{2,6},{3,7},{4,0},{5,1},{6,2},{7,3},{8,12},{9,13},{10,... | collective-permute-start | bytes 221192 | tf_op jit(solution)/shard_map/ppermute | solution.py:31
  125.5 13.8 %collective-permute-start.34 = (f32[48,4096]{1,0:T(8,128)S(1)}, f32[48,4096]{1,0:T(8,128)S(1)}, u32[]{:S(2)}, u32[]{:S(2)}) collective-permute-start(f32[48,4096]{1,0:T(8,128)S(1)} %copy-done.3), channel_id=1, source_target_pairs={{0,32},{32,0},{64,96},{96,64},{128,160},{160,128},{192,224},{224,1... | collective-permute-start | bytes 2359304 | tf_op jit(solution)/shard_map/ppermute | solution.py:21
  127.1 20.8 %collective-permute-start.31 = (f32[48,4096]{1,0:T(8,128)S(1)}, f32[48,4096]{1,0:T(8,128)S(1)}, u32[]{:S(2)}, u32[]{:S(2)}) collective-permute-start(f32[48,4096]{1,0:T(8,128)S(1)} %copy-done.3), channel_id=1, source_target_pairs={{0,64},{32,96},{64,128},{96,160},{128,192},{160,224},{192,0},{224,... | collective-permute-start | bytes 2359304 | tf_op jit(solution)/shard_map/ppermute | solution.py:16
  127.4 20.9 %collective-permute-start.38 = (f32[48,4096]{1,0:T(8,128)}, f32[48,4096]{1,0:T(8,128)}, u32[]{:S(2)}, u32[]{:S(2)}) collective-permute-start(f32[48,4096]{1,0:T(8,128)} %collective-permute-done.32.rest_23_), channel_id=1, source_target_pairs={{0,32},{32,0},{64,96},{96,64},{128,160},{160,128},{192,224},{224,1... | collective-permute-start | bytes 2359304 | tf_op jit(solution)/shard_map/ppermute | solution.py:21
  129.6 5.9 %collective-permute-start.25 = (f32[24,768]{1,0:T(8,128)S(1)}, f32[24,768]{1,0:T(8,128)S(1)}, u32[]{:S(2)}, u32[]{:S(2)}) collective-permute-start(f32[24,768]{1,0:T(8,128)S(1)} %add_add_fusion), channel_id=1, source_target_pairs={{0,1},{1,0},{2,3},{3,2},{4,5},{5,4},{6,7},{7,6},{8,9},{9,8},{10,11... | collective-permute-start | bytes 221192 | tf_op jit(solution)/shard_map/ppermute | solution.py:26
  135.5 29.3 %collective-permute-start.39 = (f32[48,4096]{1,0:T(8,128)}, f32[48,4096]{1,0:T(8,128)S(1)}, u32[]{:S(2)}, u32[]{:S(2)}) collective-permute-start(f32[48,4096]{1,0:T(8,128)} %collective-permute-done.29.rest_20_), channel_id=1, source_target_pairs={{0,64},{32,96},{64,128},{96,160},{128,192},{160,224},{192,0},{224,... | collective-permute-start | bytes 2359304 | tf_op jit(solution)/shard_map/ppermute | solution.py:16
  135.5 30.2 %collective-permute-start.40 = (f32[48,4096]{1,0:T(8,128)}, f32[48,4096]{1,0:T(8,128)}, u32[]{:S(2)}, u32[]{:S(2)}) collective-permute-start(f32[48,4096]{1,0:T(8,128)} %collective-permute-done.30.rest_21_), channel_id=1, source_target_pairs={{0,192},{32,224},{64,0},{96,32},{128,64},{160,96},{192,128},{224,1... | collective-permute-start | bytes 2359304 | tf_op jit(solution)/shard_map/ppermute | solution.py:16
  139.3 8.6 %copy-start.11 = (f32[48,4096]{1,0:T(8,128)}, f32[48,4096]{1,0:T(8,128)S(1)}, u32[]{:S(2)}) copy-start(f32[48,4096]{1,0:T(8,128)S(1)} %collective-permute-done.34.rest_25_) | copy-start | bytes 2359300
  139.3 26.4 %collective-permute-start.28 = (f32[2,24,768]{2,1,0:T(8,128)}, f32[2,24,768]{2,1,0:T(8,128)S(1)}, u32[]{:S(2)}, u32[]{:S(2)}) collective-permute-start(f32[2,24,768]{2,1,0:T(8,128)} %maximum_select_fusion.1), channel_id=1, source_target_pairs={{0,24},{1,25},{2,26},{3,27},{4,28},{5,29},{6,30},{7,31},{8,0},{9,1... | collective-permute-start | bytes 442376 | tf_op jit(solution)/shard_map/ppermute | solution.py:36
  147.9 24.4 %copy-start.12 = (f32[48,4096]{1,0:T(8,128)}, f32[48,4096]{1,0:T(8,128)S(1)}, u32[]{:S(2)}) copy-start(f32[48,4096]{1,0:T(8,128)S(1)} %collective-permute-done.31.rest_22_) | copy-start | bytes 2359300
  147.9 18.3 %collective-permute-start.27 = (f32[2,24,768]{2,1,0:T(8,128)}, f32[2,24,768]{2,1,0:T(8,128)}, u32[]{:S(2)}, u32[]{:S(2)}) collective-permute-start(f32[2,24,768]{2,1,0:T(8,128)} %maximum_select_fusion.1), channel_id=1, source_target_pairs={{0,8},{1,9},{2,10},{3,11},{4,12},{5,13},{6,14},{7,15},{8,16},{9,17... | collective-permute-start | bytes 442376 | tf_op jit(solution)/shard_map/ppermute | solution.py:36
  148.3 17.9 %collective-permute-start.26 = (f32[2,24,768]{2,1,0:T(8,128)}, f32[2,24,768]{2,1,0:T(8,128)}, u32[]{:S(2)}, u32[]{:S(2)}) collective-permute-start(f32[2,24,768]{2,1,0:T(8,128)} %maximum_select_fusion.1), channel_id=1, source_target_pairs={{0,16},{1,17},{2,18},{3,19},{4,20},{5,21},{6,22},{7,23},{8,24},{9,... | collective-permute-start | bytes 442376 | tf_op jit(solution)/shard_map/ppermute | solution.py:36
  164.8 7.5 %copy-start.13 = (f32[48,4096]{1,0:T(8,128)}, f32[48,4096]{1,0:T(8,128)S(1)}, u32[]{:S(2)}) copy-start(f32[48,4096]{1,0:T(8,128)S(1)} %collective-permute-done.39.rest_30_) | copy-start | bytes 2359300
  164.8 3.9 %collective-permute-start.35 = (f32[48,4096]{1,0:T(8,128)}, f32[48,4096]{1,0:T(8,128)S(1)}, u32[]{:S(2)}, u32[]{:S(2)}) collective-permute-start(f32[48,4096]{1,0:T(8,128)} %collective-permute-done.29.rest_20_), channel_id=1, source_target_pairs={{0,32},{32,0},{64,96},{96,64},{128,160},{160,128},{192,224},{224,1... | collective-permute-start | bytes 2359304 | tf_op jit(solution)/shard_map/ppermute | solution.py:21
  165.6 4.4 %collective-permute-start.36 = (f32[48,4096]{1,0:T(8,128)}, f32[48,4096]{1,0:T(8,128)S(1)}, u32[]{:S(2)}, u32[]{:S(2)}) collective-permute-start(f32[48,4096]{1,0:T(8,128)} %collective-permute-done.30.rest_21_), channel_id=1, source_target_pairs={{0,32},{32,0},{64,96},{96,64},{128,160},{160,128},{192,224},{224,1... | collective-permute-start | bytes 2359304 | tf_op jit(solution)/shard_map/ppermute | solution.py:21
  165.7 4.3 %collective-permute-start.37 = (f32[48,4096]{1,0:T(8,128)S(1)}, f32[48,4096]{1,0:T(8,128)S(1)}, u32[]{:S(2)}, u32[]{:S(2)}) collective-permute-start(f32[48,4096]{1,0:T(8,128)S(1)} %collective-permute-done.31.rest_22_), channel_id=1, source_target_pairs={{0,32},{32,0},{64,96},{96,64},{128,160},{160,128},{192,224},{224,1... | collective-permute-start | bytes 2359304 | tf_op jit(solution)/shard_map/ppermute | solution.py:21
  166.2 5.0 %collective-permute-start.41 = (f32[48,4096]{1,0:T(8,128)S(1)}, f32[48,4096]{1,0:T(8,128)S(1)}, u32[]{:S(2)}, u32[]{:S(2)}) collective-permute-start(f32[48,4096]{1,0:T(8,128)S(1)} %collective-permute-done.39.rest_30_), channel_id=1, source_target_pairs={{0,32},{32,0},{64,96},{96,64},{128,160},{160,128},{192,224},{224,1... | collective-permute-start | bytes 2359304 | tf_op jit(solution)/shard_map/ppermute | solution.py:21
  166.3 6.0 %collective-permute-start.42 = (f32[48,4096]{1,0:T(8,128)}, f32[48,4096]{1,0:T(8,128)S(1)}, u32[]{:S(2)}, u32[]{:S(2)}) collective-permute-start(f32[48,4096]{1,0:T(8,128)} %collective-permute-done.40.rest_31_), channel_id=1, source_target_pairs={{0,32},{32,0},{64,96},{96,64},{128,160},{160,128},{192,224},{224,1... | collective-permute-start | bytes 2359304 | tf_op jit(solution)/shard_map/ppermute | solution.py:21
  168.6 3.6 %copy-start.8 = (f32[4,2,24,768]{3,2,1,0:T(8,128)}, f32[4,2,24,768]{3,2,1,0:T(8,128)S(1)}, u32[]{:S(2)}) copy-start(f32[4,2,24,768]{3,2,1,0:T(8,128)S(1)} %bitcast_dynamic-update-slice_fusion) | copy-start | bytes 1769476
  168.7 3.6 %copy-start.14 = (f32[48,4096]{1,0:T(8,128)}, f32[48,4096]{1,0:T(8,128)S(1)}, u32[]{:S(2)}) copy-start(f32[48,4096]{1,0:T(8,128)S(1)} %collective-permute-done.35.rest_26_) | copy-start | bytes 2359300
  170.0 2.3 %copy-start.16 = (f32[48,4096]{1,0:T(8,128)}, f32[48,4096]{1,0:T(8,128)S(1)}, u32[]{:S(2)}) copy-start(f32[48,4096]{1,0:T(8,128)S(1)} %collective-permute-done.37.rest_28_) | copy-start | bytes 2359300
  170.0 2.3 %copy-start.15 = (f32[48,4096]{1,0:T(8,128)}, f32[48,4096]{1,0:T(8,128)S(1)}, u32[]{:S(2)}) copy-start(f32[48,4096]{1,0:T(8,128)S(1)} %collective-permute-done.36.rest_27_) | copy-start | bytes 2359300
  186.4 20.1 %all-to-all-start = ((f32[256,1,128]{2,1,0:T(1,128)}), f32[256,1,128]{2,1,0:T(1,128)S(1)}, u32[]{:S(2)}, u32[]{:S(2)}) async-start(f32[256,1,128]{2,1,0:T(1,128)} %bitcast.86), calls=%async_computation | async-start | bytes 262144 | tf_op jit(solution)/shard_map/all_to_all | solution.py:307
  (4 other events, 3.7 us)

commit v3 on v2

--- a/solution.py
+++ b/solution.py
@@ -7,7 +7,9 @@
 
 coeffs = (-205.0 / 72.0, 8.0 / 5.0, -1.0 / 5.0, 8.0 / 315.0, -1.0 / 560.0)
 step_length = 0.05
-VMEM_LIMIT = 56 * 1024 * 1024
+GRAM_VMEM = 56 * 1024 * 1024
+FAR_VMEM = 24 * 1024 * 1024
+GRADIENT_VMEM = 32 * 1024 * 1024
 ZS = 8
 
 
@@ -116,7 +118,7 @@
         at += ref.shape[0]
 
 
-def gram(own_blocks, blocks):
+def gram(own_blocks, blocks, grant):
     cells = blocks[0].shape[1]
     count = len(own_blocks)
     rows = sum(b.shape[0] for b in own_blocks)
@@ -149,7 +151,7 @@
             pltpu.VMEM((total, chunk), jnp.bfloat16),
             pltpu.VMEM((2 * rows, chunk), jnp.bfloat16),
         ],
-        compiler_params=pltpu.CompilerParams(vmem_limit_bytes=VMEM_LIMIT),
+        compiler_params=pltpu.CompilerParams(vmem_limit_bytes=grant),
         cost_estimate=pl.CostEstimate(
             flops=6 * rows * total * cells, bytes_accessed=4 * cells * (rows + total), transcendentals=0
         ),
@@ -250,7 +252,7 @@
             pltpu.VMEM((2 * total, chunk), jnp.bfloat16),
             pltpu.VMEM((2 * total, chunk), jnp.bfloat16),
         ],
-        compiler_params=pltpu.CompilerParams(vmem_limit_bytes=VMEM_LIMIT),
+        compiler_params=pltpu.CompilerParams(vmem_limit_bytes=GRADIENT_VMEM),
         cost_estimate=pl.CostEstimate(
             flops=12 * own * total * cells, bytes_accessed=8 * cells * total, transcendentals=0
         ),
@@ -298,9 +300,11 @@
         image.append(apply_hamiltonian(c[index], left, right, potential.reshape(1, -1)))
     near_image = gather_near(*image)
     far_image = gather_far(near_image)
-    part_near = gram(c + image, near)
-    part_far = gram(c + image, far)
-    overlap = sum_over_slabs(jnp.concatenate([part_near, part_far], axis=1))
+    part_a = gram(c + image[:1], near, GRAM_VMEM)
+    part_b = gram(image[1:], near, GRAM_VMEM)
+    part_far = gram(c + image, far, FAR_VMEM)
+    part = jnp.concatenate([jnp.concatenate([part_a, part_b], axis=0), part_far], axis=1)
+    overlap = sum_over_slabs(part)
     grad, sums = gradient_of(
         overlap, near + far, near_image + far_image, image, prev, slabs * c[0].shape[1]
     )

time: 212 us -> 226 us (1.066)
  local copies, waits for them, and re-layouts: 14 us -> 22.3 us
  waiting for transfers between devices: 79.1 us -> 86.7 us
  starting transfers between devices: 75.6 us -> 70.7 us
  Pallas kernels: 39.5 us -> 42.2 us
    ppermute x2, waiting for transfers between devices: 0.19 us -> 12.6 us  [on_device(): lax.ppermute(c[index], 'dom', [(i + 1, i) for i in range(slabs - 1)])]
    ppermute x12, waiting for transfers between devices: 60 us -> 48.7 us  [shift_orb(): return lax.ppermute(v, 'orb', [(i, (i + k) % n) for i in range(n)])]
    ppermute x3, starting transfers between devices: 12.8 us -> 3.77 us  [shift_z(): lax.ppermute(v, 'dom', [(i, i // ZS * ZS + (i + k) % ZS) for i in range(n)])]
    unnamed x52 -> x62, local copies, waits for them, and re-layouts: 9.88 us -> 18.1 us
    pallas_call x2 -> x3, Pallas kernels: 13.7 us -> 18.9 us  [gram(): pl.pallas_call(kernel, out_shape=jax.ShapeDtypeStruct((rows, total), jnp....]
    ppermute x6, starting transfers between devices: 8.9 us -> 13.8 us  [shift_y(): return lax.ppermute(v, 'dom', [(i, (i + k * ZS) % n) for i in range(n)])]
    ppermute x3, waiting for transfers between devices: 0.23 us -> 4.94 us  [shift_z(): lax.ppermute(v, 'dom', [(i, i // ZS * ZS + (i + k) % ZS) for i in range(n)])]
    ppermute x12, starting transfers between devices: 12.9 us -> 16.3 us  [shift_orb(): return lax.ppermute(v, 'orb', [(i, (i + k) % n) for i in range(n)])]
  transfers between devices with their start and end apart: 44 -> 44, of which waited for: 17 -> 15; matrix products, arithmetic and copies ran while one was open for 5% -> 5% of each run, Pallas kernels for 8% -> 10%
where the time goes in v3:
time: 226 us; the launch traced here: 225 us
  waiting for transfers between devices  86.7 us (38%)
  starting transfers between devices  70.7 us (31%)
  Pallas kernels  42.2 us (19%)
  local copies, waits for them, and re-layouts  22.3 us (10%)
    ppermute x12, waiting for transfers between devices, shift_orb(): return lax.ppermute(v, 'orb', [(i, (i + k) % n) for i in range(n)])  48.7 us
    pallas_call x3, Pallas kernels, gram(): pl.pallas_call(kernel, out_shape=jax.ShapeDtypeStruct((rows, total), jnp....  18.9 us
    ppermute x16, starting transfers between devices, swap_core(): return lax.ppermute(v, 'orb', [(i, i ^ 1) for i in range(n)])  18.1 us
    unnamed x62, local copies, waits for them, and re-layouts  18.1 us
    ppermute x12, starting transfers between devices, shift_orb(): return lax.ppermute(v, 'orb', [(i, (i + k) % n) for i in range(n)])  16.3 us
    ppermute x6, starting transfers between devices, shift_y(): return lax.ppermute(v, 'dom', [(i, (i + k * ZS) % n) for i in range(n)])  13.8 us
    ppermute x2, waiting for transfers between devices, on_device(): lax.ppermute(c[index], 'dom', [(i + 1, i) for i in range(slabs - 1)])  12.6 us
    pallas_call x1, Pallas kernels, gradient_of(): pl.pallas_call(kernel, out_shape=(jax.ShapeDtypeStruct((own, cells), jnp....  10.7 us
  transfers between devices with their start and end apart: 44, of which 15 were waited for; matrix products, arithmetic and copies ran while one was open for 5% of the time, Pallas kernels for 10%

profile of v3, /device:TPU:1, one launch (start us, length us, event | category | flops | bytes accessed | tf_op | source)
XLA Modules:
  0.0 224.9 jit_solution(8314656541160351295)
XLA Ops:
  0.6 1.5 fusion.3
  2.6 3.3 %collective-permute-start.6 = (f32[48,4096]{1,0:T(8,128)S(1)}, f32[48,4096]{1,0:T(8,128)S(1)}, u32[]{:S(2)}, u32[]{:S(2)}) collective-permute-start(f32[48,4096]{1,0:T(8,128)S(1)} %bitcast.51), channel_id=1, source_target_pairs={{0,32},{32,0},{64,96},{96,64},{128,160},{160,128},{192,224},{224,1... | collective-permute-start | bytes 2359304 | tf_op jit(solution)/shard_map/ppermute | solution.py:23
  5.9 0.8 collective-permute-start.5
  7.4 1.3 collective-permute-start.1
  8.6 4.0 %collective-permute-start = (f32[48,4096]{1,0:T(8,128)S(1)}, f32[48,4096]{1,0:T(8,128)S(1)}, u32[]{:S(2)}, u32[]{:S(2)}) collective-permute-start(f32[48,4096]{1,0:T(8,128)S(1)} %bitcast.55), channel_id=1, source_target_pairs={{0,1},{1,2},{2,3},{3,4},{4,5},{5,6},{6,7},{7,8},{8,9},{9,10},{10,1... | collective-permute-start | bytes 2359304 | tf_op jit(solution)/shard_map/ppermute | solution.py:296
  13.2 1.3 collective-permute-start.13
  14.5 10.5 %collective-permute-done.5.rest_8_.rest_6_.rest_7_ = f32[48,4096]{1,0:T(8,128)S(1)} collective-permute-done((f32[48,4096]{1,0:T(8,128)S(1)}, f32[48,4096]{1,0:T(8,128)S(1)}, u32[]{:S(2)}, u32[]{:S(2)}) %collective-permute-start.5) | collective-permute-done | bytes 786464 | tf_op jit(solution)/shard_map/ppermute | solution.py:18
  25.0 2.0 collective-permute-start.12
  27.1 3.5 %collective-permute-start.3 = (f32[48,4096]{1,0:T(8,128)S(1)}, f32[48,4096]{1,0:T(8,128)}, u32[]{:S(2)}, u32[]{:S(2)}) collective-permute-start(f32[48,4096]{1,0:T(8,128)S(1)} %bitcast.64), channel_id=1, source_target_pairs={{0,192},{32,224},{64,0},{96,32},{128,64},{160,96},{192,128},{224,1... | collective-permute-start | bytes 2359304 | tf_op jit(solution)/shard_map/ppermute | solution.py:18
  30.6 1.5 collective-permute-start.7
  32.1 12.6 %collective-permute-done.13.r_ref = f32[48,4096]{1,0:T(8,128)} collective-permute-done((f32[48,4096]{1,0:T(8,128)S(1)}, f32[48,4096]{1,0:T(8,128)}, u32[]{:S(2)}, u32[]{:S(2)}) %collective-permute-start.13) | collective-permute-done | bytes 786464 | tf_op jit(solution)/shard_map/ppermute | solution.py:297
  44.6 1.5 collective-permute-start.11
  46.2 3.5 %collective-permute-start.15 = (f32[48,4096]{1,0:T(8,128)}, f32[48,4096]{1,0:T(8,128)}, u32[]{:S(2)}, u32[]{:S(2)}) collective-permute-start(f32[48,4096]{1,0:T(8,128)} %collective-permute-done.3.rest_6_.rest_4_.rest_5_), channel_id=1, source_target_pairs={{0,192},{32,224},{64,0},{96,32},{128,64},{160,96},{192,128},{224,1... | collective-permute-start | bytes 2359304 | tf_op jit(solution)/shard_map/ppermute | solution.py:18
  49.8 2.4 %collective-permute-start.8 = (f32[48,4096]{1,0:T(8,128)}, f32[48,4096]{1,0:T(8,128)}, u32[]{:S(2)}, u32[]{:S(2)}) collective-permute-start(f32[48,4096]{1,0:T(8,128)} %collective-permute-done.2.rest_5_.rest_3_.rest_4_), channel_id=1, source_target_pairs={{0,32},{32,0},{64,96},{96,64},{128,160},{160,128},{192,224},{224,1... | collective-permute-start | bytes 2359304 | tf_op jit(solution)/shard_map/ppermute | solution.py:23
  52.4 1.5 collective-permute-start.10
  54.0 0.8 copy-done.12
  54.8 14.4 %collective-permute-done.14.rest_4_.rest_14_ = f32[48,4096]{1,0:T(8,128)} collective-permute-done((f32[48,4096]{1,0:T(8,128)}, f32[48,4096]{1,0:T(8,128)}, u32[]{:S(2)}, u32[]{:S(2)}) %collective-permute-start.14) | collective-permute-done | bytes 786464 | tf_op jit(solution)/shard_map/ppermute | solution.py:18
  69.3 1.0 collective-permute-start.16
  70.5 3.6 %copy.15 = f32[12,8,32,128]{3,1,2,0:T(8,128)} copy(f32[12,8,32,128]{3,2,1,0:T(8,128)} %bitcast.81) | data formatting | bytes 3145728
  74.2 4.3 %hamiltonian.2.rest_2_.rest_0_.rest_18_ = f32[48,4096]{1,0:T(8,128)} custom-call(f32[48,4096]{1,0:T(8,128)} %bitcast.56, f32[48,4096]{1,0:T(8,128)} %copy-done.25, f32[48,4096]{1,0:T(8,128)} %copy-done.24, f32[1,4096]{1,0:T(1,128)} %bitcast.88), custom_call_target="tpu_custom_call" | custom-call | flops 7864320 | bytes 3145728 | tf_op jit(solution)/shard_map/hamiltonian/pallas_call | solution.py:92
  78.5 4.2 %hamiltonian.3.rest_0_.rest_3_.rest_1_.rest_19_ = f32[48,4096]{1,0:T(8,128)} custom-call(f32[48,4096]{1,0:T(8,128)} %bitcast.67, f32[48,4096]{1,0:T(8,128)} %copy-done.26, f32[48,4096]{1,0:T(8,128)} %collective-permute-done.13.r_ref, f32[1,4096]{1,0:T(1,128)} %bitcast.89), custom_call_target="tpu_custom_call" | custom-call | flops 7864320 | bytes 3145728 | tf_op jit(solution)/shard_map/hamiltonian/pallas_call | solution.py:92
  82.7 6.8 %gram.4 = f32[48,576]{1,0:T(8,128)} custom-call(f32[48,4096]{1,0:T(8,128)} %hamiltonian.3.rest_0_.rest_3_.rest_1_.rest_19_, f32[48,4096]{1,0:T(8,128)} %bitcast.57, f32[48,4096]{1,0:T(8,128)} %bitcast.68, f32[48,4096]{1,0:T(8,128)} %collective-permute-done.2.rest_5_.rest_3_.rest_4_, f32[48,4096]{1,0:T(8,128)} %collective-permute-done.3.rest_6_.rest_4_.rest_5_, ...), custom_call_target="tpu_custom_call" | custom-call | flops 679477248 | bytes 10223616 | tf_op jit(solution)/shard_map/gram/pallas_call | solution.py:143
  89.6 7.9 %gram.3 = f32[144,576]{1,0:T(8,128)} custom-call(f32[48,4096]{1,0:T(8,128)} %bitcast.58, f32[48,4096]{1,0:T(8,128)} %bitcast.69, f32[48,4096]{1,0:T(8,128)} %hamiltonian.2.rest_2_.rest_0_.rest_18_, f32[48,4096]{1,0:T(8,128)} %bitcast.59, f32[48,4096]{1,0:T(8,128)} %bitcast.70, f32[48,4096]{1,0:T(8,128)} %collective-permute-done.2.rest_5_.rest_3_.rest_4_, ...), custom_call_target="tpu_custom_call" | custom-call | flops 2038431744 | bytes 11796480 | tf_op jit(solution)/shard_map/gram/pallas_call | solution.py:143
  97.6 4.2 %gram.5 = f32[192,192]{1,0:T(8,128)S(1)} custom-call(f32[48,4096]{1,0:T(8,128)S(1)} %bitcast.60, f32[48,4096]{1,0:T(8,128)S(1)} %bitcast.71, f32[48,4096]{1,0:T(8,128)S(1)} %copy-done.5, f32[48,4096]{1,0:T(8,128)S(1)} %copy-done.4, f32[48,4096]{1,0:T(8,128)} %collective-permute-done.14.rest_4_.rest_14_, f32[48,4096]{1,0:T(8,128)} %collective-permute-done.15.rest_5_.rest_15_, ...), custom_call_target="tpu_custom_call" | custom-call | flops 905969664 | bytes 6291456 | tf_op jit(solution)/shard_map/gram/pallas_call | solution.py:143
  102.0 0.8 dynamic-slice_bitcast_fusion.2
  102.8 7.5 %collective-permute-start.18 = (f32[2,24,768]{2,1,0:T(8,128)}, f32[2,24,768]{2,1,0:T(8,128)S(1)}, u32[]{:S(2)}, u32[]{:S(2)}) collective-permute-start(f32[2,24,768]{2,1,0:T(8,128)} %get-tuple-element.17), channel_id=1, source_target_pairs={{0,16},{1,17},{2,18},{3,19},{4,20},{5,21},{6,22},{7,23},{8,24},{9,... | collective-permute-start | bytes 442376 | tf_op jit(solution)/shard_map/ppermute | solution.py:38
  110.3 0.8 collective-permute-start.20
  111.8 1.3 collective-permute-start.33
  113.1 1.9 collective-permute-start.32
  115.0 3.0 %collective-permute-done.20 = f32[2,24,768]{2,1,0:T(8,128)S(1)} collective-permute-done((f32[2,24,768]{2,1,0:T(8,128)}, f32[2,24,768]{2,1,0:T(8,128)S(1)}, u32[]{:S(2)}, u32[]{:S(2)}) %collective-permute-start.20) | collective-permute-done | bytes 147488 | tf_op jit(solution)/shard_map/ppermute | solution.py:38
  118.0 2.8 %collective-permute-start.30 = (f32[48,4096]{1,0:T(8,128)S(1)}, f32[48,4096]{1,0:T(8,128)}, u32[]{:S(2)}, u32[]{:S(2)}) collective-permute-start(f32[48,4096]{1,0:T(8,128)S(1)} %copy-done.4), channel_id=1, source_target_pairs={{0,192},{32,224},{64,0},{96,32},{128,64},{160,96},{192,128},{224,1... | collective-permute-start | bytes 2359304 | tf_op jit(solution)/shard_map/ppermute | solution.py:18
  120.8 1.0 fusion.2
  121.9 3.6 %collective-permute-done.21 = f32[24,768]{1,0:T(8,128)S(1)} collective-permute-done((f32[24,768]{1,0:T(8,128)S(1)}, f32[24,768]{1,0:T(8,128)S(1)}, u32[]{:S(2)}, u32[]{:S(2)}) %collective-permute-start.21) | collective-permute-done | bytes 73760 | tf_op jit(solution)/shard_map/ppermute | solution.py:28
  125.7 2.3 %collective-permute-start.23 = (f32[24,768]{1,0:T(8,128)S(1)}, f32[24,768]{1,0:T(8,128)S(1)}, u32[]{:S(2)}, u32[]{:S(2)}) collective-permute-start(f32[24,768]{1,0:T(8,128)S(1)} %bitcast_add_fusion.1), channel_id=1, source_target_pairs={{0,2},{1,3},{2,4},{3,5},{4,6},{5,7},{6,0},{7,1},{8,10},{9,11},{10,... | collective-permute-start | bytes 221192 | tf_op jit(solution)/shard_map/ppermute | solution.py:33
  128.0 4.3 %collective-permute-done.32.rest_23_ = f32[48,4096]{1,0:T(8,128)} collective-permute-done((f32[48,4096]{1,0:T(8,128)S(1)}, f32[48,4096]{1,0:T(8,128)}, u32[]{:S(2)}, u32[]{:S(2)}) %collective-permute-start.32) | collective-permute-done | bytes 786464 | tf_op jit(solution)/shard_map/ppermute | solution.py:18
  132.3 1.3 collective-permute-start.22
  133.6 1.6 collective-permute-start.34
  135.2 4.9 %collective-permute-done.22 = f32[24,768]{1,0:T(8,128)S(1)} collective-permute-done((f32[24,768]{1,0:T(8,128)S(1)}, f32[24,768]{1,0:T(8,128)S(1)}, u32[]{:S(2)}, u32[]{:S(2)}) %collective-permute-start.22) | collective-permute-done | bytes 73760 | tf_op jit(solution)/shard_map/ppermute | solution.py:33
  140.2 1.7 collective-permute-start.38
  142.1 7.1 %collective-permute-done.30.rest_21_ = f32[48,4096]{1,0:T(8,128)} collective-permute-done((f32[48,4096]{1,0:T(8,128)S(1)}, f32[48,4096]{1,0:T(8,128)}, u32[]{:S(2)}, u32[]{:S(2)}) %collective-permute-start.30) | collective-permute-done | bytes 786464 | tf_op jit(solution)/shard_map/ppermute | solution.py:18
  149.1 3.1 %collective-permute-start.40 = (f32[48,4096]{1,0:T(8,128)}, f32[48,4096]{1,0:T(8,128)}, u32[]{:S(2)}, u32[]{:S(2)}) collective-permute-start(f32[48,4096]{1,0:T(8,128)} %collective-permute-done.30.rest_21_), channel_id=1, source_target_pairs={{0,192},{32,224},{64,0},{96,32},{128,64},{160,96},{192,128},{224,1... | collective-permute-start | bytes 2359304 | tf_op jit(solution)/shard_map/ppermute | solution.py:18
  152.9 0.9 copy-done.14
  153.8 2.0 collective-permute-start.28
  155.8 0.9 copy-done.16
  156.8 0.9 copy-done.18
  157.6 2.8 %collective-permute-start.26 = (f32[2,24,768]{2,1,0:T(8,128)}, f32[2,24,768]{2,1,0:T(8,128)}, u32[]{:S(2)}, u32[]{:S(2)}) collective-permute-start(f32[2,24,768]{2,1,0:T(8,128)} %maximum_select_fusion.1), channel_id=1, source_target_pairs={{0,16},{1,17},{2,18},{3,19},{4,20},{5,21},{6,22},{7,23},{8,24},{9,... | collective-permute-start | bytes 442376 | tf_op jit(solution)/shard_map/ppermute | solution.py:38
  160.4 12.0 %collective-permute-done.39.rest_30_ = f32[48,4096]{1,0:T(8,128)} collective-permute-done((f32[48,4096]{1,0:T(8,128)}, f32[48,4096]{1,0:T(8,128)}, u32[]{:S(2)}, u32[]{:S(2)}) %collective-permute-start.39) | collective-permute-done | bytes 786464 | tf_op jit(solution)/shard_map/ppermute | solution.py:18
  172.4 0.9 collective-permute-start.35
  174.5 0.9 bitcast_dynamic-update-slice_fusion.2
  175.4 0.9 bitcast_dynamic-update-slice_fusion.1
  176.4 1.4 collective-permute-done.37.rest_28_
  177.7 1.1 collective-permute-done.41.rest_32_
  178.9 1.1 collective-permute-done.42.rest_33_
  180.0 0.9 copy-done.23
  180.9 1.1 copy-done.11
  182.1 1.1 copy-done.13
  183.2 1.1 copy-done.15
  184.3 1.1 copy-done.17
  185.5 1.1 copy-done.19
  186.6 10.7 %gradient.1 = (f32[96,4096]{1,0:T(8,128)}, f32[256,128]{1,0:T(8,128)}) custom-call(f32[192,768]{1,0:T(8,128)S(1)} %bitcast.73, f32[96,4096]{1,0:T(8,128)} %bitcast.74, f32[48,4096]{1,0:T(8,128)S(1)} %copy-done.5, f32[48,4096]{1,0:T(8,128)S(1)} %copy-done.4, f32[48,4096]{1,0:T(8,128)S(1)} %bitcast.61, f32[48,4096]{1,0:T(8,128)S(1)} %bitcast.72, ...), custom_call_target="tpu_custom_call" | custom-call | flops 3623878656 | bytes 25165824 | tf_op jit(solution)/shard_map/gradient/pallas_call | solution.py:240
  197.3 9.9 %all-to-all-start = ((f32[256,1,128]{2,1,0:T(1,128)}), f32[256,1,128]{2,1,0:T(1,128)S(1)}, u32[]{:S(2)}, u32[]{:S(2)}) async-start(f32[256,1,128]{2,1,0:T(1,128)} %bitcast.17), calls=%async_computation | async-start | bytes 262144 | tf_op jit(solution)/shard_map/all_to_all | solution.py:311
  207.2 2.8 %copy.11 = f32[12,8,32,128]{3,2,1,0:T(8,128)} copy(f32[12,8,32,128]{3,1,2,0:T(8,128)} %bitcast.82) | data formatting | bytes 3145728
  210.0 10.2 %all-to-all-done = f32[256,1,128]{2,1,0:T(1,128)S(1)} async-done(((f32[256,1,128]{2,1,0:T(1,128)}), f32[256,1,128]{2,1,0:T(1,128)S(1)}, u32[]{:S(2)}, u32[]{:S(2)}) %all-to-all-start) | async-done | bytes 131104 | tf_op jit(solution)/shard_map/all_to_all | solution.py:311
  220.9 4.1 %advance.1 = (f32[96,4,8,128]{3,2,1,0:T(8,128)}, f32[96,4,8,128]{3,2,1,0:T(8,128)}) custom-call(f32[256,128]{1,0:T(8,128)} %bitcast.85, f32[96,4,8,128]{3,2,1,0:T(8,128)} %c_ref.1, f32[96,4,8,128]{3,2,1,0:T(8,128)} %d_ref.1, f32[96,4,8,128]{3,2,1,0:T(8,128)} %bitcast.75), custom_call_target="tpu_custom_call" | custom-call | flops 1572864 | bytes 7864320 | tf_op jit(solution)/shard_map/advance/pallas_call | solution.py:276
  (106 shorter events, 6.2 us)
Async XLA Ops:
  2.6 71.6 %copy-start = (f32[6,8,32,128]{3,1,2,0:T(8,128)}, f32[6,8,32,128]{3,1,2,0:T(8,128)S(1)}, u32[]{:S(2)}) copy-start(f32[6,8,32,128]{3,1,2,0:T(8,128)S(1)} %copy.17) | copy-start | bytes 2359300
  2.6 10.6 %collective-permute-start.6 = (f32[48,4096]{1,0:T(8,128)S(1)}, f32[48,4096]{1,0:T(8,128)S(1)}, u32[]{:S(2)}, u32[]{:S(2)}) collective-permute-start(f32[48,4096]{1,0:T(8,128)S(1)} %bitcast.51), channel_id=1, source_target_pairs={{0,32},{32,0},{64,96},{96,64},{128,160},{160,128},{192,224},{224,1... | collective-permute-start | bytes 2359304 | tf_op jit(solution)/shard_map/ppermute | solution.py:23
  5.9 19.1 %collective-permute-start.5 = (f32[48,4096]{1,0:T(8,128)S(1)}, f32[48,4096]{1,0:T(8,128)S(1)}, u32[]{:S(2)}, u32[]{:S(2)}) collective-permute-start(f32[48,4096]{1,0:T(8,128)S(1)} %bitcast.52), channel_id=1, source_target_pairs={{0,192},{32,224},{64,0},{96,32},{128,64},{160,96},{192,128},{224,1... | collective-permute-start | bytes 2359304 | tf_op jit(solution)/shard_map/ppermute | solution.py:18
  6.7 20.4 %collective-permute-start.2 = (f32[48,4096]{1,0:T(8,128)S(1)}, f32[48,4096]{1,0:T(8,128)}, u32[]{:S(2)}, u32[]{:S(2)}) collective-permute-start(f32[48,4096]{1,0:T(8,128)S(1)} %bitcast.53), channel_id=1, source_target_pairs={{0,64},{32,96},{64,128},{96,160},{128,192},{160,224},{192,0},{224,... | collective-permute-start | bytes 2359304 | tf_op jit(solution)/shard_map/ppermute | solution.py:18
  7.4 23.2 %collective-permute-start.1 = (f32[48,4096]{1,0:T(8,128)S(1)}, f32[48,4096]{1,0:T(8,128)S(1)}, u32[]{:S(2)}, u32[]{:S(2)}) collective-permute-start(f32[48,4096]{1,0:T(8,128)S(1)} %bitcast.54), channel_id=1, source_target_pairs={{1,0},{2,1},{3,2},{4,3},{5,4},{6,5},{7,6},{8,7},{9,8},{10,9},{11,1... | collective-permute-start | bytes 2359304 | tf_op jit(solution)/shard_map/ppermute | solution.py:297
  8.6 23.4 %collective-permute-start = (f32[48,4096]{1,0:T(8,128)S(1)}, f32[48,4096]{1,0:T(8,128)S(1)}, u32[]{:S(2)}, u32[]{:S(2)}) collective-permute-start(f32[48,4096]{1,0:T(8,128)S(1)} %bitcast.55), channel_id=1, source_target_pairs={{0,1},{1,2},{2,3},{3,4},{4,5},{5,6},{6,7},{7,8},{8,9},{9,10},{10,1... | collective-permute-start | bytes 2359304 | tf_op jit(solution)/shard_map/ppermute | solution.py:296
  13.2 61.1 %copy-start.2 = (f32[6,8,32,128]{3,1,2,0:T(8,128)}, f32[6,8,32,128]{3,1,2,0:T(8,128)S(1)}, u32[]{:S(2)}) copy-start(f32[6,8,32,128]{3,1,2,0:T(8,128)S(1)} %copy.16) | copy-start | bytes 2359300
  13.2 61.0 %copy-start.6 = (f32[48,4096]{1,0:T(8,128)}, f32[48,4096]{1,0:T(8,128)S(1)}, u32[]{:S(2)}) copy-start(f32[48,4096]{1,0:T(8,128)S(1)} %collective-permute-done.6.rest_9_.rest_7_.rest_8_) | copy-start | bytes 2359300
  13.2 31.5 %collective-permute-start.13 = (f32[48,4096]{1,0:T(8,128)S(1)}, f32[48,4096]{1,0:T(8,128)}, u32[]{:S(2)}, u32[]{:S(2)}) collective-permute-start(f32[48,4096]{1,0:T(8,128)S(1)} %bitcast.62), channel_id=1, source_target_pairs={{1,0},{2,1},{3,2},{4,3},{5,4},{6,5},{7,6},{8,7},{9,8},{10,9},{11,1... | collective-permute-start | bytes 2359304 | tf_op jit(solution)/shard_map/ppermute | solution.py:297
  25.0 49.2 %copy-start.8 = (f32[48,4096]{1,0:T(8,128)}, f32[48,4096]{1,0:T(8,128)S(1)}, u32[]{:S(2)}) copy-start(f32[48,4096]{1,0:T(8,128)S(1)} %collective-permute-done.5.rest_8_.rest_6_.rest_7_) | copy-start | bytes 2359300
  25.0 21.2 %collective-permute-start.12 = (f32[48,4096]{1,0:T(8,128)S(1)}, f32[48,4096]{1,0:T(8,128)S(1)}, u32[]{:S(2)}, u32[]{:S(2)}) collective-permute-start(f32[48,4096]{1,0:T(8,128)S(1)} %bitcast.63), channel_id=1, source_target_pairs={{0,1},{1,2},{2,3},{3,4},{4,5},{5,6},{6,7},{7,8},{8,9},{9,10},{10,1... | collective-permute-start | bytes 2359304 | tf_op jit(solution)/shard_map/ppermute | solution.py:296
  27.1 19.2 %collective-permute-start.3 = (f32[48,4096]{1,0:T(8,128)S(1)}, f32[48,4096]{1,0:T(8,128)}, u32[]{:S(2)}, u32[]{:S(2)}) collective-permute-start(f32[48,4096]{1,0:T(8,128)S(1)} %bitcast.64), channel_id=1, source_target_pairs={{0,192},{32,224},{64,0},{96,32},{128,64},{160,96},{192,128},{224,1... | collective-permute-start | bytes 2359304 | tf_op jit(solution)/shard_map/ppermute | solution.py:18
  30.6 38.7 %copy-start.24 = (f32[48,4096]{1,0:T(8,128)}, f32[48,4096]{1,0:T(8,128)S(1)}, u32[]{:S(2)}) copy-start(f32[48,4096]{1,0:T(8,128)S(1)} %collective-permute-done.1.r_ref) | copy-start | bytes 2359300
  30.6 19.2 %collective-permute-start.7 = (f32[48,4096]{1,0:T(8,128)S(1)}, f32[48,4096]{1,0:T(8,128)S(1)}, u32[]{:S(2)}, u32[]{:S(2)}) collective-permute-start(f32[48,4096]{1,0:T(8,128)S(1)} %bitcast.65), channel_id=1, source_target_pairs={{0,32},{32,0},{64,96},{96,64},{128,160},{160,128},{192,224},{224,1... | collective-permute-start | bytes 2359304 | tf_op jit(solution)/shard_map/ppermute | solution.py:23
  32.1 38.1 %copy-start.25 = (f32[48,4096]{1,0:T(8,128)}, f32[48,4096]{1,0:T(8,128)S(1)}, u32[]{:S(2)}) copy-start(f32[48,4096]{1,0:T(8,128)S(1)} %collective-permute-done.l_ref) | copy-start | bytes 2359300
  32.1 20.3 %collective-permute-start.4 = (f32[48,4096]{1,0:T(8,128)S(1)}, f32[48,4096]{1,0:T(8,128)}, u32[]{:S(2)}, u32[]{:S(2)}) collective-permute-start(f32[48,4096]{1,0:T(8,128)S(1)} %bitcast.66), channel_id=1, source_target_pairs={{0,64},{32,96},{64,128},{96,160},{128,192},{160,224},{192,0},{224,... | collective-permute-start | bytes 2359304 | tf_op jit(solution)/shard_map/ppermute | solution.py:18
  44.6 9.3 %collective-permute-start.11 = (f32[48,4096]{1,0:T(8,128)S(1)}, f32[48,4096]{1,0:T(8,128)S(1)}, u32[]{:S(2)}, u32[]{:S(2)}) collective-permute-start(f32[48,4096]{1,0:T(8,128)S(1)} %collective-permute-done.5.rest_8_.rest_6_.rest_7_), channel_id=1, source_target_pairs={{0,32},{32,0},{64,96},{96,64},{128,160},{160,128},{192,224},{224,1... | collective-permute-start | bytes 2359304 | tf_op jit(solution)/shard_map/ppermute | solution.py:23
  46.2 24.1 %copy-start.26 = (f32[48,4096]{1,0:T(8,128)}, f32[48,4096]{1,0:T(8,128)S(1)}, u32[]{:S(2)}) copy-start(f32[48,4096]{1,0:T(8,128)S(1)} %collective-permute-done.12.l_ref) | copy-start | bytes 2359300
  46.2 23.1 %collective-permute-start.14 = (f32[48,4096]{1,0:T(8,128)}, f32[48,4096]{1,0:T(8,128)}, u32[]{:S(2)}, u32[]{:S(2)}) collective-permute-start(f32[48,4096]{1,0:T(8,128)} %collective-permute-done.2.rest_5_.rest_3_.rest_4_), channel_id=1, source_target_pairs={{0,64},{32,96},{64,128},{96,160},{128,192},{160,224},{192,0},{224,... | collective-permute-start | bytes 2359304 | tf_op jit(solution)/shard_map/ppermute | solution.py:18
  46.2 24.0 %collective-permute-start.15 = (f32[48,4096]{1,0:T(8,128)}, f32[48,4096]{1,0:T(8,128)}, u32[]{:S(2)}, u32[]{:S(2)}) collective-permute-start(f32[48,4096]{1,0:T(8,128)} %collective-permute-done.3.rest_6_.rest_4_.rest_5_), channel_id=1, source_target_pairs={{0,192},{32,224},{64,0},{96,32},{128,64},{160,96},{192,128},{224,1... | collective-permute-start | bytes 2359304 | tf_op jit(solution)/shard_map/ppermute | solution.py:18
  49.7 4.2 %copy-start.10 = (f32[48,4096]{1,0:T(8,128)}, f32[48,4096]{1,0:T(8,128)S(1)}, u32[]{:S(2)}) copy-start(f32[48,4096]{1,0:T(8,128)S(1)} %collective-permute-done.7.rest_10_.rest_8_.rest_9_) | copy-start | bytes 2359300
  49.8 33.0 %collective-permute-start.8 = (f32[48,4096]{1,0:T(8,128)}, f32[48,4096]{1,0:T(8,128)}, u32[]{:S(2)}, u32[]{:S(2)}) collective-permute-start(f32[48,4096]{1,0:T(8,128)} %collective-permute-done.2.rest_5_.rest_3_.rest_4_), channel_id=1, source_target_pairs={{0,32},{32,0},{64,96},{96,64},{128,160},{160,128},{192,224},{224,1... | collective-permute-start | bytes 2359304 | tf_op jit(solution)/shard_map/ppermute | solution.py:23
  52.4 30.3 %collective-permute-start.10 = (f32[48,4096]{1,0:T(8,128)}, f32[48,4096]{1,0:T(8,128)}, u32[]{:S(2)}, u32[]{:S(2)}) collective-permute-start(f32[48,4096]{1,0:T(8,128)} %collective-permute-done.4.rest_7_.rest_5_.rest_6_), channel_id=1, source_target_pairs={{0,32},{32,0},{64,96},{96,64},{128,160},{160,128},{192,224},{224,1... | collective-permute-start | bytes 2359304 | tf_op jit(solution)/shard_map/ppermute | solution.py:23
  53.9 28.8 %collective-permute-start.9 = (f32[48,4096]{1,0:T(8,128)}, f32[48,4096]{1,0:T(8,128)}, u32[]{:S(2)}, u32[]{:S(2)}) collective-permute-start(f32[48,4096]{1,0:T(8,128)} %collective-permute-done.3.rest_6_.rest_4_.rest_5_), channel_id=1, source_target_pairs={{0,32},{32,0},{64,96},{96,64},{128,160},{160,128},{192,224},{224,1... | collective-permute-start | bytes 2359304 | tf_op jit(solution)/shard_map/ppermute | solution.py:23
  69.3 28.3 %collective-permute-start.16 = (f32[48,4096]{1,0:T(8,128)}, f32[48,4096]{1,0:T(8,128)}, u32[]{:S(2)}, u32[]{:S(2)}) collective-permute-start(f32[48,4096]{1,0:T(8,128)} %collective-permute-done.14.rest_4_.rest_14_), channel_id=1, source_target_pairs={{0,32},{32,0},{64,96},{96,64},{128,160},{160,128},{192,224},{224,1... | collective-permute-start | bytes 2359304 | tf_op jit(solution)/shard_map/ppermute | solution.py:23
  70.2 27.3 %collective-permute-start.17 = (f32[48,4096]{1,0:T(8,128)}, f32[48,4096]{1,0:T(8,128)}, u32[]{:S(2)}, u32[]{:S(2)}) collective-permute-start(f32[48,4096]{1,0:T(8,128)} %collective-permute-done.15.rest_5_.rest_15_), channel_id=1, source_target_pairs={{0,32},{32,0},{64,96},{96,64},{128,160},{160,128},{192,224},{224,1... | collective-permute-start | bytes 2359304 | tf_op jit(solution)/shard_map/ppermute | solution.py:23
  89.6 8.0 %copy-start.1 = (f32[6,8,32,128]{3,1,2,0:T(8,128)S(1)}, f32[6,8,32,128]{3,1,2,0:T(8,128)}, u32[]{:S(2)}) copy-start(f32[6,8,32,128]{3,1,2,0:T(8,128)} %copy-done) | copy-start | bytes 2359300
  89.6 8.0 %copy-start.3 = (f32[6,8,32,128]{3,1,2,0:T(8,128)S(1)}, f32[6,8,32,128]{3,1,2,0:T(8,128)}, u32[]{:S(2)}) copy-start(f32[6,8,32,128]{3,1,2,0:T(8,128)} %copy-done.2) | copy-start | bytes 2359300
  89.6 8.0 %copy-start.4 = (f32[48,4096]{1,0:T(8,128)S(1)}, f32[48,4096]{1,0:T(8,128)}, u32[]{:S(2)}) copy-start(f32[48,4096]{1,0:T(8,128)} %hamiltonian.3.rest_0_.rest_3_.rest_1_.rest_19_) | copy-start | bytes 2359300
  89.6 8.0 %copy-start.5 = (f32[48,4096]{1,0:T(8,128)S(1)}, f32[48,4096]{1,0:T(8,128)}, u32[]{:S(2)}) copy-start(f32[48,4096]{1,0:T(8,128)} %hamiltonian.2.rest_2_.rest_0_.rest_18_) | copy-start | bytes 2359300
  97.5 4.3 %copy-start.21 = (f32[144,576]{1,0:T(8,128)S(1)}, f32[144,576]{1,0:T(8,128)}, u32[]{:S(2)}) copy-start(f32[144,576]{1,0:T(8,128)} %gram.3) | copy-start | bytes 995332
  97.5 4.3 %copy-start.28 = (f32[48,576]{1,0:T(8,128)S(1)}, f32[48,576]{1,0:T(8,128)}, u32[]{:S(2)}) copy-start(f32[48,576]{1,0:T(8,128)} %gram.4) | copy-start | bytes 331780
  102.0 9.8 %copy-start.20 = (f32[192,768]{1,0:T(8,128)}, f32[192,768]{1,0:T(8,128)S(1)}, u32[]{:S(2)}) copy-start(f32[192,768]{1,0:T(8,128)S(1)} %pad_maximum_fusion) | copy-start | bytes 1769476
  102.8 12.2 %collective-permute-start.18 = (f32[2,24,768]{2,1,0:T(8,128)}, f32[2,24,768]{2,1,0:T(8,128)S(1)}, u32[]{:S(2)}, u32[]{:S(2)}) collective-permute-start(f32[2,24,768]{2,1,0:T(8,128)} %get-tuple-element.17), channel_id=1, source_target_pairs={{0,16},{1,17},{2,18},{3,19},{4,20},{5,21},{6,22},{7,23},{8,24},{9,... | collective-permute-start | bytes 442376 | tf_op jit(solution)/shard_map/ppermute | solution.py:38
  110.3 7.7 %collective-permute-start.20 = (f32[2,24,768]{2,1,0:T(8,128)}, f32[2,24,768]{2,1,0:T(8,128)S(1)}, u32[]{:S(2)}, u32[]{:S(2)}) collective-permute-start(f32[2,24,768]{2,1,0:T(8,128)} %get-tuple-element.18), channel_id=1, source_target_pairs={{0,24},{1,25},{2,26},{3,27},{4,28},{5,29},{6,30},{7,31},{8,0},{9,1... | collective-permute-start | bytes 442376 | tf_op jit(solution)/shard_map/ppermute | solution.py:38
  111.1 9.7 %collective-permute-start.19 = (f32[2,24,768]{2,1,0:T(8,128)}, f32[2,24,768]{2,1,0:T(8,128)}, u32[]{:S(2)}, u32[]{:S(2)}) collective-permute-start(f32[2,24,768]{2,1,0:T(8,128)} %get-tuple-element.19), channel_id=1, source_target_pairs={{0,8},{1,9},{2,10},{3,11},{4,12},{5,13},{6,14},{7,15},{8,16},{9,17... | collective-permute-start | bytes 442376 | tf_op jit(solution)/shard_map/ppermute | solution.py:38
  111.8 13.9 %collective-permute-start.33 = (f32[48,4096]{1,0:T(8,128)S(1)}, f32[48,4096]{1,0:T(8,128)}, u32[]{:S(2)}, u32[]{:S(2)}) collective-permute-start(f32[48,4096]{1,0:T(8,128)S(1)} %copy-done.5), channel_id=1, source_target_pairs={{0,32},{32,0},{64,96},{96,64},{128,160},{160,128},{192,224},{224,1... | collective-permute-start | bytes 2359304 | tf_op jit(solution)/shard_map/ppermute | solution.py:23
  113.1 19.2 %collective-permute-start.32 = (f32[48,4096]{1,0:T(8,128)S(1)}, f32[48,4096]{1,0:T(8,128)}, u32[]{:S(2)}, u32[]{:S(2)}) collective-permute-start(f32[48,4096]{1,0:T(8,128)S(1)} %copy-done.5), channel_id=1, source_target_pairs={{0,192},{32,224},{64,0},{96,32},{128,64},{160,96},{192,128},{224,1... | collective-permute-start | bytes 2359304 | tf_op jit(solution)/shard_map/ppermute | solution.py:18
  115.0 27.0 %collective-permute-start.29 = (f32[48,4096]{1,0:T(8,128)S(1)}, f32[48,4096]{1,0:T(8,128)}, u32[]{:S(2)}, u32[]{:S(2)}) collective-permute-start(f32[48,4096]{1,0:T(8,128)S(1)} %copy-done.5), channel_id=1, source_target_pairs={{0,64},{32,96},{64,128},{96,160},{128,192},{160,224},{192,0},{224,... | collective-permute-start | bytes 2359304 | tf_op jit(solution)/shard_map/ppermute | solution.py:18
  118.0 31.1 %collective-permute-start.30 = (f32[48,4096]{1,0:T(8,128)S(1)}, f32[48,4096]{1,0:T(8,128)}, u32[]{:S(2)}, u32[]{:S(2)}) collective-permute-start(f32[48,4096]{1,0:T(8,128)S(1)} %copy-done.4), channel_id=1, source_target_pairs={{0,192},{32,224},{64,0},{96,32},{128,64},{160,96},{192,128},{224,1... | collective-permute-start | bytes 2359304 | tf_op jit(solution)/shard_map/ppermute | solution.py:18
  121.8 3.7 %collective-permute-start.21 = (f32[24,768]{1,0:T(8,128)S(1)}, f32[24,768]{1,0:T(8,128)S(1)}, u32[]{:S(2)}, u32[]{:S(2)}) collective-permute-start(f32[24,768]{1,0:T(8,128)S(1)} %select_bitcast_fusion), channel_id=1, source_target_pairs={{0,1},{1,0},{2,3},{3,2},{4,5},{5,4},{6,7},{7,6},{8,9},{9,8},{10,11... | collective-permute-start | bytes 221192 | tf_op jit(solution)/shard_map/ppermute | solution.py:28
  125.6 8.1 %collective-permute-start.24 = (f32[24,768]{1,0:T(8,128)S(1)}, f32[24,768]{1,0:T(8,128)S(1)}, u32[]{:S(2)}, u32[]{:S(2)}) collective-permute-start(f32[24,768]{1,0:T(8,128)S(1)} %bitcast_add_fusion.1), channel_id=1, source_target_pairs={{0,6},{1,7},{2,0},{3,1},{4,2},{5,3},{6,4},{7,5},{8,14},{9,15},{10,... | collective-permute-start | bytes 221192 | tf_op jit(solution)/shard_map/ppermute | solution.py:33
  125.7 9.6 %collective-permute-start.23 = (f32[24,768]{1,0:T(8,128)S(1)}, f32[24,768]{1,0:T(8,128)S(1)}, u32[]{:S(2)}, u32[]{:S(2)}) collective-permute-start(f32[24,768]{1,0:T(8,128)S(1)} %bitcast_add_fusion.1), channel_id=1, source_target_pairs={{0,2},{1,3},{2,4},{3,5},{4,6},{5,7},{6,0},{7,1},{8,10},{9,11},{10,... | collective-permute-start | bytes 221192 | tf_op jit(solution)/shard_map/ppermute | solution.py:33
  132.3 7.9 %collective-permute-start.22 = (f32[24,768]{1,0:T(8,128)S(1)}, f32[24,768]{1,0:T(8,128)S(1)}, u32[]{:S(2)}, u32[]{:S(2)}) collective-permute-start(f32[24,768]{1,0:T(8,128)S(1)} %bitcast_add_fusion.1), channel_id=1, source_target_pairs={{0,4},{1,5},{2,6},{3,7},{4,0},{5,1},{6,2},{7,3},{8,12},{9,13},{10,... | collective-permute-start | bytes 221192 | tf_op jit(solution)/shard_map/ppermute | solution.py:33
  133.6 19.3 %collective-permute-start.34 = (f32[48,4096]{1,0:T(8,128)S(1)}, f32[48,4096]{1,0:T(8,128)S(1)}, u32[]{:S(2)}, u32[]{:S(2)}) collective-permute-start(f32[48,4096]{1,0:T(8,128)S(1)} %copy-done.4), channel_id=1, source_target_pairs={{0,32},{32,0},{64,96},{96,64},{128,160},{160,128},{192,224},{224,1... | collective-permute-start | bytes 2359304 | tf_op jit(solution)/shard_map/ppermute | solution.py:23
  135.2 20.5 %collective-permute-start.31 = (f32[48,4096]{1,0:T(8,128)S(1)}, f32[48,4096]{1,0:T(8,128)S(1)}, u32[]{:S(2)}, u32[]{:S(2)}) collective-permute-start(f32[48,4096]{1,0:T(8,128)S(1)} %copy-done.4), channel_id=1, source_target_pairs={{0,64},{32,96},{64,128},{96,160},{128,192},{160,224},{192,0},{224,... | collective-permute-start | bytes 2359304 | tf_op jit(solution)/shard_map/ppermute | solution.py:18
  140.2 16.6 %collective-permute-start.38 = (f32[48,4096]{1,0:T(8,128)}, f32[48,4096]{1,0:T(8,128)S(1)}, u32[]{:S(2)}, u32[]{:S(2)}) collective-permute-start(f32[48,4096]{1,0:T(8,128)} %collective-permute-done.32.rest_23_), channel_id=1, source_target_pairs={{0,32},{32,0},{64,96},{96,64},{128,160},{160,128},{192,224},{224,1... | collective-permute-start | bytes 2359304 | tf_op jit(solution)/shard_map/ppermute | solution.py:23
  142.0 7.2 %collective-permute-start.25 = (f32[24,768]{1,0:T(8,128)S(1)}, f32[24,768]{1,0:T(8,128)S(1)}, u32[]{:S(2)}, u32[]{:S(2)}) collective-permute-start(f32[24,768]{1,0:T(8,128)S(1)} %add_add_fusion), channel_id=1, source_target_pairs={{0,1},{1,0},{2,3},{3,2},{4,5},{5,4},{6,7},{7,6},{8,9},{9,8},{10,11... | collective-permute-start | bytes 221192 | tf_op jit(solution)/shard_map/ppermute | solution.py:28
  149.1 23.3 %collective-permute-start.39 = (f32[48,4096]{1,0:T(8,128)}, f32[48,4096]{1,0:T(8,128)}, u32[]{:S(2)}, u32[]{:S(2)}) collective-permute-start(f32[48,4096]{1,0:T(8,128)} %collective-permute-done.29.rest_20_), channel_id=1, source_target_pairs={{0,64},{32,96},{64,128},{96,160},{128,192},{160,224},{192,0},{224,... | collective-permute-start | bytes 2359304 | tf_op jit(solution)/shard_map/ppermute | solution.py:18
  149.1 24.2 %collective-permute-start.40 = (f32[48,4096]{1,0:T(8,128)}, f32[48,4096]{1,0:T(8,128)}, u32[]{:S(2)}, u32[]{:S(2)}) collective-permute-start(f32[48,4096]{1,0:T(8,128)} %collective-permute-done.30.rest_21_), channel_id=1, source_target_pairs={{0,192},{32,224},{64,0},{96,32},{128,64},{160,96},{192,128},{224,1... | collective-permute-start | bytes 2359304 | tf_op jit(solution)/shard_map/ppermute | solution.py:18
  153.8 19.6 %collective-permute-start.28 = (f32[2,24,768]{2,1,0:T(8,128)}, f32[2,24,768]{2,1,0:T(8,128)S(1)}, u32[]{:S(2)}, u32[]{:S(2)}) collective-permute-start(f32[2,24,768]{2,1,0:T(8,128)} %maximum_select_fusion.1), channel_id=1, source_target_pairs={{0,24},{1,25},{2,26},{3,27},{4,28},{5,29},{6,30},{7,31},{8,0},{9,1... | collective-permute-start | bytes 442376 | tf_op jit(solution)/shard_map/ppermute | solution.py:38
  156.7 17.2 %collective-permute-start.27 = (f32[2,24,768]{2,1,0:T(8,128)}, f32[2,24,768]{2,1,0:T(8,128)}, u32[]{:S(2)}, u32[]{:S(2)}) collective-permute-start(f32[2,24,768]{2,1,0:T(8,128)} %maximum_select_fusion.1), channel_id=1, source_target_pairs={{0,8},{1,9},{2,10},{3,11},{4,12},{5,13},{6,14},{7,15},{8,16},{9,17... | collective-permute-start | bytes 442376 | tf_op jit(solution)/shard_map/ppermute | solution.py:38
  157.6 16.4 %collective-permute-start.26 = (f32[2,24,768]{2,1,0:T(8,128)}, f32[2,24,768]{2,1,0:T(8,128)}, u32[]{:S(2)}, u32[]{:S(2)}) collective-permute-start(f32[2,24,768]{2,1,0:T(8,128)} %maximum_select_fusion.1), channel_id=1, source_target_pairs={{0,16},{1,17},{2,18},{3,19},{4,20},{5,21},{6,22},{7,23},{8,24},{9,... | collective-permute-start | bytes 442376 | tf_op jit(solution)/shard_map/ppermute | solution.py:38
  160.4 20.5 %copy-start.7 = (f32[48,4096]{1,0:T(8,128)S(1)}, f32[48,4096]{1,0:T(8,128)}, u32[]{:S(2)}) copy-start(f32[48,4096]{1,0:T(8,128)} %copy-done.6) | copy-start | bytes 2359300
  160.4 20.5 %copy-start.9 = (f32[48,4096]{1,0:T(8,128)S(1)}, f32[48,4096]{1,0:T(8,128)}, u32[]{:S(2)}) copy-start(f32[48,4096]{1,0:T(8,128)} %copy-done.8) | copy-start | bytes 2359300
  172.4 3.9 %collective-permute-start.35 = (f32[48,4096]{1,0:T(8,128)}, f32[48,4096]{1,0:T(8,128)S(1)}, u32[]{:S(2)}, u32[]{:S(2)}) collective-permute-start(f32[48,4096]{1,0:T(8,128)} %collective-permute-done.29.rest_20_), channel_id=1, source_target_pairs={{0,32},{32,0},{64,96},{96,64},{128,160},{160,128},{192,224},{224,1... | collective-permute-start | bytes 2359304 | tf_op jit(solution)/shard_map/ppermute | solution.py:23
  173.4 4.4 %collective-permute-start.36 = (f32[48,4096]{1,0:T(8,128)}, f32[48,4096]{1,0:T(8,128)S(1)}, u32[]{:S(2)}, u32[]{:S(2)}) collective-permute-start(f32[48,4096]{1,0:T(8,128)} %collective-permute-done.30.rest_21_), channel_id=1, source_target_pairs={{0,32},{32,0},{64,96},{96,64},{128,160},{160,128},{192,224},{224,1... | collective-permute-start | bytes 2359304 | tf_op jit(solution)/shard_map/ppermute | solution.py:23
  173.4 4.4 %collective-permute-start.37 = (f32[48,4096]{1,0:T(8,128)}, f32[48,4096]{1,0:T(8,128)S(1)}, u32[]{:S(2)}, u32[]{:S(2)}) collective-permute-start(f32[48,4096]{1,0:T(8,128)} %copy-done.16), channel_id=1, source_target_pairs={{0,32},{32,0},{64,96},{96,64},{128,160},{160,128},{192,224},{224,1... | collective-permute-start | bytes 2359304 | tf_op jit(solution)/shard_map/ppermute | solution.py:23
  173.9 5.0 %collective-permute-start.41 = (f32[48,4096]{1,0:T(8,128)}, f32[48,4096]{1,0:T(8,128)S(1)}, u32[]{:S(2)}, u32[]{:S(2)}) collective-permute-start(f32[48,4096]{1,0:T(8,128)} %collective-permute-done.39.rest_30_), channel_id=1, source_target_pairs={{0,32},{32,0},{64,96},{96,64},{128,160},{160,128},{192,224},{224,1... | collective-permute-start | bytes 2359304 | tf_op jit(solution)/shard_map/ppermute | solution.py:23
  174.0 6.0 %collective-permute-start.42 = (f32[48,4096]{1,0:T(8,128)}, f32[48,4096]{1,0:T(8,128)S(1)}, u32[]{:S(2)}, u32[]{:S(2)}) collective-permute-start(f32[48,4096]{1,0:T(8,128)} %collective-permute-done.40.rest_31_), channel_id=1, source_target_pairs={{0,32},{32,0},{64,96},{96,64},{128,160},{160,128},{192,224},{224,1... | collective-permute-start | bytes 2359304 | tf_op jit(solution)/shard_map/ppermute | solution.py:23
  180.9 1.1 copy-start.11
  182.1 1.1 copy-start.13
  183.2 1.1 copy-start.15
  197.3 22.9 %all-to-all-start = ((f32[256,1,128]{2,1,0:T(1,128)}), f32[256,1,128]{2,1,0:T(1,128)S(1)}, u32[]{:S(2)}, u32[]{:S(2)}) async-start(f32[256,1,128]{2,1,0:T(1,128)} %bitcast.17), calls=%async_computation | async-start | bytes 262144 | tf_op jit(solution)/shard_map/all_to_all | solution.py:311
  (9 other events, 8.5 us)

commit v4 on v3

--- a/solution.py
+++ b/solution.py
@@ -8,7 +8,6 @@
 coeffs = (-205.0 / 72.0, 8.0 / 5.0, -1.0 / 5.0, 8.0 / 315.0, -1.0 / 560.0)
 step_length = 0.05
 GRAM_VMEM = 56 * 1024 * 1024
-FAR_VMEM = 24 * 1024 * 1024
 GRADIENT_VMEM = 32 * 1024 * 1024
 ZS = 8
 
@@ -118,7 +117,7 @@
         at += ref.shape[0]
 
 
-def gram(own_blocks, blocks, grant):
+def gram(own_blocks, blocks):
     cells = blocks[0].shape[1]
     count = len(own_blocks)
     rows = sum(b.shape[0] for b in own_blocks)
@@ -151,7 +150,7 @@
             pltpu.VMEM((total, chunk), jnp.bfloat16),
             pltpu.VMEM((2 * rows, chunk), jnp.bfloat16),
         ],
-        compiler_params=pltpu.CompilerParams(vmem_limit_bytes=grant),
+        compiler_params=pltpu.CompilerParams(vmem_limit_bytes=GRAM_VMEM),
         cost_estimate=pl.CostEstimate(
             flops=6 * rows * total * cells, bytes_accessed=4 * cells * (rows + total), transcendentals=0
         ),
@@ -300,10 +299,7 @@
         image.append(apply_hamiltonian(c[index], left, right, potential.reshape(1, -1)))
     near_image = gather_near(*image)
     far_image = gather_far(near_image)
-    part_a = gram(c + image[:1], near, GRAM_VMEM)
-    part_b = gram(image[1:], near, GRAM_VMEM)
-    part_far = gram(c + image, far, FAR_VMEM)
-    part = jnp.concatenate([jnp.concatenate([part_a, part_b], axis=0), part_far], axis=1)
+    part = gram(c + image, near + far)
     overlap = sum_over_slabs(part)
     grad, sums = gradient_of(
         overlap, near + far, near_image + far_image, image, prev, slabs * c[0].shape[1]

time: 226 us -> 210 us (0.929)
  waiting for transfers between devices: 86.7 us -> 75.9 us
  Pallas kernels: 42.2 us -> 32.5 us
  starting transfers between devices: 70.7 us -> 75.5 us
    ppermute x2, waiting for transfers between devices: 12.6 us -> 0.19 us  [on_device(): lax.ppermute(c[index], 'dom', [(i + 1, i) for i in range(slabs - 1)])]
    pallas_call x3 -> x1, Pallas kernels: 18.9 us -> 9.47 us  [gram(): pl.pallas_call(kernel, out_shape=jax.ShapeDtypeStruct((rows, total), jnp....]
    ppermute x3, starting transfers between devices: 3.77 us -> 12.9 us  [shift_z(): lax.ppermute(v, 'dom', [(i, i // ZS * ZS + (i + k) % ZS) for i in range(n)])]
    ppermute x12, waiting for transfers between devices: 48.7 us -> 56.9 us  [shift_orb(): return lax.ppermute(v, 'orb', [(i, (i + k) % n) for i in range(n)])]
    ppermute x6, starting transfers between devices: 13.8 us -> 9.02 us  [shift_y(): return lax.ppermute(v, 'dom', [(i, (i + k * ZS) % n) for i in range(n)])]
    ppermute x3, waiting for transfers between devices: 4.94 us -> 0.25 us  [shift_z(): lax.ppermute(v, 'dom', [(i, i // ZS * ZS + (i + k) % ZS) for i in range(n)])]
    ppermute x12, starting transfers between devices: 16.3 us -> 12.9 us  [shift_orb(): return lax.ppermute(v, 'orb', [(i, (i + k) % n) for i in range(n)])]
    ppermute x2, starting transfers between devices: 0.19 us -> 3.15 us  [flip_z(): return lax.ppermute(v, 'dom', [(i, i ^ 1) for i in range(n)])]
  transfers between devices with their start and end apart: 44 -> 44, of which waited for: 15 -> 17; matrix products, arithmetic and copies ran while one was open for 5% -> 4% of each run, Pallas kernels for 10% -> 4%
where the time goes in v4:
time: 210 us; the launch traced here: 209 us
  waiting for transfers between devices  75.9 us (36%)
  starting transfers between devices  75.5 us (36%)
  Pallas kernels  32.5 us (15%)
  local copies, waits for them, and re-layouts  22.3 us (11%)
    ppermute x12, waiting for transfers between devices, shift_orb(): return lax.ppermute(v, 'orb', [(i, (i + k) % n) for i in range(n)])  56.9 us
    ppermute x16, starting transfers between devices, swap_core(): return lax.ppermute(v, 'orb', [(i, i ^ 1) for i in range(n)])  19.7 us
    unnamed x60, local copies, waits for them, and re-layouts  17.9 us
    ppermute x12, starting transfers between devices, shift_orb(): return lax.ppermute(v, 'orb', [(i, (i + k) % n) for i in range(n)])  12.9 us
    ppermute x3, starting transfers between devices, shift_z(): lax.ppermute(v, 'dom', [(i, i // ZS * ZS + (i + k) % ZS) for i in range(n)])  12.9 us
    pallas_call x1, Pallas kernels, gradient_of(): pl.pallas_call(kernel, out_shape=(jax.ShapeDtypeStruct((own, cells), jnp....  10.7 us
    all_to_all x1, waiting for transfers between devices, on_device(): lax.all_to_all(sums, ('orb', 'dom'), split_axis=0, concat_axis=0, tiled=T...  10.2 us
    pallas_call x1, Pallas kernels, gram(): pl.pallas_call(kernel, out_shape=jax.ShapeDtypeStruct((rows, total), jnp....  9.47 us
  transfers between devices with their start and end apart: 44, of which 17 were waited for; matrix products, arithmetic and copies ran while one was open for 4% of the time, Pallas kernels for 4%

profile of v4, /device:TPU:1, one launch (start us, length us, event | category | flops | bytes accessed | tf_op | source)
XLA Modules:
  0.0 209.0 jit_solution(3042640036198564735)
XLA Ops:
  0.6 1.5 fusion.3
  2.6 3.3 %collective-permute-start.8 = (f32[48,4096]{1,0:T(8,128)S(1)}, f32[48,4096]{1,0:T(8,128)S(1)}, u32[]{:S(2)}, u32[]{:S(2)}) collective-permute-start(f32[48,4096]{1,0:T(8,128)S(1)} %bitcast.51), channel_id=1, source_target_pairs={{0,32},{32,0},{64,96},{96,64},{128,160},{160,128},{192,224},{224,1... | collective-permute-start | bytes 2359304 | tf_op jit(solution)/shard_map/ppermute | solution.py:22
  7.4 1.3 collective-permute-start.1
  8.7 4.0 %collective-permute-start = (f32[48,4096]{1,0:T(8,128)S(1)}, f32[48,4096]{1,0:T(8,128)S(1)}, u32[]{:S(2)}, u32[]{:S(2)}) collective-permute-start(f32[48,4096]{1,0:T(8,128)S(1)} %bitcast.55), channel_id=1, source_target_pairs={{0,1},{1,2},{2,3},{3,4},{4,5},{5,6},{6,7},{7,8},{8,9},{9,10},{10,1... | collective-permute-start | bytes 2359304 | tf_op jit(solution)/shard_map/ppermute | solution.py:295
  13.2 1.3 collective-permute-start.9
  14.5 10.5 %collective-permute-done.7.rest_9_.rest_7_ = f32[48,4096]{1,0:T(8,128)S(1)} collective-permute-done((f32[48,4096]{1,0:T(8,128)S(1)}, f32[48,4096]{1,0:T(8,128)S(1)}, u32[]{:S(2)}, u32[]{:S(2)}) %collective-permute-start.7) | collective-permute-done | bytes 786464 | tf_op jit(solution)/shard_map/ppermute | solution.py:17
  25.0 1.7 collective-permute-done.4.rest_6_.rest_4_
  26.7 1.0 collective-permute-start.5
  27.7 1.3 collective-permute-start.3
  29.0 4.2 %collective-permute-start.2 = (f32[48,4096]{1,0:T(8,128)S(1)}, f32[48,4096]{1,0:T(8,128)S(1)}, u32[]{:S(2)}, u32[]{:S(2)}) collective-permute-start(f32[48,4096]{1,0:T(8,128)S(1)} %bitcast.64), channel_id=1, source_target_pairs={{0,1},{1,2},{2,3},{3,4},{4,5},{5,6},{6,7},{7,8},{8,9},{9,10},{10,1... | collective-permute-start | bytes 2359304 | tf_op jit(solution)/shard_map/ppermute | solution.py:295
  33.2 2.0 collective-permute-start.13
  35.2 9.4 %collective-permute-done.6.rest_8_.rest_6_ = f32[48,4096]{1,0:T(8,128)} collective-permute-done((f32[48,4096]{1,0:T(8,128)S(1)}, f32[48,4096]{1,0:T(8,128)}, u32[]{:S(2)}, u32[]{:S(2)}) %collective-permute-start.6) | collective-permute-done | bytes 786464 | tf_op jit(solution)/shard_map/ppermute | solution.py:17
  44.7 2.6 %collective-permute-start.15 = (f32[48,4096]{1,0:T(8,128)}, f32[48,4096]{1,0:T(8,128)}, u32[]{:S(2)}, u32[]{:S(2)}) collective-permute-start(f32[48,4096]{1,0:T(8,128)} %collective-permute-done.5.rest_7_.rest_5_), channel_id=1, source_target_pairs={{0,192},{32,224},{64,0},{96,32},{128,64},{160,96},{192,128},{224,1... | collective-permute-start | bytes 2359304 | tf_op jit(solution)/shard_map/ppermute | solution.py:17
  47.5 2.2 %collective-permute-start.10 = (f32[48,4096]{1,0:T(8,128)}, f32[48,4096]{1,0:T(8,128)}, u32[]{:S(2)}, u32[]{:S(2)}) collective-permute-start(f32[48,4096]{1,0:T(8,128)} %collective-permute-done.4.rest_6_.rest_4_), channel_id=1, source_target_pairs={{0,32},{32,0},{64,96},{96,64},{128,160},{160,128},{192,224},{224,1... | collective-permute-start | bytes 2359304 | tf_op jit(solution)/shard_map/ppermute | solution.py:22
  49.7 1.2 collective-permute-start.11
  51.0 0.8 copy-done.12
  51.8 11.7 %collective-permute-done.14.rest_16_.rest_14_ = f32[48,4096]{1,0:T(8,128)} collective-permute-done((f32[48,4096]{1,0:T(8,128)}, f32[48,4096]{1,0:T(8,128)}, u32[]{:S(2)}, u32[]{:S(2)}) %collective-permute-start.14) | collective-permute-done | bytes 786464 | tf_op jit(solution)/shard_map/ppermute | solution.py:17
  63.5 2.6 %collective-permute-start.16 = (f32[48,4096]{1,0:T(8,128)}, f32[48,4096]{1,0:T(8,128)}, u32[]{:S(2)}, u32[]{:S(2)}) collective-permute-start(f32[48,4096]{1,0:T(8,128)} %collective-permute-done.14.rest_16_.rest_14_), channel_id=1, source_target_pairs={{0,32},{32,0},{64,96},{96,64},{128,160},{160,128},{192,224},{224,1... | collective-permute-start | bytes 2359304 | tf_op jit(solution)/shard_map/ppermute | solution.py:22
  66.4 2.2 %copy.15 = f32[12,8,32,128]{3,1,2,0:T(8,128)} copy(f32[12,8,32,128]{3,2,1,0:T(8,128)S(1)} %bitcast.77) | data formatting | bytes 3145728
  68.7 4.2 %hamiltonian.2.rest_2_.rest_0_.rest_18_ = f32[48,4096]{1,0:T(8,128)} custom-call(f32[48,4096]{1,0:T(8,128)} %bitcast.56, f32[48,4096]{1,0:T(8,128)} %copy-done.24, f32[48,4096]{1,0:T(8,128)} %copy-done.23, f32[1,4096]{1,0:T(1,128)} %bitcast.84), custom_call_target="tpu_custom_call" | custom-call | flops 7864320 | bytes 3145728 | tf_op jit(solution)/shard_map/hamiltonian/pallas_call | solution.py:91
  72.9 4.1 %hamiltonian.3.rest_3_.rest_1_.rest_19_ = f32[48,4096]{1,0:T(8,128)} custom-call(f32[48,4096]{1,0:T(8,128)} %bitcast.65, f32[48,4096]{1,0:T(8,128)} %copy-done.26, f32[48,4096]{1,0:T(8,128)} %copy-done.25, f32[1,4096]{1,0:T(1,128)} %bitcast.85), custom_call_target="tpu_custom_call" | custom-call | flops 7864320 | bytes 3145728 | tf_op jit(solution)/shard_map/hamiltonian/pallas_call | solution.py:91
  77.0 9.5 %gram.1 = f32[192,768]{1,0:T(8,128)} custom-call(f32[48,4096]{1,0:T(8,128)} %bitcast.57, f32[48,4096]{1,0:T(8,128)} %bitcast.66, f32[48,4096]{1,0:T(8,128)} %hamiltonian.2.rest_2_.rest_0_.rest_18_, f32[48,4096]{1,0:T(8,128)} %hamiltonian.3.rest_3_.rest_1_.rest_19_, f32[48,4096]{1,0:T(8,128)} %bitcast.58, f32[48,4096]{1,0:T(8,128)} %bitcast.67, ...), custom_call_target="tpu_custom_call" | custom-call | flops 3623878656 | bytes 15728640 | tf_op jit(solution)/shard_map/gram/pallas_call | solution.py:142
  86.5 1.1 dynamic-slice_bitcast_fusion.2
  87.6 2.4 %collective-permute-start.18 = (f32[2,24,768]{2,1,0:T(8,128)S(1)}, f32[2,24,768]{2,1,0:T(8,128)S(1)}, u32[]{:S(2)}, u32[]{:S(2)}) collective-permute-start(f32[2,24,768]{2,1,0:T(8,128)S(1)} %get-tuple-element.17), channel_id=1, source_target_pairs={{0,16},{1,17},{2,18},{3,19},{4,20},{5,21},{6,22},{7,23},{8,24},{9,... | collective-permute-start | bytes 442376 | tf_op jit(solution)/shard_map/ppermute | solution.py:37
  90.0 0.8 collective-permute-start.20
  91.5 1.3 collective-permute-start.33
  92.8 1.9 collective-permute-start.32
  94.7 2.5 %collective-permute-done.20 = f32[2,24,768]{2,1,0:T(8,128)S(1)} collective-permute-done((f32[2,24,768]{2,1,0:T(8,128)S(1)}, f32[2,24,768]{2,1,0:T(8,128)S(1)}, u32[]{:S(2)}, u32[]{:S(2)}) %collective-permute-start.20) | collective-permute-done | bytes 147488 | tf_op jit(solution)/shard_map/ppermute | solution.py:37
  97.2 2.8 %collective-permute-start.30 = (f32[48,4096]{1,0:T(8,128)S(1)}, f32[48,4096]{1,0:T(8,128)}, u32[]{:S(2)}, u32[]{:S(2)}) collective-permute-start(f32[48,4096]{1,0:T(8,128)S(1)} %copy-done.5), channel_id=1, source_target_pairs={{0,192},{32,224},{64,0},{96,32},{128,64},{160,96},{192,128},{224,1... | collective-permute-start | bytes 2359304 | tf_op jit(solution)/shard_map/ppermute | solution.py:17
  100.0 0.9 fusion.2
  101.0 1.6 collective-permute-start.21
  102.6 2.1 %collective-permute-done.21 = f32[24,768]{1,0:T(8,128)S(1)} collective-permute-done((f32[24,768]{1,0:T(8,128)S(1)}, f32[24,768]{1,0:T(8,128)S(1)}, u32[]{:S(2)}, u32[]{:S(2)}) %collective-permute-start.21) | collective-permute-done | bytes 73760 | tf_op jit(solution)/shard_map/ppermute | solution.py:27
  104.7 6.0 %collective-permute-start.24 = (f32[24,768]{1,0:T(8,128)S(1)}, f32[24,768]{1,0:T(8,128)S(1)}, u32[]{:S(2)}, u32[]{:S(2)}) collective-permute-start(f32[24,768]{1,0:T(8,128)S(1)} %bitcast_add_fusion.1), channel_id=1, source_target_pairs={{0,6},{1,7},{2,0},{3,1},{4,2},{5,3},{6,4},{7,5},{8,14},{9,15},{10,... | collective-permute-start | bytes 221192 | tf_op jit(solution)/shard_map/ppermute | solution.py:32
  110.7 1.2 collective-permute-done.32.rest_23_
  112.0 6.9 %collective-permute-start.22 = (f32[24,768]{1,0:T(8,128)S(1)}, f32[24,768]{1,0:T(8,128)S(1)}, u32[]{:S(2)}, u32[]{:S(2)}) collective-permute-start(f32[24,768]{1,0:T(8,128)S(1)} %bitcast_add_fusion.1), channel_id=1, source_target_pairs={{0,4},{1,5},{2,6},{3,7},{4,0},{5,1},{6,2},{7,3},{8,12},{9,13},{10,... | collective-permute-start | bytes 221192 | tf_op jit(solution)/shard_map/ppermute | solution.py:32
  118.9 1.6 collective-permute-start.34
  120.7 2.2 %collective-permute-start.38 = (f32[48,4096]{1,0:T(8,128)}, f32[48,4096]{1,0:T(8,128)S(1)}, u32[]{:S(2)}, u32[]{:S(2)}) collective-permute-start(f32[48,4096]{1,0:T(8,128)} %collective-permute-done.32.rest_23_), channel_id=1, source_target_pairs={{0,32},{32,0},{64,96},{96,64},{128,160},{160,128},{192,224},{224,1... | collective-permute-start | bytes 2359304 | tf_op jit(solution)/shard_map/ppermute | solution.py:22
  122.9 1.5 collective-permute-start.25
  124.5 4.4 %collective-permute-done.30.rest_21_ = f32[48,4096]{1,0:T(8,128)} collective-permute-done((f32[48,4096]{1,0:T(8,128)S(1)}, f32[48,4096]{1,0:T(8,128)}, u32[]{:S(2)}, u32[]{:S(2)}) %collective-permute-start.30) | collective-permute-done | bytes 786464 | tf_op jit(solution)/shard_map/ppermute | solution.py:17
  128.8 3.1 %collective-permute-start.40 = (f32[48,4096]{1,0:T(8,128)}, f32[48,4096]{1,0:T(8,128)}, u32[]{:S(2)}, u32[]{:S(2)}) collective-permute-start(f32[48,4096]{1,0:T(8,128)} %collective-permute-done.30.rest_21_), channel_id=1, source_target_pairs={{0,192},{32,224},{64,0},{96,32},{128,64},{160,96},{192,128},{224,1... | collective-permute-start | bytes 2359304 | tf_op jit(solution)/shard_map/ppermute | solution.py:17
  132.6 0.9 copy-done.14
  133.5 2.0 collective-permute-start.28
  135.5 5.9 %collective-permute-done.31.rest_22_ = f32[48,4096]{1,0:T(8,128)S(1)} collective-permute-done((f32[48,4096]{1,0:T(8,128)S(1)}, f32[48,4096]{1,0:T(8,128)S(1)}, u32[]{:S(2)}, u32[]{:S(2)}) %collective-permute-start.31) | collective-permute-done | bytes 786464 | tf_op jit(solution)/shard_map/ppermute | solution.py:17
  141.5 0.9 copy-done.16
  142.7 0.9 copy-done.18
  143.6 2.8 %collective-permute-start.26 = (f32[2,24,768]{2,1,0:T(8,128)}, f32[2,24,768]{2,1,0:T(8,128)}, u32[]{:S(2)}, u32[]{:S(2)}) collective-permute-start(f32[2,24,768]{2,1,0:T(8,128)} %maximum_select_fusion.1), channel_id=1, source_target_pairs={{0,16},{1,17},{2,18},{3,19},{4,20},{5,21},{6,22},{7,23},{8,24},{9,... | collective-permute-start | bytes 442376 | tf_op jit(solution)/shard_map/ppermute | solution.py:37
  146.4 12.0 %collective-permute-done.39.rest_30_ = f32[48,4096]{1,0:T(8,128)} collective-permute-done((f32[48,4096]{1,0:T(8,128)}, f32[48,4096]{1,0:T(8,128)}, u32[]{:S(2)}, u32[]{:S(2)}) %collective-permute-start.39) | collective-permute-done | bytes 786464 | tf_op jit(solution)/shard_map/ppermute | solution.py:17
  160.2 0.9 bitcast_dynamic-update-slice_fusion.2
  161.1 0.9 bitcast_dynamic-update-slice_fusion.1
  162.1 1.4 collective-permute-done.37.rest_28_
  163.5 1.1 collective-permute-done.41.rest_32_
  164.6 1.1 collective-permute-done.42.rest_33_
  165.7 0.9 copy-done.22
  166.6 1.1 copy-done.9
  167.8 1.1 copy-done.11
  168.9 1.1 copy-done.13
  170.0 1.1 copy-done.15
  171.2 1.1 copy-done.17
  172.3 1.1 copy-done.19
  173.4 10.7 %gradient.1 = (f32[96,4096]{1,0:T(8,128)}, f32[256,128]{1,0:T(8,128)}) custom-call(f32[192,768]{1,0:T(8,128)S(1)} %bitcast.69, f32[96,4096]{1,0:T(8,128)} %bitcast.70, f32[48,4096]{1,0:T(8,128)S(1)} %copy-done.4, f32[48,4096]{1,0:T(8,128)S(1)} %copy-done.5, f32[48,4096]{1,0:T(8,128)S(1)} %bitcast.59, f32[48,4096]{1,0:T(8,128)S(1)} %bitcast.68, ...), custom_call_target="tpu_custom_call" | custom-call | flops 3623878656 | bytes 25165824 | tf_op jit(solution)/shard_map/gradient/pallas_call | solution.py:239
  184.1 7.1 %all-to-all-start = ((f32[256,1,128]{2,1,0:T(1,128)}), f32[256,1,128]{2,1,0:T(1,128)S(1)}, u32[]{:S(2)}, u32[]{:S(2)}) async-start(f32[256,1,128]{2,1,0:T(1,128)} %bitcast.17), calls=%async_computation | async-start | bytes 262144 | tf_op jit(solution)/shard_map/all_to_all | solution.py:307
  191.2 2.8 %copy.11 = f32[12,8,32,128]{3,2,1,0:T(8,128)} copy(f32[12,8,32,128]{3,1,2,0:T(8,128)} %bitcast.78) | data formatting | bytes 3145728
  194.0 10.2 %all-to-all-done = f32[256,1,128]{2,1,0:T(1,128)S(1)} async-done(((f32[256,1,128]{2,1,0:T(1,128)}), f32[256,1,128]{2,1,0:T(1,128)S(1)}, u32[]{:S(2)}, u32[]{:S(2)}) %all-to-all-start) | async-done | bytes 131104 | tf_op jit(solution)/shard_map/all_to_all | solution.py:307
  204.9 4.1 %advance.1 = (f32[96,4,8,128]{3,2,1,0:T(8,128)}, f32[96,4,8,128]{3,2,1,0:T(8,128)}) custom-call(f32[256,128]{1,0:T(8,128)} %bitcast.81, f32[96,4,8,128]{3,2,1,0:T(8,128)} %c_ref.1, f32[96,4,8,128]{3,2,1,0:T(8,128)} %d_ref.1, f32[96,4,8,128]{3,2,1,0:T(8,128)} %bitcast.71), custom_call_target="tpu_custom_call" | custom-call | flops 1572864 | bytes 7864320 | tf_op jit(solution)/shard_map/advance/pallas_call | solution.py:275
  (101 shorter events, 7.7 us)
Async XLA Ops:
  2.1 64.3 %copy-start.20 = (f32[96,4,8,128]{3,2,1,0:T(8,128)S(1)}, f32[96,4,8,128]{3,2,1,0:T(8,128)}, u32[]{:S(2)}) copy-start(f32[96,4,8,128]{3,2,1,0:T(8,128)} %param.6) | copy-start | bytes 4718596
  2.6 66.1 %copy-start = (f32[6,8,32,128]{3,1,2,0:T(8,128)}, f32[6,8,32,128]{3,1,2,0:T(8,128)S(1)}, u32[]{:S(2)}) copy-start(f32[6,8,32,128]{3,1,2,0:T(8,128)S(1)} %copy.17) | copy-start | bytes 2359300
  2.6 10.6 %collective-permute-start.8 = (f32[48,4096]{1,0:T(8,128)S(1)}, f32[48,4096]{1,0:T(8,128)S(1)}, u32[]{:S(2)}, u32[]{:S(2)}) collective-permute-start(f32[48,4096]{1,0:T(8,128)S(1)} %bitcast.51), channel_id=1, source_target_pairs={{0,32},{32,0},{64,96},{96,64},{128,160},{160,128},{192,224},{224,1... | collective-permute-start | bytes 2359304 | tf_op jit(solution)/shard_map/ppermute | solution.py:22
  5.9 19.1 %collective-permute-start.7 = (f32[48,4096]{1,0:T(8,128)S(1)}, f32[48,4096]{1,0:T(8,128)S(1)}, u32[]{:S(2)}, u32[]{:S(2)}) collective-permute-start(f32[48,4096]{1,0:T(8,128)S(1)} %bitcast.52), channel_id=1, source_target_pairs={{0,192},{32,224},{64,0},{96,32},{128,64},{160,96},{192,128},{224,1... | collective-permute-start | bytes 2359304 | tf_op jit(solution)/shard_map/ppermute | solution.py:17
  6.7 20.0 %collective-permute-start.4 = (f32[48,4096]{1,0:T(8,128)S(1)}, f32[48,4096]{1,0:T(8,128)}, u32[]{:S(2)}, u32[]{:S(2)}) collective-permute-start(f32[48,4096]{1,0:T(8,128)S(1)} %bitcast.53), channel_id=1, source_target_pairs={{0,64},{32,96},{64,128},{96,160},{128,192},{160,224},{192,0},{224,... | collective-permute-start | bytes 2359304 | tf_op jit(solution)/shard_map/ppermute | solution.py:17
  7.4 20.3 %collective-permute-start.1 = (f32[48,4096]{1,0:T(8,128)S(1)}, f32[48,4096]{1,0:T(8,128)S(1)}, u32[]{:S(2)}, u32[]{:S(2)}) collective-permute-start(f32[48,4096]{1,0:T(8,128)S(1)} %bitcast.54), channel_id=1, source_target_pairs={{1,0},{2,1},{3,2},{4,3},{5,4},{6,5},{7,6},{8,7},{9,8},{10,9},{11,1... | collective-permute-start | bytes 2359304 | tf_op jit(solution)/shard_map/ppermute | solution.py:296
  8.7 20.3 %collective-permute-start = (f32[48,4096]{1,0:T(8,128)S(1)}, f32[48,4096]{1,0:T(8,128)S(1)}, u32[]{:S(2)}, u32[]{:S(2)}) collective-permute-start(f32[48,4096]{1,0:T(8,128)S(1)} %bitcast.55), channel_id=1, source_target_pairs={{0,1},{1,2},{2,3},{3,4},{4,5},{5,6},{6,7},{7,8},{8,9},{9,10},{10,1... | collective-permute-start | bytes 2359304 | tf_op jit(solution)/shard_map/ppermute | solution.py:295
  13.2 55.5 %copy-start.2 = (f32[6,8,32,128]{3,1,2,0:T(8,128)}, f32[6,8,32,128]{3,1,2,0:T(8,128)S(1)}, u32[]{:S(2)}) copy-start(f32[6,8,32,128]{3,1,2,0:T(8,128)S(1)} %copy.16) | copy-start | bytes 2359300
  13.2 36.5 %copy-start.6 = (f32[48,4096]{1,0:T(8,128)}, f32[48,4096]{1,0:T(8,128)S(1)}, u32[]{:S(2)}) copy-start(f32[48,4096]{1,0:T(8,128)S(1)} %collective-permute-done.8.rest_10_.rest_8_) | copy-start | bytes 2359300
  13.2 20.0 %collective-permute-start.9 = (f32[48,4096]{1,0:T(8,128)S(1)}, f32[48,4096]{1,0:T(8,128)S(1)}, u32[]{:S(2)}, u32[]{:S(2)}) collective-permute-start(f32[48,4096]{1,0:T(8,128)S(1)} %bitcast.60), channel_id=1, source_target_pairs={{0,32},{32,0},{64,96},{96,64},{128,160},{160,128},{192,224},{224,1... | collective-permute-start | bytes 2359304 | tf_op jit(solution)/shard_map/ppermute | solution.py:22
  25.0 25.9 %copy-start.8 = (f32[48,4096]{1,0:T(8,128)}, f32[48,4096]{1,0:T(8,128)S(1)}, u32[]{:S(2)}) copy-start(f32[48,4096]{1,0:T(8,128)S(1)} %collective-permute-done.7.rest_9_.rest_7_) | copy-start | bytes 2359300
  25.0 19.6 %collective-permute-start.6 = (f32[48,4096]{1,0:T(8,128)S(1)}, f32[48,4096]{1,0:T(8,128)}, u32[]{:S(2)}, u32[]{:S(2)}) collective-permute-start(f32[48,4096]{1,0:T(8,128)S(1)} %bitcast.61), channel_id=1, source_target_pairs={{0,64},{32,96},{64,128},{96,160},{128,192},{160,224},{192,0},{224,... | collective-permute-start | bytes 2359304 | tf_op jit(solution)/shard_map/ppermute | solution.py:17
  26.7 18.0 %collective-permute-start.5 = (f32[48,4096]{1,0:T(8,128)S(1)}, f32[48,4096]{1,0:T(8,128)}, u32[]{:S(2)}, u32[]{:S(2)}) collective-permute-start(f32[48,4096]{1,0:T(8,128)S(1)} %bitcast.62), channel_id=1, source_target_pairs={{0,192},{32,224},{64,0},{96,32},{128,64},{160,96},{192,128},{224,1... | collective-permute-start | bytes 2359304 | tf_op jit(solution)/shard_map/ppermute | solution.py:17
  27.7 35.8 %copy-start.23 = (f32[48,4096]{1,0:T(8,128)}, f32[48,4096]{1,0:T(8,128)S(1)}, u32[]{:S(2)}) copy-start(f32[48,4096]{1,0:T(8,128)S(1)} %collective-permute-done.1.r_ref) | copy-start | bytes 2359300
  27.7 19.8 %collective-permute-start.3 = (f32[48,4096]{1,0:T(8,128)S(1)}, f32[48,4096]{1,0:T(8,128)S(1)}, u32[]{:S(2)}, u32[]{:S(2)}) collective-permute-start(f32[48,4096]{1,0:T(8,128)S(1)} %bitcast.63), channel_id=1, source_target_pairs={{1,0},{2,1},{3,2},{4,3},{5,4},{6,5},{7,6},{8,7},{9,8},{10,9},{11,1... | collective-permute-start | bytes 2359304 | tf_op jit(solution)/shard_map/ppermute | solution.py:296
  29.0 37.1 %copy-start.24 = (f32[48,4096]{1,0:T(8,128)}, f32[48,4096]{1,0:T(8,128)S(1)}, u32[]{:S(2)}) copy-start(f32[48,4096]{1,0:T(8,128)S(1)} %collective-permute-done.l_ref) | copy-start | bytes 2359300
  29.0 20.7 %collective-permute-start.2 = (f32[48,4096]{1,0:T(8,128)S(1)}, f32[48,4096]{1,0:T(8,128)S(1)}, u32[]{:S(2)}, u32[]{:S(2)}) collective-permute-start(f32[48,4096]{1,0:T(8,128)S(1)} %bitcast.64), channel_id=1, source_target_pairs={{0,1},{1,2},{2,3},{3,4},{4,5},{5,6},{6,7},{7,8},{8,9},{9,10},{10,1... | collective-permute-start | bytes 2359304 | tf_op jit(solution)/shard_map/ppermute | solution.py:295
  33.2 17.7 %copy-start.10 = (f32[48,4096]{1,0:T(8,128)}, f32[48,4096]{1,0:T(8,128)S(1)}, u32[]{:S(2)}) copy-start(f32[48,4096]{1,0:T(8,128)S(1)} %collective-permute-done.9.rest_11_.rest_9_) | copy-start | bytes 2359300
  33.2 17.7 %collective-permute-start.13 = (f32[48,4096]{1,0:T(8,128)S(1)}, f32[48,4096]{1,0:T(8,128)S(1)}, u32[]{:S(2)}, u32[]{:S(2)}) collective-permute-start(f32[48,4096]{1,0:T(8,128)S(1)} %collective-permute-done.7.rest_9_.rest_7_), channel_id=1, source_target_pairs={{0,32},{32,0},{64,96},{96,64},{128,160},{160,128},{192,224},{224,1... | collective-permute-start | bytes 2359304 | tf_op jit(solution)/shard_map/ppermute | solution.py:22
  44.6 18.9 %collective-permute-start.14 = (f32[48,4096]{1,0:T(8,128)}, f32[48,4096]{1,0:T(8,128)}, u32[]{:S(2)}, u32[]{:S(2)}) collective-permute-start(f32[48,4096]{1,0:T(8,128)} %collective-permute-done.4.rest_6_.rest_4_), channel_id=1, source_target_pairs={{0,64},{32,96},{64,128},{96,160},{128,192},{160,224},{192,0},{224,... | collective-permute-start | bytes 2359304 | tf_op jit(solution)/shard_map/ppermute | solution.py:17
  44.7 21.4 %collective-permute-start.15 = (f32[48,4096]{1,0:T(8,128)}, f32[48,4096]{1,0:T(8,128)}, u32[]{:S(2)}, u32[]{:S(2)}) collective-permute-start(f32[48,4096]{1,0:T(8,128)} %collective-permute-done.5.rest_7_.rest_5_), channel_id=1, source_target_pairs={{0,192},{32,224},{64,0},{96,32},{128,64},{160,96},{192,128},{224,1... | collective-permute-start | bytes 2359304 | tf_op jit(solution)/shard_map/ppermute | solution.py:17
  47.5 18.6 %copy-start.25 = (f32[48,4096]{1,0:T(8,128)}, f32[48,4096]{1,0:T(8,128)S(1)}, u32[]{:S(2)}) copy-start(f32[48,4096]{1,0:T(8,128)S(1)} %collective-permute-done.3.r_ref) | copy-start | bytes 2359300
  47.5 29.5 %collective-permute-start.10 = (f32[48,4096]{1,0:T(8,128)}, f32[48,4096]{1,0:T(8,128)}, u32[]{:S(2)}, u32[]{:S(2)}) collective-permute-start(f32[48,4096]{1,0:T(8,128)} %collective-permute-done.4.rest_6_.rest_4_), channel_id=1, source_target_pairs={{0,32},{32,0},{64,96},{96,64},{128,160},{160,128},{192,224},{224,1... | collective-permute-start | bytes 2359304 | tf_op jit(solution)/shard_map/ppermute | solution.py:22
  49.7 16.7 %copy-start.26 = (f32[48,4096]{1,0:T(8,128)}, f32[48,4096]{1,0:T(8,128)S(1)}, u32[]{:S(2)}) copy-start(f32[48,4096]{1,0:T(8,128)S(1)} %collective-permute-done.2.l_ref) | copy-start | bytes 2359300
  49.7 27.3 %collective-permute-start.11 = (f32[48,4096]{1,0:T(8,128)}, f32[48,4096]{1,0:T(8,128)}, u32[]{:S(2)}, u32[]{:S(2)}) collective-permute-start(f32[48,4096]{1,0:T(8,128)} %collective-permute-done.5.rest_7_.rest_5_), channel_id=1, source_target_pairs={{0,32},{32,0},{64,96},{96,64},{128,160},{160,128},{192,224},{224,1... | collective-permute-start | bytes 2359304 | tf_op jit(solution)/shard_map/ppermute | solution.py:22
  50.9 26.1 %collective-permute-start.12 = (f32[48,4096]{1,0:T(8,128)}, f32[48,4096]{1,0:T(8,128)}, u32[]{:S(2)}, u32[]{:S(2)}) collective-permute-start(f32[48,4096]{1,0:T(8,128)} %collective-permute-done.6.rest_8_.rest_6_), channel_id=1, source_target_pairs={{0,32},{32,0},{64,96},{96,64},{128,160},{160,128},{192,224},{224,1... | collective-permute-start | bytes 2359304 | tf_op jit(solution)/shard_map/ppermute | solution.py:22
  63.5 13.5 %collective-permute-start.16 = (f32[48,4096]{1,0:T(8,128)}, f32[48,4096]{1,0:T(8,128)}, u32[]{:S(2)}, u32[]{:S(2)}) collective-permute-start(f32[48,4096]{1,0:T(8,128)} %collective-permute-done.14.rest_16_.rest_14_), channel_id=1, source_target_pairs={{0,32},{32,0},{64,96},{96,64},{128,160},{160,128},{192,224},{224,1... | collective-permute-start | bytes 2359304 | tf_op jit(solution)/shard_map/ppermute | solution.py:22
  66.1 11.0 %collective-permute-start.17 = (f32[48,4096]{1,0:T(8,128)}, f32[48,4096]{1,0:T(8,128)}, u32[]{:S(2)}, u32[]{:S(2)}) collective-permute-start(f32[48,4096]{1,0:T(8,128)} %collective-permute-done.15.rest_17_.rest_15_), channel_id=1, source_target_pairs={{0,32},{32,0},{64,96},{96,64},{128,160},{160,128},{192,224},{224,1... | collective-permute-start | bytes 2359304 | tf_op jit(solution)/shard_map/ppermute | solution.py:22
  77.0 14.5 %copy-start.4 = (f32[48,4096]{1,0:T(8,128)S(1)}, f32[48,4096]{1,0:T(8,128)}, u32[]{:S(2)}) copy-start(f32[48,4096]{1,0:T(8,128)} %hamiltonian.2.rest_2_.rest_0_.rest_18_) | copy-start | bytes 2359300
  77.0 20.2 %copy-start.5 = (f32[48,4096]{1,0:T(8,128)S(1)}, f32[48,4096]{1,0:T(8,128)}, u32[]{:S(2)}) copy-start(f32[48,4096]{1,0:T(8,128)} %hamiltonian.3.rest_3_.rest_1_.rest_19_) | copy-start | bytes 2359300
  87.6 7.1 %collective-permute-start.18 = (f32[2,24,768]{2,1,0:T(8,128)S(1)}, f32[2,24,768]{2,1,0:T(8,128)S(1)}, u32[]{:S(2)}, u32[]{:S(2)}) collective-permute-start(f32[2,24,768]{2,1,0:T(8,128)S(1)} %get-tuple-element.17), channel_id=1, source_target_pairs={{0,16},{1,17},{2,18},{3,19},{4,20},{5,21},{6,22},{7,23},{8,24},{9,... | collective-permute-start | bytes 442376 | tf_op jit(solution)/shard_map/ppermute | solution.py:37
  90.0 7.2 %collective-permute-start.20 = (f32[2,24,768]{2,1,0:T(8,128)S(1)}, f32[2,24,768]{2,1,0:T(8,128)S(1)}, u32[]{:S(2)}, u32[]{:S(2)}) collective-permute-start(f32[2,24,768]{2,1,0:T(8,128)S(1)} %get-tuple-element.18), channel_id=1, source_target_pairs={{0,24},{1,25},{2,26},{3,27},{4,28},{5,29},{6,30},{7,31},{8,0},{9,1... | collective-permute-start | bytes 442376 | tf_op jit(solution)/shard_map/ppermute | solution.py:37
  90.8 9.2 %collective-permute-start.19 = (f32[2,24,768]{2,1,0:T(8,128)S(1)}, f32[2,24,768]{2,1,0:T(8,128)S(1)}, u32[]{:S(2)}, u32[]{:S(2)}) collective-permute-start(f32[2,24,768]{2,1,0:T(8,128)S(1)} %get-tuple-element.19), channel_id=1, source_target_pairs={{0,8},{1,9},{2,10},{3,11},{4,12},{5,13},{6,14},{7,15},{8,16},{9,17... | collective-permute-start | bytes 442376 | tf_op jit(solution)/shard_map/ppermute | solution.py:37
  91.5 19.2 %collective-permute-start.33 = (f32[48,4096]{1,0:T(8,128)S(1)}, f32[48,4096]{1,0:T(8,128)}, u32[]{:S(2)}, u32[]{:S(2)}) collective-permute-start(f32[48,4096]{1,0:T(8,128)S(1)} %copy-done.4), channel_id=1, source_target_pairs={{0,32},{32,0},{64,96},{96,64},{128,160},{160,128},{192,224},{224,1... | collective-permute-start | bytes 2359304 | tf_op jit(solution)/shard_map/ppermute | solution.py:22
  92.8 19.2 %collective-permute-start.32 = (f32[48,4096]{1,0:T(8,128)S(1)}, f32[48,4096]{1,0:T(8,128)}, u32[]{:S(2)}, u32[]{:S(2)}) collective-permute-start(f32[48,4096]{1,0:T(8,128)S(1)} %copy-done.4), channel_id=1, source_target_pairs={{0,192},{32,224},{64,0},{96,32},{128,64},{160,96},{192,128},{224,1... | collective-permute-start | bytes 2359304 | tf_op jit(solution)/shard_map/ppermute | solution.py:17
  94.7 28.2 %collective-permute-start.29 = (f32[48,4096]{1,0:T(8,128)S(1)}, f32[48,4096]{1,0:T(8,128)}, u32[]{:S(2)}, u32[]{:S(2)}) collective-permute-start(f32[48,4096]{1,0:T(8,128)S(1)} %copy-done.4), channel_id=1, source_target_pairs={{0,64},{32,96},{64,128},{96,160},{128,192},{160,224},{192,0},{224,... | collective-permute-start | bytes 2359304 | tf_op jit(solution)/shard_map/ppermute | solution.py:17
  97.2 31.6 %collective-permute-start.30 = (f32[48,4096]{1,0:T(8,128)S(1)}, f32[48,4096]{1,0:T(8,128)}, u32[]{:S(2)}, u32[]{:S(2)}) collective-permute-start(f32[48,4096]{1,0:T(8,128)S(1)} %copy-done.5), channel_id=1, source_target_pairs={{0,192},{32,224},{64,0},{96,32},{128,64},{160,96},{192,128},{224,1... | collective-permute-start | bytes 2359304 | tf_op jit(solution)/shard_map/ppermute | solution.py:17
  100.9 65.7 %copy-start.1 = (f32[6,8,32,128]{3,1,2,0:T(8,128)S(1)}, f32[6,8,32,128]{3,1,2,0:T(8,128)}, u32[]{:S(2)}) copy-start(f32[6,8,32,128]{3,1,2,0:T(8,128)} %copy-done) | copy-start | bytes 2359300
  100.9 65.7 %copy-start.3 = (f32[6,8,32,128]{3,1,2,0:T(8,128)S(1)}, f32[6,8,32,128]{3,1,2,0:T(8,128)}, u32[]{:S(2)}) copy-start(f32[6,8,32,128]{3,1,2,0:T(8,128)} %copy-done.2) | copy-start | bytes 2359300
  101.0 3.8 %collective-permute-start.21 = (f32[24,768]{1,0:T(8,128)S(1)}, f32[24,768]{1,0:T(8,128)S(1)}, u32[]{:S(2)}, u32[]{:S(2)}) collective-permute-start(f32[24,768]{1,0:T(8,128)S(1)} %select_bitcast_fusion), channel_id=1, source_target_pairs={{0,1},{1,0},{2,3},{3,2},{4,5},{5,4},{6,7},{7,6},{8,9},{9,8},{10,11... | collective-permute-start | bytes 221192 | tf_op jit(solution)/shard_map/ppermute | solution.py:27
  104.7 14.1 %collective-permute-start.24 = (f32[24,768]{1,0:T(8,128)S(1)}, f32[24,768]{1,0:T(8,128)S(1)}, u32[]{:S(2)}, u32[]{:S(2)}) collective-permute-start(f32[24,768]{1,0:T(8,128)S(1)} %bitcast_add_fusion.1), channel_id=1, source_target_pairs={{0,6},{1,7},{2,0},{3,1},{4,2},{5,3},{6,4},{7,5},{8,14},{9,15},{10,... | collective-permute-start | bytes 221192 | tf_op jit(solution)/shard_map/ppermute | solution.py:32
  110.7 9.8 %collective-permute-start.23 = (f32[24,768]{1,0:T(8,128)S(1)}, f32[24,768]{1,0:T(8,128)S(1)}, u32[]{:S(2)}, u32[]{:S(2)}) collective-permute-start(f32[24,768]{1,0:T(8,128)S(1)} %bitcast_add_fusion.1), channel_id=1, source_target_pairs={{0,2},{1,3},{2,4},{3,5},{4,6},{5,7},{6,0},{7,1},{8,10},{9,11},{10,... | collective-permute-start | bytes 221192 | tf_op jit(solution)/shard_map/ppermute | solution.py:32
  112.0 8.8 %collective-permute-start.22 = (f32[24,768]{1,0:T(8,128)S(1)}, f32[24,768]{1,0:T(8,128)S(1)}, u32[]{:S(2)}, u32[]{:S(2)}) collective-permute-start(f32[24,768]{1,0:T(8,128)S(1)} %bitcast_add_fusion.1), channel_id=1, source_target_pairs={{0,4},{1,5},{2,6},{3,7},{4,0},{5,1},{6,2},{7,3},{8,12},{9,13},{10,... | collective-permute-start | bytes 221192 | tf_op jit(solution)/shard_map/ppermute | solution.py:32
  118.9 13.8 %collective-permute-start.34 = (f32[48,4096]{1,0:T(8,128)S(1)}, f32[48,4096]{1,0:T(8,128)S(1)}, u32[]{:S(2)}, u32[]{:S(2)}) collective-permute-start(f32[48,4096]{1,0:T(8,128)S(1)} %copy-done.5), channel_id=1, source_target_pairs={{0,32},{32,0},{64,96},{96,64},{128,160},{160,128},{192,224},{224,1... | collective-permute-start | bytes 2359304 | tf_op jit(solution)/shard_map/ppermute | solution.py:22
  120.5 21.0 %collective-permute-start.31 = (f32[48,4096]{1,0:T(8,128)S(1)}, f32[48,4096]{1,0:T(8,128)S(1)}, u32[]{:S(2)}, u32[]{:S(2)}) collective-permute-start(f32[48,4096]{1,0:T(8,128)S(1)} %copy-done.5), channel_id=1, source_target_pairs={{0,64},{32,96},{64,128},{96,160},{128,192},{160,224},{192,0},{224,... | collective-permute-start | bytes 2359304 | tf_op jit(solution)/shard_map/ppermute | solution.py:17
  120.7 22.0 %collective-permute-start.38 = (f32[48,4096]{1,0:T(8,128)}, f32[48,4096]{1,0:T(8,128)S(1)}, u32[]{:S(2)}, u32[]{:S(2)}) collective-permute-start(f32[48,4096]{1,0:T(8,128)} %collective-permute-done.32.rest_23_), channel_id=1, source_target_pairs={{0,32},{32,0},{64,96},{96,64},{128,160},{160,128},{192,224},{224,1... | collective-permute-start | bytes 2359304 | tf_op jit(solution)/shard_map/ppermute | solution.py:22
  122.9 5.9 %collective-permute-start.25 = (f32[24,768]{1,0:T(8,128)S(1)}, f32[24,768]{1,0:T(8,128)S(1)}, u32[]{:S(2)}, u32[]{:S(2)}) collective-permute-start(f32[24,768]{1,0:T(8,128)S(1)} %add_add_fusion), channel_id=1, source_target_pairs={{0,1},{1,0},{2,3},{3,2},{4,5},{5,4},{6,7},{7,6},{8,9},{9,8},{10,11... | collective-permute-start | bytes 221192 | tf_op jit(solution)/shard_map/ppermute | solution.py:27
  128.8 29.6 %collective-permute-start.39 = (f32[48,4096]{1,0:T(8,128)}, f32[48,4096]{1,0:T(8,128)}, u32[]{:S(2)}, u32[]{:S(2)}) collective-permute-start(f32[48,4096]{1,0:T(8,128)} %collective-permute-done.29.rest_20_), channel_id=1, source_target_pairs={{0,64},{32,96},{64,128},{96,160},{128,192},{160,224},{192,0},{224,... | collective-permute-start | bytes 2359304 | tf_op jit(solution)/shard_map/ppermute | solution.py:17
  128.8 30.3 %collective-permute-start.40 = (f32[48,4096]{1,0:T(8,128)}, f32[48,4096]{1,0:T(8,128)}, u32[]{:S(2)}, u32[]{:S(2)}) collective-permute-start(f32[48,4096]{1,0:T(8,128)} %collective-permute-done.30.rest_21_), channel_id=1, source_target_pairs={{0,192},{32,224},{64,0},{96,32},{128,64},{160,96},{192,128},{224,1... | collective-permute-start | bytes 2359304 | tf_op jit(solution)/shard_map/ppermute | solution.py:17
  133.5 25.6 %collective-permute-start.28 = (f32[2,24,768]{2,1,0:T(8,128)}, f32[2,24,768]{2,1,0:T(8,128)S(1)}, u32[]{:S(2)}, u32[]{:S(2)}) collective-permute-start(f32[2,24,768]{2,1,0:T(8,128)} %maximum_select_fusion.1), channel_id=1, source_target_pairs={{0,24},{1,25},{2,26},{3,27},{4,28},{5,29},{6,30},{7,31},{8,0},{9,1... | collective-permute-start | bytes 442376 | tf_op jit(solution)/shard_map/ppermute | solution.py:37
  142.3 17.3 %collective-permute-start.27 = (f32[2,24,768]{2,1,0:T(8,128)}, f32[2,24,768]{2,1,0:T(8,128)}, u32[]{:S(2)}, u32[]{:S(2)}) collective-permute-start(f32[2,24,768]{2,1,0:T(8,128)} %maximum_select_fusion.1), channel_id=1, source_target_pairs={{0,8},{1,9},{2,10},{3,11},{4,12},{5,13},{6,14},{7,15},{8,16},{9,17... | collective-permute-start | bytes 442376 | tf_op jit(solution)/shard_map/ppermute | solution.py:37
  143.6 16.1 %collective-permute-start.26 = (f32[2,24,768]{2,1,0:T(8,128)}, f32[2,24,768]{2,1,0:T(8,128)}, u32[]{:S(2)}, u32[]{:S(2)}) collective-permute-start(f32[2,24,768]{2,1,0:T(8,128)} %maximum_select_fusion.1), channel_id=1, source_target_pairs={{0,16},{1,17},{2,18},{3,19},{4,20},{5,21},{6,22},{7,23},{8,24},{9,... | collective-permute-start | bytes 442376 | tf_op jit(solution)/shard_map/ppermute | solution.py:37
  146.4 20.2 %copy-start.7 = (f32[48,4096]{1,0:T(8,128)S(1)}, f32[48,4096]{1,0:T(8,128)}, u32[]{:S(2)}) copy-start(f32[48,4096]{1,0:T(8,128)} %copy-done.6) | copy-start | bytes 2359300
  158.4 3.7 %collective-permute-start.35 = (f32[48,4096]{1,0:T(8,128)}, f32[48,4096]{1,0:T(8,128)S(1)}, u32[]{:S(2)}, u32[]{:S(2)}) collective-permute-start(f32[48,4096]{1,0:T(8,128)} %collective-permute-done.29.rest_20_), channel_id=1, source_target_pairs={{0,32},{32,0},{64,96},{96,64},{128,160},{160,128},{192,224},{224,1... | collective-permute-start | bytes 2359304 | tf_op jit(solution)/shard_map/ppermute | solution.py:22
  159.1 4.4 %collective-permute-start.36 = (f32[48,4096]{1,0:T(8,128)}, f32[48,4096]{1,0:T(8,128)S(1)}, u32[]{:S(2)}, u32[]{:S(2)}) collective-permute-start(f32[48,4096]{1,0:T(8,128)} %collective-permute-done.30.rest_21_), channel_id=1, source_target_pairs={{0,32},{32,0},{64,96},{96,64},{128,160},{160,128},{192,224},{224,1... | collective-permute-start | bytes 2359304 | tf_op jit(solution)/shard_map/ppermute | solution.py:22
  159.1 4.4 %collective-permute-start.37 = (f32[48,4096]{1,0:T(8,128)}, f32[48,4096]{1,0:T(8,128)S(1)}, u32[]{:S(2)}, u32[]{:S(2)}) collective-permute-start(f32[48,4096]{1,0:T(8,128)} %copy-done.16), channel_id=1, source_target_pairs={{0,32},{32,0},{64,96},{96,64},{128,160},{160,128},{192,224},{224,1... | collective-permute-start | bytes 2359304 | tf_op jit(solution)/shard_map/ppermute | solution.py:22
  159.6 5.0 %collective-permute-start.41 = (f32[48,4096]{1,0:T(8,128)}, f32[48,4096]{1,0:T(8,128)S(1)}, u32[]{:S(2)}, u32[]{:S(2)}) collective-permute-start(f32[48,4096]{1,0:T(8,128)} %collective-permute-done.39.rest_30_), channel_id=1, source_target_pairs={{0,32},{32,0},{64,96},{96,64},{128,160},{160,128},{192,224},{224,1... | collective-permute-start | bytes 2359304 | tf_op jit(solution)/shard_map/ppermute | solution.py:22
  159.7 6.0 %collective-permute-start.42 = (f32[48,4096]{1,0:T(8,128)}, f32[48,4096]{1,0:T(8,128)S(1)}, u32[]{:S(2)}, u32[]{:S(2)}) collective-permute-start(f32[48,4096]{1,0:T(8,128)} %collective-permute-done.40.rest_31_), channel_id=1, source_target_pairs={{0,32},{32,0},{64,96},{96,64},{128,160},{160,128},{192,224},{224,1... | collective-permute-start | bytes 2359304 | tf_op jit(solution)/shard_map/ppermute | solution.py:22
  166.6 1.1 copy-start.9
  167.8 1.1 copy-start.11
  168.9 1.1 copy-start.13
  170.0 1.1 copy-start.15
  172.3 1.1 copy-start.19
  184.1 20.1 %all-to-all-start = ((f32[256,1,128]{2,1,0:T(1,128)}), f32[256,1,128]{2,1,0:T(1,128)S(1)}, u32[]{:S(2)}, u32[]{:S(2)}) async-start(f32[256,1,128]{2,1,0:T(1,128)} %bitcast.17), calls=%async_computation | async-start | bytes 262144 | tf_op jit(solution)/shard_map/all_to_all | solution.py:307
  (8 other events, 7.4 us)

commit v5 on v4

--- a/solution.py
+++ b/solution.py
@@ -8,7 +8,9 @@
 coeffs = (-205.0 / 72.0, 8.0 / 5.0, -1.0 / 5.0, 8.0 / 315.0, -1.0 / 560.0)
 step_length = 0.05
 GRAM_VMEM = 56 * 1024 * 1024
-GRADIENT_VMEM = 32 * 1024 * 1024
+GRAM_STRIPS = 4
+GRADIENT_STRIPS = 1
+GRADIENT_VMEM = 28 * 1024 * 1024
 ZS = 8
 
 
@@ -108,13 +110,17 @@
     return lax.dot_general(a, b, (((1,), (1,)), ((), ())), preferred_element_type=jnp.float32)
 
 
-def store_split(refs, hi_ref, lo_ref):
+def store_split(refs, hi_ref, lo_ref, columns):
     at = 0
     for ref in refs:
-        hi, lo = split(ref[...])
-        hi_ref[at : at + ref.shape[0], :] = hi
-        lo_ref[at : at + ref.shape[0], :] = lo
+        hi, lo = split(ref[:, columns])
+        hi_ref[at : at + ref.shape[0], columns] = hi
+        lo_ref[at : at + ref.shape[0], columns] = lo
         at += ref.shape[0]
+
+
+def strips(chunk, count):
+    return [slice(k * chunk // count, (k + 1) * chunk // count) for k in range(count)]
 
 
 def gram(own_blocks, blocks):
@@ -122,14 +128,16 @@
     count = len(own_blocks)
     rows = sum(b.shape[0] for b in own_blocks)
     total = sum(b.shape[0] for b in blocks)
-    chunk = 1024
+    chunk = 2048
 
     def kernel(*rest):
         o_ref, hi_ref, lo_ref, w_ref = rest[-4:]
-        store_split(rest[count:-4], hi_ref, lo_ref)
-        store_split(rest[:count], w_ref.at[0:rows], w_ref.at[rows : 2 * rows])
-        with_hi = dot_nt(w_ref[...], hi_ref[...])
-        part = with_hi[:rows] + with_hi[rows:] + dot_nt(w_ref[0:rows, :], lo_ref[...])
+        part = 0.0
+        for strip in strips(chunk, GRAM_STRIPS):
+            store_split(rest[count:-4], hi_ref, lo_ref, strip)
+            store_split(rest[:count], w_ref.at[0:rows], w_ref.at[rows : 2 * rows], strip)
+            with_hi = dot_nt(w_ref[:, strip], hi_ref[:, strip])
+            part = part + with_hi[:rows] + with_hi[rows:] + dot_nt(w_ref[0:rows, strip], lo_ref[:, strip])
 
         @pl.when(pl.program_id(0) == 0)
         def _():
@@ -209,21 +217,21 @@
                 w_ref[own:, index * total : (index + 1) * total] = lo
             acc_ref[...] = jnp.zeros_like(acc_ref)
 
-        store_split(refs, hi_ref, lo_ref)
-        with_hi = jnp.dot(w_ref[...], hi_ref[...], preferred_element_type=jnp.float32)
-        grad = with_hi[:own] + with_hi[own:]
-        grad = grad + jnp.dot(w_ref[:own, :], lo_ref[...], preferred_element_type=jnp.float32)
-        grad = grad + 4.0 * jnp.concatenate([own_refs[0][...], own_refs[1][...]], axis=0)
-        g_ref[...] = grad
-        prev_block = p_ref[...]
-
         def folded(v):
-            v = v.reshape(own // 8, 8, chunk).sum(0)
-            return sum(v[:, k * 128 : (k + 1) * 128] for k in range(chunk // 128))
-
-        acc_ref[0:8, :] += folded(grad * grad)
-        acc_ref[8:16, :] += folded(grad * prev_block)
-        acc_ref[16:24, :] += folded(prev_block * prev_block)
+            v = v.reshape(own // 8, 8, v.shape[1]).sum(0)
+            return sum(v[:, k : k + 128] for k in range(0, v.shape[1], 128))
+
+        for strip in strips(chunk, GRADIENT_STRIPS):
+            store_split(refs, hi_ref, lo_ref, strip)
+            with_hi = jnp.dot(w_ref[...], hi_ref[:, strip], preferred_element_type=jnp.float32)
+            grad = with_hi[:own] + with_hi[own:]
+            grad = grad + jnp.dot(w_ref[:own, :], lo_ref[:, strip], preferred_element_type=jnp.float32)
+            grad = grad + 4.0 * jnp.concatenate([own_refs[0][:, strip], own_refs[1][:, strip]], axis=0)
+            g_ref[:, strip] = grad
+            prev_block = p_ref[:, strip]
+            acc_ref[0:8, :] += folded(grad * grad)
+            acc_ref[8:16, :] += folded(grad * prev_block)
+            acc_ref[16:24, :] += folded(prev_block * prev_block)
 
         @pl.when(pl.program_id(0) == cells // chunk - 1)
         def _():

time: 210 us -> 208 us (level)
    unnamed x60 -> x56, local copies, waits for them, and re-layouts: 17.9 us -> 16.9 us
where the time goes in v5:
time: 208 us; the launch traced here: 207 us
  waiting for transfers between devices  75.9 us (36%)
  starting transfers between devices  75.5 us (36%)
  Pallas kernels  31.8 us (15%)
  local copies, waits for them, and re-layouts  21.4 us (10%)
    ppermute x12, waiting for transfers between devices, shift_orb(): return lax.ppermute(v, 'orb', [(i, (i + k) % n) for i in range(n)])  57 us
    ppermute x16, starting transfers between devices, swap_core(): return lax.ppermute(v, 'orb', [(i, i ^ 1) for i in range(n)])  19.7 us
    unnamed x56, local copies, waits for them, and re-layouts  16.9 us
    ppermute x12, starting transfers between devices, shift_orb(): return lax.ppermute(v, 'orb', [(i, (i + k) % n) for i in range(n)])  12.9 us
    ppermute x3, starting transfers between devices, shift_z(): lax.ppermute(v, 'dom', [(i, i // ZS * ZS + (i + k) % ZS) for i in range(n)])  12.8 us
    pallas_call x1, Pallas kernels, gradient_of(): pl.pallas_call(kernel, out_shape=(jax.ShapeDtypeStruct((own, cells), jnp....  10.5 us
    all_to_all x1, waiting for transfers between devices, on_device(): lax.all_to_all(sums, ('orb', 'dom'), split_axis=0, concat_axis=0, tiled=T...  10.2 us
    ppermute x6, starting transfers between devices, shift_y(): return lax.ppermute(v, 'dom', [(i, (i + k * ZS) % n) for i in range(n)])  9 us
  transfers between devices with their start and end apart: 44, of which 17 were waited for; matrix products, arithmetic and copies ran while one was open for 4% of the time, Pallas kernels for 4%

profile of v5, /device:TPU:1, one launch (start us, length us, event | category | flops | bytes accessed | tf_op | source)
XLA Modules:
  0.0 207.3 jit_solution(2404732152325589074)
XLA Ops:
  0.6 1.5 fusion.3
  2.6 3.3 %collective-permute-start.8 = (f32[48,4096]{1,0:T(8,128)S(1)}, f32[48,4096]{1,0:T(8,128)S(1)}, u32[]{:S(2)}, u32[]{:S(2)}) collective-permute-start(f32[48,4096]{1,0:T(8,128)S(1)} %bitcast.51), channel_id=1, source_target_pairs={{0,32},{32,0},{64,96},{96,64},{128,160},{160,128},{192,224},{224,1... | collective-permute-start | bytes 2359304 | tf_op jit(solution)/shard_map/ppermute | solution.py:24
  5.9 0.8 collective-permute-start.7
  7.4 1.3 collective-permute-start.1
  8.7 4.0 %collective-permute-start = (f32[48,4096]{1,0:T(8,128)S(1)}, f32[48,4096]{1,0:T(8,128)S(1)}, u32[]{:S(2)}, u32[]{:S(2)}) collective-permute-start(f32[48,4096]{1,0:T(8,128)S(1)} %bitcast.55), channel_id=1, source_target_pairs={{0,1},{1,2},{2,3},{3,4},{4,5},{5,6},{6,7},{7,8},{8,9},{9,10},{10,1... | collective-permute-start | bytes 2359304 | tf_op jit(solution)/shard_map/ppermute | solution.py:303
  13.2 1.3 collective-permute-start.9
  14.5 10.5 %collective-permute-done.7.rest_9_.rest_7_ = f32[48,4096]{1,0:T(8,128)S(1)} collective-permute-done((f32[48,4096]{1,0:T(8,128)S(1)}, f32[48,4096]{1,0:T(8,128)S(1)}, u32[]{:S(2)}, u32[]{:S(2)}) %collective-permute-start.7) | collective-permute-done | bytes 786464 | tf_op jit(solution)/shard_map/ppermute | solution.py:19
  25.0 1.7 collective-permute-done.4.rest_6_.rest_4_
  26.7 1.0 collective-permute-start.5
  27.7 1.3 collective-permute-start.3
  29.0 4.2 %collective-permute-start.2 = (f32[48,4096]{1,0:T(8,128)S(1)}, f32[48,4096]{1,0:T(8,128)S(1)}, u32[]{:S(2)}, u32[]{:S(2)}) collective-permute-start(f32[48,4096]{1,0:T(8,128)S(1)} %bitcast.64), channel_id=1, source_target_pairs={{0,1},{1,2},{2,3},{3,4},{4,5},{5,6},{6,7},{7,8},{8,9},{9,10},{10,1... | collective-permute-start | bytes 2359304 | tf_op jit(solution)/shard_map/ppermute | solution.py:303
  33.2 2.0 collective-permute-start.13
  35.2 9.4 %collective-permute-done.6.rest_8_.rest_6_ = f32[48,4096]{1,0:T(8,128)} collective-permute-done((f32[48,4096]{1,0:T(8,128)S(1)}, f32[48,4096]{1,0:T(8,128)}, u32[]{:S(2)}, u32[]{:S(2)}) %collective-permute-start.6) | collective-permute-done | bytes 786464 | tf_op jit(solution)/shard_map/ppermute | solution.py:19
  44.7 2.6 %collective-permute-start.15 = (f32[48,4096]{1,0:T(8,128)}, f32[48,4096]{1,0:T(8,128)}, u32[]{:S(2)}, u32[]{:S(2)}) collective-permute-start(f32[48,4096]{1,0:T(8,128)} %collective-permute-done.5.rest_7_.rest_5_), channel_id=1, source_target_pairs={{0,192},{32,224},{64,0},{96,32},{128,64},{160,96},{192,128},{224,1... | collective-permute-start | bytes 2359304 | tf_op jit(solution)/shard_map/ppermute | solution.py:19
  47.5 2.2 %collective-permute-start.10 = (f32[48,4096]{1,0:T(8,128)}, f32[48,4096]{1,0:T(8,128)}, u32[]{:S(2)}, u32[]{:S(2)}) collective-permute-start(f32[48,4096]{1,0:T(8,128)} %collective-permute-done.4.rest_6_.rest_4_), channel_id=1, source_target_pairs={{0,32},{32,0},{64,96},{96,64},{128,160},{160,128},{192,224},{224,1... | collective-permute-start | bytes 2359304 | tf_op jit(solution)/shard_map/ppermute | solution.py:24
  49.7 1.2 collective-permute-start.11
  51.0 0.8 copy-done.12
  51.8 11.7 %collective-permute-done.14.rest_16_.rest_14_ = f32[48,4096]{1,0:T(8,128)} collective-permute-done((f32[48,4096]{1,0:T(8,128)}, f32[48,4096]{1,0:T(8,128)}, u32[]{:S(2)}, u32[]{:S(2)}) %collective-permute-start.14) | collective-permute-done | bytes 786464 | tf_op jit(solution)/shard_map/ppermute | solution.py:19
  63.5 2.6 %collective-permute-start.16 = (f32[48,4096]{1,0:T(8,128)}, f32[48,4096]{1,0:T(8,128)}, u32[]{:S(2)}, u32[]{:S(2)}) collective-permute-start(f32[48,4096]{1,0:T(8,128)} %collective-permute-done.14.rest_16_.rest_14_), channel_id=1, source_target_pairs={{0,32},{32,0},{64,96},{96,64},{128,160},{160,128},{192,224},{224,1... | collective-permute-start | bytes 2359304 | tf_op jit(solution)/shard_map/ppermute | solution.py:24
  66.4 2.2 %copy.15 = f32[12,8,32,128]{3,1,2,0:T(8,128)} copy(f32[12,8,32,128]{3,2,1,0:T(8,128)S(1)} %bitcast.77) | data formatting | bytes 3145728
  68.7 4.2 %hamiltonian.2.rest_2_.rest_0_.rest_18_ = f32[48,4096]{1,0:T(8,128)} custom-call(f32[48,4096]{1,0:T(8,128)} %bitcast.56, f32[48,4096]{1,0:T(8,128)} %copy-done.22, f32[48,4096]{1,0:T(8,128)} %copy-done.21, f32[1,4096]{1,0:T(1,128)} %bitcast.84), custom_call_target="tpu_custom_call" | custom-call | flops 7864320 | bytes 3145728 | tf_op jit(solution)/shard_map/hamiltonian/pallas_call | solution.py:93
  72.8 4.1 %hamiltonian.3.rest_3_.rest_1_.rest_19_ = f32[48,4096]{1,0:T(8,128)} custom-call(f32[48,4096]{1,0:T(8,128)} %bitcast.65, f32[48,4096]{1,0:T(8,128)} %copy-done.24, f32[48,4096]{1,0:T(8,128)} %copy-done.23, f32[1,4096]{1,0:T(1,128)} %bitcast.85), custom_call_target="tpu_custom_call" | custom-call | flops 7864320 | bytes 3145728 | tf_op jit(solution)/shard_map/hamiltonian/pallas_call | solution.py:93
  77.0 9.0 %gram.1 = f32[192,768]{1,0:T(8,128)} custom-call(f32[48,4096]{1,0:T(8,128)} %bitcast.57, f32[48,4096]{1,0:T(8,128)} %bitcast.66, f32[48,4096]{1,0:T(8,128)} %hamiltonian.2.rest_2_.rest_0_.rest_18_, f32[48,4096]{1,0:T(8,128)} %hamiltonian.3.rest_3_.rest_1_.rest_19_, f32[48,4096]{1,0:T(8,128)} %bitcast.58, f32[48,4096]{1,0:T(8,128)} %bitcast.67, ...), custom_call_target="tpu_custom_call" | custom-call | flops 3623878656 | bytes 15728640 | tf_op jit(solution)/shard_map/gram/pallas_call | solution.py:150
  86.0 1.1 dynamic-slice_bitcast_fusion.2
  87.1 2.4 %collective-permute-start.18 = (f32[2,24,768]{2,1,0:T(8,128)S(1)}, f32[2,24,768]{2,1,0:T(8,128)S(1)}, u32[]{:S(2)}, u32[]{:S(2)}) collective-permute-start(f32[2,24,768]{2,1,0:T(8,128)S(1)} %get-tuple-element.17), channel_id=1, source_target_pairs={{0,16},{1,17},{2,18},{3,19},{4,20},{5,21},{6,22},{7,23},{8,24},{9,... | collective-permute-start | bytes 442376 | tf_op jit(solution)/shard_map/ppermute | solution.py:39
  89.5 0.8 collective-permute-start.20
  91.0 1.3 collective-permute-start.33
  92.2 2.0 collective-permute-start.32
  94.2 2.5 %collective-permute-done.20 = f32[2,24,768]{2,1,0:T(8,128)S(1)} collective-permute-done((f32[2,24,768]{2,1,0:T(8,128)S(1)}, f32[2,24,768]{2,1,0:T(8,128)S(1)}, u32[]{:S(2)}, u32[]{:S(2)}) %collective-permute-start.20) | collective-permute-done | bytes 147488 | tf_op jit(solution)/shard_map/ppermute | solution.py:39
  96.7 2.7 %collective-permute-start.30 = (f32[48,4096]{1,0:T(8,128)S(1)}, f32[48,4096]{1,0:T(8,128)}, u32[]{:S(2)}, u32[]{:S(2)}) collective-permute-start(f32[48,4096]{1,0:T(8,128)S(1)} %copy-done.5), channel_id=1, source_target_pairs={{0,192},{32,224},{64,0},{96,32},{128,64},{160,96},{192,128},{224,1... | collective-permute-start | bytes 2359304 | tf_op jit(solution)/shard_map/ppermute | solution.py:19
  99.4 0.9 fusion.2
  100.4 1.7 collective-permute-start.21
  102.1 2.1 %collective-permute-done.21 = f32[24,768]{1,0:T(8,128)S(1)} collective-permute-done((f32[24,768]{1,0:T(8,128)S(1)}, f32[24,768]{1,0:T(8,128)S(1)}, u32[]{:S(2)}, u32[]{:S(2)}) %collective-permute-start.21) | collective-permute-done | bytes 73760 | tf_op jit(solution)/shard_map/ppermute | solution.py:29
  104.3 5.9 %collective-permute-start.24 = (f32[24,768]{1,0:T(8,128)S(1)}, f32[24,768]{1,0:T(8,128)S(1)}, u32[]{:S(2)}, u32[]{:S(2)}) collective-permute-start(f32[24,768]{1,0:T(8,128)S(1)} %bitcast_add_fusion.1), channel_id=1, source_target_pairs={{0,6},{1,7},{2,0},{3,1},{4,2},{5,3},{6,4},{7,5},{8,14},{9,15},{10,... | collective-permute-start | bytes 221192 | tf_op jit(solution)/shard_map/ppermute | solution.py:34
  110.2 1.2 collective-permute-done.32.rest_23_
  111.4 6.9 %collective-permute-start.22 = (f32[24,768]{1,0:T(8,128)S(1)}, f32[24,768]{1,0:T(8,128)S(1)}, u32[]{:S(2)}, u32[]{:S(2)}) collective-permute-start(f32[24,768]{1,0:T(8,128)S(1)} %bitcast_add_fusion.1), channel_id=1, source_target_pairs={{0,4},{1,5},{2,6},{3,7},{4,0},{5,1},{6,2},{7,3},{8,12},{9,13},{10,... | collective-permute-start | bytes 221192 | tf_op jit(solution)/shard_map/ppermute | solution.py:34
  118.4 1.6 collective-permute-start.34
  120.2 2.2 %collective-permute-start.38 = (f32[48,4096]{1,0:T(8,128)}, f32[48,4096]{1,0:T(8,128)S(1)}, u32[]{:S(2)}, u32[]{:S(2)}) collective-permute-start(f32[48,4096]{1,0:T(8,128)} %collective-permute-done.32.rest_23_), channel_id=1, source_target_pairs={{0,32},{32,0},{64,96},{96,64},{128,160},{160,128},{192,224},{224,1... | collective-permute-start | bytes 2359304 | tf_op jit(solution)/shard_map/ppermute | solution.py:24
  122.4 1.5 collective-permute-start.25
  123.9 4.4 %collective-permute-done.30.rest_21_ = f32[48,4096]{1,0:T(8,128)} collective-permute-done((f32[48,4096]{1,0:T(8,128)S(1)}, f32[48,4096]{1,0:T(8,128)}, u32[]{:S(2)}, u32[]{:S(2)}) %collective-permute-start.30) | collective-permute-done | bytes 786464 | tf_op jit(solution)/shard_map/ppermute | solution.py:19
  128.3 3.2 %collective-permute-start.40 = (f32[48,4096]{1,0:T(8,128)}, f32[48,4096]{1,0:T(8,128)}, u32[]{:S(2)}, u32[]{:S(2)}) collective-permute-start(f32[48,4096]{1,0:T(8,128)} %collective-permute-done.30.rest_21_), channel_id=1, source_target_pairs={{0,192},{32,224},{64,0},{96,32},{128,64},{160,96},{192,128},{224,1... | collective-permute-start | bytes 2359304 | tf_op jit(solution)/shard_map/ppermute | solution.py:19
  132.1 0.9 copy-done.14
  133.1 2.0 collective-permute-start.28
  135.0 5.9 %collective-permute-done.31.rest_22_ = f32[48,4096]{1,0:T(8,128)S(1)} collective-permute-done((f32[48,4096]{1,0:T(8,128)S(1)}, f32[48,4096]{1,0:T(8,128)S(1)}, u32[]{:S(2)}, u32[]{:S(2)}) %collective-permute-start.31) | collective-permute-done | bytes 786464 | tf_op jit(solution)/shard_map/ppermute | solution.py:19
  141.0 0.9 copy-done.16
  142.2 0.9 copy-done.18
  143.1 2.8 %collective-permute-start.26 = (f32[2,24,768]{2,1,0:T(8,128)}, f32[2,24,768]{2,1,0:T(8,128)}, u32[]{:S(2)}, u32[]{:S(2)}) collective-permute-start(f32[2,24,768]{2,1,0:T(8,128)} %maximum_select_fusion.1), channel_id=1, source_target_pairs={{0,16},{1,17},{2,18},{3,19},{4,20},{5,21},{6,22},{7,23},{8,24},{9,... | collective-permute-start | bytes 442376 | tf_op jit(solution)/shard_map/ppermute | solution.py:39
  145.9 12.0 %collective-permute-done.39.rest_30_ = f32[48,4096]{1,0:T(8,128)} collective-permute-done((f32[48,4096]{1,0:T(8,128)}, f32[48,4096]{1,0:T(8,128)}, u32[]{:S(2)}, u32[]{:S(2)}) %collective-permute-start.39) | collective-permute-done | bytes 786464 | tf_op jit(solution)/shard_map/ppermute | solution.py:19
  159.7 0.9 bitcast_dynamic-update-slice_fusion.2
  160.6 0.9 bitcast_dynamic-update-slice_fusion.1
  161.6 1.4 collective-permute-done.37.rest_28_
  163.0 1.1 collective-permute-done.41.rest_32_
  164.1 1.1 collective-permute-done.42.rest_33_
  165.2 1.1 copy-done.9
  166.3 1.1 copy-done.11
  167.5 1.1 copy-done.13
  168.6 1.1 copy-done.15
  169.7 1.1 copy-done.17
  170.9 1.1 copy-done.19
  172.0 10.5 %gradient.1 = (f32[96,4096]{1,0:T(8,128)}, f32[256,128]{1,0:T(8,128)}) custom-call(f32[192,768]{1,0:T(8,128)S(1)} %bitcast.69, f32[96,4096]{1,0:T(8,128)} %bitcast.70, f32[48,4096]{1,0:T(8,128)S(1)} %copy-done.4, f32[48,4096]{1,0:T(8,128)S(1)} %copy-done.5, f32[48,4096]{1,0:T(8,128)S(1)} %bitcast.59, f32[48,4096]{1,0:T(8,128)S(1)} %bitcast.68, ...), custom_call_target="tpu_custom_call" | custom-call | flops 3623878656 | bytes 25165824 | tf_op jit(solution)/shard_map/gradient/pallas_call | solution.py:247
  182.5 7.1 %all-to-all-start = ((f32[256,1,128]{2,1,0:T(1,128)}), f32[256,1,128]{2,1,0:T(1,128)S(1)}, u32[]{:S(2)}, u32[]{:S(2)}) async-start(f32[256,1,128]{2,1,0:T(1,128)} %bitcast.17), calls=%async_computation | async-start | bytes 262144 | tf_op jit(solution)/shard_map/all_to_all | solution.py:315
  189.6 2.8 %copy.11 = f32[12,8,32,128]{3,2,1,0:T(8,128)} copy(f32[12,8,32,128]{3,1,2,0:T(8,128)} %bitcast.78) | data formatting | bytes 3145728
  192.4 10.2 %all-to-all-done = f32[256,1,128]{2,1,0:T(1,128)S(1)} async-done(((f32[256,1,128]{2,1,0:T(1,128)}), f32[256,1,128]{2,1,0:T(1,128)S(1)}, u32[]{:S(2)}, u32[]{:S(2)}) %all-to-all-start) | async-done | bytes 131104 | tf_op jit(solution)/shard_map/all_to_all | solution.py:315
  203.2 4.1 %advance.1 = (f32[96,4,8,128]{3,2,1,0:T(8,128)}, f32[96,4,8,128]{3,2,1,0:T(8,128)}) custom-call(f32[256,128]{1,0:T(8,128)} %bitcast.81, f32[96,4,8,128]{3,2,1,0:T(8,128)} %c_ref.1, f32[96,4,8,128]{3,2,1,0:T(8,128)} %d_ref.1, f32[96,4,8,128]{3,2,1,0:T(8,128)} %bitcast.71), custom_call_target="tpu_custom_call" | custom-call | flops 1572864 | bytes 7864320 | tf_op jit(solution)/shard_map/advance/pallas_call | solution.py:283
  (97 shorter events, 6.9 us)
Async XLA Ops:
  2.1 64.3 %copy-start.20 = (f32[96,4,8,128]{3,2,1,0:T(8,128)S(1)}, f32[96,4,8,128]{3,2,1,0:T(8,128)}, u32[]{:S(2)}) copy-start(f32[96,4,8,128]{3,2,1,0:T(8,128)} %param.6) | copy-start | bytes 4718596
  2.6 66.1 %copy-start = (f32[6,8,32,128]{3,1,2,0:T(8,128)}, f32[6,8,32,128]{3,1,2,0:T(8,128)S(1)}, u32[]{:S(2)}) copy-start(f32[6,8,32,128]{3,1,2,0:T(8,128)S(1)} %copy.17) | copy-start | bytes 2359300
  2.6 10.6 %collective-permute-start.8 = (f32[48,4096]{1,0:T(8,128)S(1)}, f32[48,4096]{1,0:T(8,128)S(1)}, u32[]{:S(2)}, u32[]{:S(2)}) collective-permute-start(f32[48,4096]{1,0:T(8,128)S(1)} %bitcast.51), channel_id=1, source_target_pairs={{0,32},{32,0},{64,96},{96,64},{128,160},{160,128},{192,224},{224,1... | collective-permute-start | bytes 2359304 | tf_op jit(solution)/shard_map/ppermute | solution.py:24
  5.9 19.1 %collective-permute-start.7 = (f32[48,4096]{1,0:T(8,128)S(1)}, f32[48,4096]{1,0:T(8,128)S(1)}, u32[]{:S(2)}, u32[]{:S(2)}) collective-permute-start(f32[48,4096]{1,0:T(8,128)S(1)} %bitcast.52), channel_id=1, source_target_pairs={{0,192},{32,224},{64,0},{96,32},{128,64},{160,96},{192,128},{224,1... | collective-permute-start | bytes 2359304 | tf_op jit(solution)/shard_map/ppermute | solution.py:19
  6.7 20.0 %collective-permute-start.4 = (f32[48,4096]{1,0:T(8,128)S(1)}, f32[48,4096]{1,0:T(8,128)}, u32[]{:S(2)}, u32[]{:S(2)}) collective-permute-start(f32[48,4096]{1,0:T(8,128)S(1)} %bitcast.53), channel_id=1, source_target_pairs={{0,64},{32,96},{64,128},{96,160},{128,192},{160,224},{192,0},{224,... | collective-permute-start | bytes 2359304 | tf_op jit(solution)/shard_map/ppermute | solution.py:19
  7.4 20.3 %collective-permute-start.1 = (f32[48,4096]{1,0:T(8,128)S(1)}, f32[48,4096]{1,0:T(8,128)S(1)}, u32[]{:S(2)}, u32[]{:S(2)}) collective-permute-start(f32[48,4096]{1,0:T(8,128)S(1)} %bitcast.54), channel_id=1, source_target_pairs={{1,0},{2,1},{3,2},{4,3},{5,4},{6,5},{7,6},{8,7},{9,8},{10,9},{11,1... | collective-permute-start | bytes 2359304 | tf_op jit(solution)/shard_map/ppermute | solution.py:304
  8.7 20.3 %collective-permute-start = (f32[48,4096]{1,0:T(8,128)S(1)}, f32[48,4096]{1,0:T(8,128)S(1)}, u32[]{:S(2)}, u32[]{:S(2)}) collective-permute-start(f32[48,4096]{1,0:T(8,128)S(1)} %bitcast.55), channel_id=1, source_target_pairs={{0,1},{1,2},{2,3},{3,4},{4,5},{5,6},{6,7},{7,8},{8,9},{9,10},{10,1... | collective-permute-start | bytes 2359304 | tf_op jit(solution)/shard_map/ppermute | solution.py:303
  13.2 55.5 %copy-start.2 = (f32[6,8,32,128]{3,1,2,0:T(8,128)}, f32[6,8,32,128]{3,1,2,0:T(8,128)S(1)}, u32[]{:S(2)}) copy-start(f32[6,8,32,128]{3,1,2,0:T(8,128)S(1)} %copy.16) | copy-start | bytes 2359300
  13.2 36.5 %copy-start.6 = (f32[48,4096]{1,0:T(8,128)}, f32[48,4096]{1,0:T(8,128)S(1)}, u32[]{:S(2)}) copy-start(f32[48,4096]{1,0:T(8,128)S(1)} %collective-permute-done.8.rest_10_.rest_8_) | copy-start | bytes 2359300
  13.2 20.0 %collective-permute-start.9 = (f32[48,4096]{1,0:T(8,128)S(1)}, f32[48,4096]{1,0:T(8,128)S(1)}, u32[]{:S(2)}, u32[]{:S(2)}) collective-permute-start(f32[48,4096]{1,0:T(8,128)S(1)} %bitcast.60), channel_id=1, source_target_pairs={{0,32},{32,0},{64,96},{96,64},{128,160},{160,128},{192,224},{224,1... | collective-permute-start | bytes 2359304 | tf_op jit(solution)/shard_map/ppermute | solution.py:24
  25.0 25.9 %copy-start.8 = (f32[48,4096]{1,0:T(8,128)}, f32[48,4096]{1,0:T(8,128)S(1)}, u32[]{:S(2)}) copy-start(f32[48,4096]{1,0:T(8,128)S(1)} %collective-permute-done.7.rest_9_.rest_7_) | copy-start | bytes 2359300
  25.0 19.6 %collective-permute-start.6 = (f32[48,4096]{1,0:T(8,128)S(1)}, f32[48,4096]{1,0:T(8,128)}, u32[]{:S(2)}, u32[]{:S(2)}) collective-permute-start(f32[48,4096]{1,0:T(8,128)S(1)} %bitcast.61), channel_id=1, source_target_pairs={{0,64},{32,96},{64,128},{96,160},{128,192},{160,224},{192,0},{224,... | collective-permute-start | bytes 2359304 | tf_op jit(solution)/shard_map/ppermute | solution.py:19
  26.7 18.0 %collective-permute-start.5 = (f32[48,4096]{1,0:T(8,128)S(1)}, f32[48,4096]{1,0:T(8,128)}, u32[]{:S(2)}, u32[]{:S(2)}) collective-permute-start(f32[48,4096]{1,0:T(8,128)S(1)} %bitcast.62), channel_id=1, source_target_pairs={{0,192},{32,224},{64,0},{96,32},{128,64},{160,96},{192,128},{224,1... | collective-permute-start | bytes 2359304 | tf_op jit(solution)/shard_map/ppermute | solution.py:19
  27.7 35.8 %copy-start.21 = (f32[48,4096]{1,0:T(8,128)}, f32[48,4096]{1,0:T(8,128)S(1)}, u32[]{:S(2)}) copy-start(f32[48,4096]{1,0:T(8,128)S(1)} %collective-permute-done.1.r_ref) | copy-start | bytes 2359300
  27.7 19.8 %collective-permute-start.3 = (f32[48,4096]{1,0:T(8,128)S(1)}, f32[48,4096]{1,0:T(8,128)S(1)}, u32[]{:S(2)}, u32[]{:S(2)}) collective-permute-start(f32[48,4096]{1,0:T(8,128)S(1)} %bitcast.63), channel_id=1, source_target_pairs={{1,0},{2,1},{3,2},{4,3},{5,4},{6,5},{7,6},{8,7},{9,8},{10,9},{11,1... | collective-permute-start | bytes 2359304 | tf_op jit(solution)/shard_map/ppermute | solution.py:304
  29.0 37.1 %copy-start.22 = (f32[48,4096]{1,0:T(8,128)}, f32[48,4096]{1,0:T(8,128)S(1)}, u32[]{:S(2)}) copy-start(f32[48,4096]{1,0:T(8,128)S(1)} %collective-permute-done.l_ref) | copy-start | bytes 2359300
  29.0 20.7 %collective-permute-start.2 = (f32[48,4096]{1,0:T(8,128)S(1)}, f32[48,4096]{1,0:T(8,128)S(1)}, u32[]{:S(2)}, u32[]{:S(2)}) collective-permute-start(f32[48,4096]{1,0:T(8,128)S(1)} %bitcast.64), channel_id=1, source_target_pairs={{0,1},{1,2},{2,3},{3,4},{4,5},{5,6},{6,7},{7,8},{8,9},{9,10},{10,1... | collective-permute-start | bytes 2359304 | tf_op jit(solution)/shard_map/ppermute | solution.py:303
  33.2 17.7 %copy-start.10 = (f32[48,4096]{1,0:T(8,128)}, f32[48,4096]{1,0:T(8,128)S(1)}, u32[]{:S(2)}) copy-start(f32[48,4096]{1,0:T(8,128)S(1)} %collective-permute-done.9.rest_11_.rest_9_) | copy-start | bytes 2359300
  33.2 17.7 %collective-permute-start.13 = (f32[48,4096]{1,0:T(8,128)S(1)}, f32[48,4096]{1,0:T(8,128)S(1)}, u32[]{:S(2)}, u32[]{:S(2)}) collective-permute-start(f32[48,4096]{1,0:T(8,128)S(1)} %collective-permute-done.7.rest_9_.rest_7_), channel_id=1, source_target_pairs={{0,32},{32,0},{64,96},{96,64},{128,160},{160,128},{192,224},{224,1... | collective-permute-start | bytes 2359304 | tf_op jit(solution)/shard_map/ppermute | solution.py:24
  44.6 18.9 %collective-permute-start.14 = (f32[48,4096]{1,0:T(8,128)}, f32[48,4096]{1,0:T(8,128)}, u32[]{:S(2)}, u32[]{:S(2)}) collective-permute-start(f32[48,4096]{1,0:T(8,128)} %collective-permute-done.4.rest_6_.rest_4_), channel_id=1, source_target_pairs={{0,64},{32,96},{64,128},{96,160},{128,192},{160,224},{192,0},{224,... | collective-permute-start | bytes 2359304 | tf_op jit(solution)/shard_map/ppermute | solution.py:19
  44.7 21.4 %collective-permute-start.15 = (f32[48,4096]{1,0:T(8,128)}, f32[48,4096]{1,0:T(8,128)}, u32[]{:S(2)}, u32[]{:S(2)}) collective-permute-start(f32[48,4096]{1,0:T(8,128)} %collective-permute-done.5.rest_7_.rest_5_), channel_id=1, source_target_pairs={{0,192},{32,224},{64,0},{96,32},{128,64},{160,96},{192,128},{224,1... | collective-permute-start | bytes 2359304 | tf_op jit(solution)/shard_map/ppermute | solution.py:19
  47.5 18.6 %copy-start.23 = (f32[48,4096]{1,0:T(8,128)}, f32[48,4096]{1,0:T(8,128)S(1)}, u32[]{:S(2)}) copy-start(f32[48,4096]{1,0:T(8,128)S(1)} %collective-permute-done.3.r_ref) | copy-start | bytes 2359300
  47.5 29.5 %collective-permute-start.10 = (f32[48,4096]{1,0:T(8,128)}, f32[48,4096]{1,0:T(8,128)}, u32[]{:S(2)}, u32[]{:S(2)}) collective-permute-start(f32[48,4096]{1,0:T(8,128)} %collective-permute-done.4.rest_6_.rest_4_), channel_id=1, source_target_pairs={{0,32},{32,0},{64,96},{96,64},{128,160},{160,128},{192,224},{224,1... | collective-permute-start | bytes 2359304 | tf_op jit(solution)/shard_map/ppermute | solution.py:24
  49.7 16.7 %copy-start.24 = (f32[48,4096]{1,0:T(8,128)}, f32[48,4096]{1,0:T(8,128)S(1)}, u32[]{:S(2)}) copy-start(f32[48,4096]{1,0:T(8,128)S(1)} %collective-permute-done.2.l_ref) | copy-start | bytes 2359300
  49.7 27.3 %collective-permute-start.11 = (f32[48,4096]{1,0:T(8,128)}, f32[48,4096]{1,0:T(8,128)}, u32[]{:S(2)}, u32[]{:S(2)}) collective-permute-start(f32[48,4096]{1,0:T(8,128)} %collective-permute-done.5.rest_7_.rest_5_), channel_id=1, source_target_pairs={{0,32},{32,0},{64,96},{96,64},{128,160},{160,128},{192,224},{224,1... | collective-permute-start | bytes 2359304 | tf_op jit(solution)/shard_map/ppermute | solution.py:24
  50.9 26.1 %collective-permute-start.12 = (f32[48,4096]{1,0:T(8,128)}, f32[48,4096]{1,0:T(8,128)}, u32[]{:S(2)}, u32[]{:S(2)}) collective-permute-start(f32[48,4096]{1,0:T(8,128)} %collective-permute-done.6.rest_8_.rest_6_), channel_id=1, source_target_pairs={{0,32},{32,0},{64,96},{96,64},{128,160},{160,128},{192,224},{224,1... | collective-permute-start | bytes 2359304 | tf_op jit(solution)/shard_map/ppermute | solution.py:24
  63.5 13.5 %collective-permute-start.16 = (f32[48,4096]{1,0:T(8,128)}, f32[48,4096]{1,0:T(8,128)}, u32[]{:S(2)}, u32[]{:S(2)}) collective-permute-start(f32[48,4096]{1,0:T(8,128)} %collective-permute-done.14.rest_16_.rest_14_), channel_id=1, source_target_pairs={{0,32},{32,0},{64,96},{96,64},{128,160},{160,128},{192,224},{224,1... | collective-permute-start | bytes 2359304 | tf_op jit(solution)/shard_map/ppermute | solution.py:24
  66.1 10.9 %collective-permute-start.17 = (f32[48,4096]{1,0:T(8,128)}, f32[48,4096]{1,0:T(8,128)}, u32[]{:S(2)}, u32[]{:S(2)}) collective-permute-start(f32[48,4096]{1,0:T(8,128)} %collective-permute-done.15.rest_17_.rest_15_), channel_id=1, source_target_pairs={{0,32},{32,0},{64,96},{96,64},{128,160},{160,128},{192,224},{224,1... | collective-permute-start | bytes 2359304 | tf_op jit(solution)/shard_map/ppermute | solution.py:24
  77.0 14.0 %copy-start.4 = (f32[48,4096]{1,0:T(8,128)S(1)}, f32[48,4096]{1,0:T(8,128)}, u32[]{:S(2)}) copy-start(f32[48,4096]{1,0:T(8,128)} %hamiltonian.2.rest_2_.rest_0_.rest_18_) | copy-start | bytes 2359300
  77.0 19.7 %copy-start.5 = (f32[48,4096]{1,0:T(8,128)S(1)}, f32[48,4096]{1,0:T(8,128)}, u32[]{:S(2)}) copy-start(f32[48,4096]{1,0:T(8,128)} %hamiltonian.3.rest_3_.rest_1_.rest_19_) | copy-start | bytes 2359300
  87.1 7.1 %collective-permute-start.18 = (f32[2,24,768]{2,1,0:T(8,128)S(1)}, f32[2,24,768]{2,1,0:T(8,128)S(1)}, u32[]{:S(2)}, u32[]{:S(2)}) collective-permute-start(f32[2,24,768]{2,1,0:T(8,128)S(1)} %get-tuple-element.17), channel_id=1, source_target_pairs={{0,16},{1,17},{2,18},{3,19},{4,20},{5,21},{6,22},{7,23},{8,24},{9,... | collective-permute-start | bytes 442376 | tf_op jit(solution)/shard_map/ppermute | solution.py:39
  89.5 7.2 %collective-permute-start.20 = (f32[2,24,768]{2,1,0:T(8,128)S(1)}, f32[2,24,768]{2,1,0:T(8,128)S(1)}, u32[]{:S(2)}, u32[]{:S(2)}) collective-permute-start(f32[2,24,768]{2,1,0:T(8,128)S(1)} %get-tuple-element.18), channel_id=1, source_target_pairs={{0,24},{1,25},{2,26},{3,27},{4,28},{5,29},{6,30},{7,31},{8,0},{9,1... | collective-permute-start | bytes 442376 | tf_op jit(solution)/shard_map/ppermute | solution.py:39
  90.3 9.2 %collective-permute-start.19 = (f32[2,24,768]{2,1,0:T(8,128)S(1)}, f32[2,24,768]{2,1,0:T(8,128)S(1)}, u32[]{:S(2)}, u32[]{:S(2)}) collective-permute-start(f32[2,24,768]{2,1,0:T(8,128)S(1)} %get-tuple-element.19), channel_id=1, source_target_pairs={{0,8},{1,9},{2,10},{3,11},{4,12},{5,13},{6,14},{7,15},{8,16},{9,17... | collective-permute-start | bytes 442376 | tf_op jit(solution)/shard_map/ppermute | solution.py:39
  91.0 19.2 %collective-permute-start.33 = (f32[48,4096]{1,0:T(8,128)S(1)}, f32[48,4096]{1,0:T(8,128)}, u32[]{:S(2)}, u32[]{:S(2)}) collective-permute-start(f32[48,4096]{1,0:T(8,128)S(1)} %copy-done.4), channel_id=1, source_target_pairs={{0,32},{32,0},{64,96},{96,64},{128,160},{160,128},{192,224},{224,1... | collective-permute-start | bytes 2359304 | tf_op jit(solution)/shard_map/ppermute | solution.py:24
  92.2 19.2 %collective-permute-start.32 = (f32[48,4096]{1,0:T(8,128)S(1)}, f32[48,4096]{1,0:T(8,128)}, u32[]{:S(2)}, u32[]{:S(2)}) collective-permute-start(f32[48,4096]{1,0:T(8,128)S(1)} %copy-done.4), channel_id=1, source_target_pairs={{0,192},{32,224},{64,0},{96,32},{128,64},{160,96},{192,128},{224,1... | collective-permute-start | bytes 2359304 | tf_op jit(solution)/shard_map/ppermute | solution.py:19
  94.2 28.2 %collective-permute-start.29 = (f32[48,4096]{1,0:T(8,128)S(1)}, f32[48,4096]{1,0:T(8,128)}, u32[]{:S(2)}, u32[]{:S(2)}) collective-permute-start(f32[48,4096]{1,0:T(8,128)S(1)} %copy-done.4), channel_id=1, source_target_pairs={{0,64},{32,96},{64,128},{96,160},{128,192},{160,224},{192,0},{224,... | collective-permute-start | bytes 2359304 | tf_op jit(solution)/shard_map/ppermute | solution.py:19
  96.7 31.6 %collective-permute-start.30 = (f32[48,4096]{1,0:T(8,128)S(1)}, f32[48,4096]{1,0:T(8,128)}, u32[]{:S(2)}, u32[]{:S(2)}) collective-permute-start(f32[48,4096]{1,0:T(8,128)S(1)} %copy-done.5), channel_id=1, source_target_pairs={{0,192},{32,224},{64,0},{96,32},{128,64},{160,96},{192,128},{224,1... | collective-permute-start | bytes 2359304 | tf_op jit(solution)/shard_map/ppermute | solution.py:19
  100.4 64.8 %copy-start.1 = (f32[6,8,32,128]{3,1,2,0:T(8,128)S(1)}, f32[6,8,32,128]{3,1,2,0:T(8,128)}, u32[]{:S(2)}) copy-start(f32[6,8,32,128]{3,1,2,0:T(8,128)} %copy-done) | copy-start | bytes 2359300
  100.4 64.8 %copy-start.3 = (f32[6,8,32,128]{3,1,2,0:T(8,128)S(1)}, f32[6,8,32,128]{3,1,2,0:T(8,128)}, u32[]{:S(2)}) copy-start(f32[6,8,32,128]{3,1,2,0:T(8,128)} %copy-done.2) | copy-start | bytes 2359300
  100.4 3.9 %collective-permute-start.21 = (f32[24,768]{1,0:T(8,128)S(1)}, f32[24,768]{1,0:T(8,128)S(1)}, u32[]{:S(2)}, u32[]{:S(2)}) collective-permute-start(f32[24,768]{1,0:T(8,128)S(1)} %select_bitcast_fusion), channel_id=1, source_target_pairs={{0,1},{1,0},{2,3},{3,2},{4,5},{5,4},{6,7},{7,6},{8,9},{9,8},{10,11... | collective-permute-start | bytes 221192 | tf_op jit(solution)/shard_map/ppermute | solution.py:29
  104.3 14.1 %collective-permute-start.24 = (f32[24,768]{1,0:T(8,128)S(1)}, f32[24,768]{1,0:T(8,128)S(1)}, u32[]{:S(2)}, u32[]{:S(2)}) collective-permute-start(f32[24,768]{1,0:T(8,128)S(1)} %bitcast_add_fusion.1), channel_id=1, source_target_pairs={{0,6},{1,7},{2,0},{3,1},{4,2},{5,3},{6,4},{7,5},{8,14},{9,15},{10,... | collective-permute-start | bytes 221192 | tf_op jit(solution)/shard_map/ppermute | solution.py:34
  110.2 9.8 %collective-permute-start.23 = (f32[24,768]{1,0:T(8,128)S(1)}, f32[24,768]{1,0:T(8,128)S(1)}, u32[]{:S(2)}, u32[]{:S(2)}) collective-permute-start(f32[24,768]{1,0:T(8,128)S(1)} %bitcast_add_fusion.1), channel_id=1, source_target_pairs={{0,2},{1,3},{2,4},{3,5},{4,6},{5,7},{6,0},{7,1},{8,10},{9,11},{10,... | collective-permute-start | bytes 221192 | tf_op jit(solution)/shard_map/ppermute | solution.py:34
  111.4 8.8 %collective-permute-start.22 = (f32[24,768]{1,0:T(8,128)S(1)}, f32[24,768]{1,0:T(8,128)S(1)}, u32[]{:S(2)}, u32[]{:S(2)}) collective-permute-start(f32[24,768]{1,0:T(8,128)S(1)} %bitcast_add_fusion.1), channel_id=1, source_target_pairs={{0,4},{1,5},{2,6},{3,7},{4,0},{5,1},{6,2},{7,3},{8,12},{9,13},{10,... | collective-permute-start | bytes 221192 | tf_op jit(solution)/shard_map/ppermute | solution.py:34
  118.4 13.8 %collective-permute-start.34 = (f32[48,4096]{1,0:T(8,128)S(1)}, f32[48,4096]{1,0:T(8,128)S(1)}, u32[]{:S(2)}, u32[]{:S(2)}) collective-permute-start(f32[48,4096]{1,0:T(8,128)S(1)} %copy-done.5), channel_id=1, source_target_pairs={{0,32},{32,0},{64,96},{96,64},{128,160},{160,128},{192,224},{224,1... | collective-permute-start | bytes 2359304 | tf_op jit(solution)/shard_map/ppermute | solution.py:24
  120.0 21.0 %collective-permute-start.31 = (f32[48,4096]{1,0:T(8,128)S(1)}, f32[48,4096]{1,0:T(8,128)S(1)}, u32[]{:S(2)}, u32[]{:S(2)}) collective-permute-start(f32[48,4096]{1,0:T(8,128)S(1)} %copy-done.5), channel_id=1, source_target_pairs={{0,64},{32,96},{64,128},{96,160},{128,192},{160,224},{192,0},{224,... | collective-permute-start | bytes 2359304 | tf_op jit(solution)/shard_map/ppermute | solution.py:19
  120.2 22.0 %collective-permute-start.38 = (f32[48,4096]{1,0:T(8,128)}, f32[48,4096]{1,0:T(8,128)S(1)}, u32[]{:S(2)}, u32[]{:S(2)}) collective-permute-start(f32[48,4096]{1,0:T(8,128)} %collective-permute-done.32.rest_23_), channel_id=1, source_target_pairs={{0,32},{32,0},{64,96},{96,64},{128,160},{160,128},{192,224},{224,1... | collective-permute-start | bytes 2359304 | tf_op jit(solution)/shard_map/ppermute | solution.py:24
  122.4 5.9 %collective-permute-start.25 = (f32[24,768]{1,0:T(8,128)S(1)}, f32[24,768]{1,0:T(8,128)S(1)}, u32[]{:S(2)}, u32[]{:S(2)}) collective-permute-start(f32[24,768]{1,0:T(8,128)S(1)} %add_add_fusion), channel_id=1, source_target_pairs={{0,1},{1,0},{2,3},{3,2},{4,5},{5,4},{6,7},{7,6},{8,9},{9,8},{10,11... | collective-permute-start | bytes 221192 | tf_op jit(solution)/shard_map/ppermute | solution.py:29
  128.3 29.6 %collective-permute-start.39 = (f32[48,4096]{1,0:T(8,128)}, f32[48,4096]{1,0:T(8,128)}, u32[]{:S(2)}, u32[]{:S(2)}) collective-permute-start(f32[48,4096]{1,0:T(8,128)} %collective-permute-done.29.rest_20_), channel_id=1, source_target_pairs={{0,64},{32,96},{64,128},{96,160},{128,192},{160,224},{192,0},{224,... | collective-permute-start | bytes 2359304 | tf_op jit(solution)/shard_map/ppermute | solution.py:19
  128.3 30.3 %collective-permute-start.40 = (f32[48,4096]{1,0:T(8,128)}, f32[48,4096]{1,0:T(8,128)}, u32[]{:S(2)}, u32[]{:S(2)}) collective-permute-start(f32[48,4096]{1,0:T(8,128)} %collective-permute-done.30.rest_21_), channel_id=1, source_target_pairs={{0,192},{32,224},{64,0},{96,32},{128,64},{160,96},{192,128},{224,1... | collective-permute-start | bytes 2359304 | tf_op jit(solution)/shard_map/ppermute | solution.py:19
  133.1 25.5 %collective-permute-start.28 = (f32[2,24,768]{2,1,0:T(8,128)}, f32[2,24,768]{2,1,0:T(8,128)S(1)}, u32[]{:S(2)}, u32[]{:S(2)}) collective-permute-start(f32[2,24,768]{2,1,0:T(8,128)} %maximum_select_fusion.1), channel_id=1, source_target_pairs={{0,24},{1,25},{2,26},{3,27},{4,28},{5,29},{6,30},{7,31},{8,0},{9,1... | collective-permute-start | bytes 442376 | tf_op jit(solution)/shard_map/ppermute | solution.py:39
  141.8 17.3 %collective-permute-start.27 = (f32[2,24,768]{2,1,0:T(8,128)}, f32[2,24,768]{2,1,0:T(8,128)}, u32[]{:S(2)}, u32[]{:S(2)}) collective-permute-start(f32[2,24,768]{2,1,0:T(8,128)} %maximum_select_fusion.1), channel_id=1, source_target_pairs={{0,8},{1,9},{2,10},{3,11},{4,12},{5,13},{6,14},{7,15},{8,16},{9,17... | collective-permute-start | bytes 442376 | tf_op jit(solution)/shard_map/ppermute | solution.py:39
  143.1 16.1 %collective-permute-start.26 = (f32[2,24,768]{2,1,0:T(8,128)}, f32[2,24,768]{2,1,0:T(8,128)}, u32[]{:S(2)}, u32[]{:S(2)}) collective-permute-start(f32[2,24,768]{2,1,0:T(8,128)} %maximum_select_fusion.1), channel_id=1, source_target_pairs={{0,16},{1,17},{2,18},{3,19},{4,20},{5,21},{6,22},{7,23},{8,24},{9,... | collective-permute-start | bytes 442376 | tf_op jit(solution)/shard_map/ppermute | solution.py:39
  145.9 19.3 %copy-start.7 = (f32[48,4096]{1,0:T(8,128)S(1)}, f32[48,4096]{1,0:T(8,128)}, u32[]{:S(2)}) copy-start(f32[48,4096]{1,0:T(8,128)} %copy-done.6) | copy-start | bytes 2359300
  157.9 3.7 %collective-permute-start.35 = (f32[48,4096]{1,0:T(8,128)}, f32[48,4096]{1,0:T(8,128)S(1)}, u32[]{:S(2)}, u32[]{:S(2)}) collective-permute-start(f32[48,4096]{1,0:T(8,128)} %collective-permute-done.29.rest_20_), channel_id=1, source_target_pairs={{0,32},{32,0},{64,96},{96,64},{128,160},{160,128},{192,224},{224,1... | collective-permute-start | bytes 2359304 | tf_op jit(solution)/shard_map/ppermute | solution.py:24
  158.6 4.4 %collective-permute-start.36 = (f32[48,4096]{1,0:T(8,128)}, f32[48,4096]{1,0:T(8,128)S(1)}, u32[]{:S(2)}, u32[]{:S(2)}) collective-permute-start(f32[48,4096]{1,0:T(8,128)} %collective-permute-done.30.rest_21_), channel_id=1, source_target_pairs={{0,32},{32,0},{64,96},{96,64},{128,160},{160,128},{192,224},{224,1... | collective-permute-start | bytes 2359304 | tf_op jit(solution)/shard_map/ppermute | solution.py:24
  158.6 4.4 %collective-permute-start.37 = (f32[48,4096]{1,0:T(8,128)}, f32[48,4096]{1,0:T(8,128)S(1)}, u32[]{:S(2)}, u32[]{:S(2)}) collective-permute-start(f32[48,4096]{1,0:T(8,128)} %copy-done.16), channel_id=1, source_target_pairs={{0,32},{32,0},{64,96},{96,64},{128,160},{160,128},{192,224},{224,1... | collective-permute-start | bytes 2359304 | tf_op jit(solution)/shard_map/ppermute | solution.py:24
  159.1 5.0 %collective-permute-start.41 = (f32[48,4096]{1,0:T(8,128)}, f32[48,4096]{1,0:T(8,128)S(1)}, u32[]{:S(2)}, u32[]{:S(2)}) collective-permute-start(f32[48,4096]{1,0:T(8,128)} %collective-permute-done.39.rest_30_), channel_id=1, source_target_pairs={{0,32},{32,0},{64,96},{96,64},{128,160},{160,128},{192,224},{224,1... | collective-permute-start | bytes 2359304 | tf_op jit(solution)/shard_map/ppermute | solution.py:24
  159.2 6.0 %collective-permute-start.42 = (f32[48,4096]{1,0:T(8,128)}, f32[48,4096]{1,0:T(8,128)S(1)}, u32[]{:S(2)}, u32[]{:S(2)}) collective-permute-start(f32[48,4096]{1,0:T(8,128)} %collective-permute-done.40.rest_31_), channel_id=1, source_target_pairs={{0,32},{32,0},{64,96},{96,64},{128,160},{160,128},{192,224},{224,1... | collective-permute-start | bytes 2359304 | tf_op jit(solution)/shard_map/ppermute | solution.py:24
  165.2 1.1 copy-start.9
  166.3 1.1 copy-start.11
  167.5 1.1 copy-start.13
  168.6 1.1 copy-start.15
  169.7 1.1 copy-start.17
  182.5 20.1 %all-to-all-start = ((f32[256,1,128]{2,1,0:T(1,128)}), f32[256,1,128]{2,1,0:T(1,128)S(1)}, u32[]{:S(2)}, u32[]{:S(2)}) async-start(f32[256,1,128]{2,1,0:T(1,128)} %bitcast.17), calls=%async_computation | async-start | bytes 262144 | tf_op jit(solution)/shard_map/all_to_all | solution.py:315
  (6 other events, 5.3 us)
